TPU v7x, 32 devices: a whole 2x2x4 slice. The times are simulated.
32 devices in a mesh: wide: 8 (over z, x), narrow: 4 (over y, core).
Axes of the slice: x: 2, y: 2, z: 4, core: 2. Of those that a mesh axis runs over, the one named last changes fastest.
Arguments:
- tokens: bfloat16 [224, 72, 768], P(('wide', 'narrow')), may hold values from -6 to 6
- visible: int32 [224], P(('wide', 'narrow')), may hold values from 48 to 72
- first_gain: bfloat16 [768], replicated, may hold values from 0.5 to 1.5
- first_shift: bfloat16 [768], replicated, may hold values from -4 to 4
- joint_weight: bfloat16 [768, 2304], replicated, may hold values from -0.21875 to 0.21875
- query_bias: bfloat16 [768], replicated, may hold values from -4 to 4
- value_bias: bfloat16 [768], replicated, may hold values from -4 to 4
- mixer_weight: bfloat16 [768, 768], replicated, may hold values from -2 to 2
- mixer_bias: bfloat16 [768], replicated, may hold values from -4 to 4
- second_gain: bfloat16 [768], replicated, may hold values from 0.5 to 1.5
- second_shift: bfloat16 [768], replicated, may hold values from -4 to 4
- expand_weight: bfloat16 [768, 3072], replicated, may hold values from -0.21875 to 0.21875
- expand_bias: bfloat16 [3072], replicated, may hold values from -4 to 4
- shrink_weight: bfloat16 [3072, 768], replicated, may hold values from -0.15625 to 0.15625
- shrink_bias: bfloat16 [768], replicated, may hold values from -4 to 4
- cotangent: bfloat16 [224, 72, 768], P(('wide', 'narrow')), may hold values from -6 to 6
Outputs:
- layer_out: bfloat16 [224, 72, 768], P(('wide', 'narrow'))
- input_grad: bfloat16 [224, 72, 768], P(('wide', 'narrow'))
- delta_firstgain: float32 [768], P('narrow')
- delta_firstshift: float32 [768], P('narrow')
- delta_joint: float32 [768, 2304], P('narrow')
- delta_query: float32 [768], P('narrow')
- delta_value: float32 [768], P('narrow')
- delta_mixer: float32 [768, 768], P('narrow')
- delta_mixerbias: float32 [768], P('narrow')
- delta_secondgain: float32 [768], P('narrow')
- delta_secondshift: float32 [768], P('narrow')
- delta_expand: float32 [768, 3072], P('narrow')
- delta_expandbias: float32 [3072], P('narrow')
- delta_shrink: float32 [3072, 768], P('narrow')
- delta_shrinkbias: float32 [768], P('narrow')
Inputs may be any that keep to these rules, and one draw needn't show every extreme that they name: Each item's visible patches fill its first slots; later slots are padding.
All inputs are finite; a program needn't handle non-finite values.
Results may differ from a plain program's by a relative error of at most 0.013.
Values sent between devices are 32-bit elements; how exact they have to be, the bound alone decides.
A program may use at most 192 MiB of HBM per device.

v0:
```python
import jax
import jax.numpy as jnp
from jax import lax
from jax.sharding import PartitionSpec as P

HEAD_DIM = 64


EPSILON = 1e-06


def normalize(features, gain_vec, shift_vec):
    center = features - jnp.mean(features, axis=-1, keepdims=True)
    spread = jnp.mean(center * center, axis=-1, keepdims=True)
    return center * lax.rsqrt(spread + EPSILON) * gain_vec + shift_vec


def gelu_exact(pre_act):
    return jax.nn.gelu(pre_act, approximate=False)


def contract_rows(left_mat, right_mat):
    return lax.dot_general(
        left_mat, right_mat, (((0,), (0,)), ((), ())), preferred_element_type=jnp.float32
    )


def contract_cols(left_mat, right_mat):
    return lax.dot_general(
        left_mat, right_mat, (((1,), (1,)), ((), ())), preferred_element_type=jnp.float32
    )


def attention_logits(query_low, key_part, key_live, score_scale):
    logits = (
        jnp.einsum("iqhe,ikhe->ihqk", query_low, key_part, preferred_element_type=jnp.float32)
        * score_scale
    )
    return jnp.where(key_live, logits, -1000000000.0)


def pack_rows(pieces):
    narrow_count = lax.axis_size("narrow")
    wide_count = lax.axis_size("wide")
    joined = jnp.concatenate([piece.reshape(narrow_count, -1) for piece in pieces], axis=1)
    padding = -joined.shape[1] % wide_count
    return jnp.concatenate([joined, jnp.zeros((narrow_count, padding), jnp.float32)], axis=1)


def arrange_flat(joined):
    narrow_count = lax.axis_size("narrow")
    wide_count = lax.axis_size("wide")
    width_each = joined.shape[1] // wide_count
    arranged = joined.reshape(narrow_count, wide_count, width_each).transpose(1, 0, 2)
    return arranged.reshape(wide_count * narrow_count, width_each)


def unpack_rows(own_row, pieces):
    narrow_count = lax.axis_size("narrow")
    result = []
    offset = 0
    for piece in pieces:
        length = piece.size // narrow_count
        shard_shape = (piece.shape[0] // narrow_count,) + piece.shape[1:]
        result.append(own_row[offset : offset + length].reshape(shard_shape))
        offset = offset + length
    return tuple(result)


def sum_feedforward(
    shrink_grad, shrink_bias_grad, expand_grad, expand_bias_grad, gain_grad, shift_grad
):
    pieces = (shrink_grad, shrink_bias_grad, expand_grad, expand_bias_grad, gain_grad, shift_grad)
    joined = pack_rows(pieces)
    share = lax.psum_scatter(
        arrange_flat(joined), ("wide", "narrow"), scatter_dimension=0, tiled=True
    )
    own_row = lax.all_gather(share, "wide", axis=0, tiled=True).reshape(-1)
    return unpack_rows(own_row, pieces)


def sum_attention(
    joint_grad, query_grad, value_grad, mixer_grad, mixer_bias_grad, gain_grad, shift_grad
):
    pieces = (
        joint_grad,
        query_grad,
        value_grad,
        mixer_grad,
        mixer_bias_grad,
        gain_grad,
        shift_grad,
    )
    joined = pack_rows(pieces)
    share = lax.psum_scatter(
        arrange_flat(joined), ("wide", "narrow"), scatter_dimension=0, tiled=True
    )
    own_row = lax.all_gather(share, "wide", axis=0, tiled=True).reshape(-1)
    return unpack_rows(own_row, pieces)


def shards(
    tokens,
    visible,
    first_gain,
    first_shift,
    joint_weight,
    query_bias,
    value_bias,
    mixer_weight,
    mixer_bias,
    second_gain,
    second_shift,
    expand_weight,
    expand_bias,
    shrink_weight,
    shrink_bias,
    cotangent,
):
    item_count, slot_count, model_width = tokens.shape
    head_count = model_width // HEAD_DIM
    row_count = item_count * slot_count
    head_shape = (item_count, slot_count, head_count, HEAD_DIM)
    score_scale = HEAD_DIM ** (-0.5)
    live_slots = (jnp.arange(slot_count, dtype=jnp.int32)[None, :] < visible[:, None]).astype(
        jnp.float32
    )
    live_rows = live_slots.reshape(row_count, 1)
    key_live = live_slots[:, None, None, :] > 0.5
    flat_in = tokens.reshape(row_count, model_width).astype(jnp.float32)
    first_vals, first_back = jax.vjp(
        normalize, flat_in, first_gain.astype(jnp.float32), first_shift.astype(jnp.float32)
    )
    first_low = first_vals.astype(jnp.bfloat16)
    joint_out = jnp.dot(first_low, joint_weight, preferred_element_type=jnp.float32)
    query_low = (
        (joint_out[:, :model_width] + query_bias.astype(jnp.float32))
        .astype(jnp.bfloat16)
        .reshape(head_shape)
    )
    key_part = joint_out[:, model_width : 2 * model_width].astype(jnp.bfloat16).reshape(head_shape)
    value_part = (
        (joint_out[:, 2 * model_width :] + value_bias.astype(jnp.float32))
        .astype(jnp.bfloat16)
        .reshape(head_shape)
    )
    logits = attention_logits(query_low, key_part, key_live, score_scale)
    row_max = jnp.max(logits, axis=-1, keepdims=True)
    log_total = row_max + jnp.log(jnp.sum(jnp.exp(logits - row_max), axis=-1, keepdims=True))
    attend_low = jnp.exp(logits - log_total).astype(jnp.bfloat16)
    mixed_low = jnp.einsum(
        "ihqk,ikhe->iqhe", attend_low, value_part, preferred_element_type=jnp.float32
    )
    mixed_low = mixed_low.reshape(row_count, model_width).astype(jnp.bfloat16)
    branch = jnp.dot(
        mixed_low, mixer_weight, preferred_element_type=jnp.float32
    ) + mixer_bias.astype(jnp.float32)
    middle = flat_in + branch
    second_vals, second_back = jax.vjp(
        normalize, middle, second_gain.astype(jnp.float32), second_shift.astype(jnp.float32)
    )
    second_low = second_vals.astype(jnp.bfloat16)
    hidden = jnp.dot(
        second_low, expand_weight, preferred_element_type=jnp.float32
    ) + expand_bias.astype(jnp.float32)
    active_vals, gelu_back = jax.vjp(gelu_exact, hidden)
    active_low = active_vals.astype(jnp.bfloat16)
    output = jnp.dot(
        active_low, shrink_weight, preferred_element_type=jnp.float32
    ) + shrink_bias.astype(jnp.float32)
    layer_out = (
        ((middle + output) * live_rows)
        .astype(jnp.bfloat16)
        .reshape(item_count, slot_count, model_width)
    )
    grad_out = cotangent.reshape(row_count, model_width).astype(jnp.float32) * live_rows
    grad_out_low = grad_out.astype(jnp.bfloat16)
    shrink_bias_grad = jnp.sum(grad_out, axis=0)
    shrink_grad = contract_rows(active_low, grad_out_low)
    grad_active = contract_cols(grad_out_low, shrink_weight)
    grad_hidden = gelu_back(grad_active)[0].astype(jnp.bfloat16)
    expand_bias_grad = jnp.sum(grad_hidden.astype(jnp.float32), axis=0)
    expand_grad = contract_rows(second_low, grad_hidden)
    grad_second = contract_cols(grad_hidden, expand_weight)
    grad_norm_two, second_gain_grad, second_shift_grad = second_back(grad_second)
    grad_middle = grad_out + grad_norm_two
    (
        total_shrink,
        total_shrink_bias,
        total_expand,
        total_expand_bias,
        total_second_gain,
        total_second_shift,
    ) = sum_feedforward(
        shrink_grad,
        shrink_bias_grad,
        expand_grad,
        expand_bias_grad,
        second_gain_grad,
        second_shift_grad,
    )
    grad_branch = grad_middle.astype(jnp.bfloat16)
    mixer_bias_grad = jnp.sum(grad_branch.astype(jnp.float32), axis=0)
    mixer_grad = contract_rows(mixed_low, grad_branch)
    grad_mixed = contract_cols(grad_branch, mixer_weight).astype(jnp.bfloat16).reshape(head_shape)
    attend_again = jnp.exp(attention_logits(query_low, key_part, key_live, score_scale) - log_total)
    grad_attend = jnp.einsum(
        "iqhe,ikhe->ihqk", grad_mixed, value_part, preferred_element_type=jnp.float32
    )
    grad_value = jnp.einsum(
        "ihqk,iqhe->ikhe",
        attend_again.astype(jnp.bfloat16),
        grad_mixed,
        preferred_element_type=jnp.float32,
    )
    grad_logits = attend_again * (
        grad_attend - jnp.sum(attend_again * grad_attend, axis=-1, keepdims=True)
    )
    grad_logits = grad_logits.astype(jnp.bfloat16)
    grad_query = (
        jnp.einsum("ihqk,ikhe->iqhe", grad_logits, key_part, preferred_element_type=jnp.float32)
        * score_scale
    )
    grad_key = (
        jnp.einsum("ihqk,iqhe->ikhe", grad_logits, query_low, preferred_element_type=jnp.float32)
        * score_scale
    )
    grad_joint = jnp.concatenate(
        [
            grad_query.reshape(row_count, model_width),
            grad_key.reshape(row_count, model_width),
            grad_value.reshape(row_count, model_width),
        ],
        axis=1,
    ).astype(jnp.bfloat16)
    grad_joint_float = grad_joint.astype(jnp.float32)
    query_grad = jnp.sum(grad_joint_float[:, :model_width], axis=0)
    value_grad = jnp.sum(grad_joint_float[:, 2 * model_width :], axis=0)
    joint_grad = contract_rows(first_low, grad_joint)
    grad_first = contract_cols(grad_joint, joint_weight)
    grad_norm_one, first_gain_grad, first_shift_grad = first_back(grad_first)
    input_grad = (
        (grad_middle + grad_norm_one)
        .astype(jnp.bfloat16)
        .reshape(item_count, slot_count, model_width)
    )
    (
        total_joint,
        total_query,
        total_value,
        total_mixer,
        total_mixer_bias,
        total_first_gain,
        total_first_shift,
    ) = sum_attention(
        joint_grad,
        query_grad,
        value_grad,
        mixer_grad,
        mixer_bias_grad,
        first_gain_grad,
        first_shift_grad,
    )
    return (
        layer_out,
        input_grad,
        total_first_gain,
        total_first_shift,
        total_joint,
        total_query,
        total_value,
        total_mixer,
        total_mixer_bias,
        total_second_gain,
        total_second_shift,
        total_expand,
        total_expand_bias,
        total_shrink,
        total_shrink_bias,
    )


def solution(mesh):
    return jax.shard_map(
        shards,
        mesh=mesh,
        in_specs=(
            P(("wide", "narrow"), None, None),
            P(("wide", "narrow")),
            P(),
            P(),
            P(),
            P(),
            P(),
            P(),
            P(),
            P(),
            P(),
            P(),
            P(),
            P(),
            P(),
            P(("wide", "narrow"), None, None),
        ),
        out_specs=(
            P(("wide", "narrow"), None, None),
            P(("wide", "narrow"), None, None),
            P("narrow"),
            P("narrow"),
            P("narrow", None),
            P("narrow"),
            P("narrow"),
            P("narrow", None),
            P("narrow"),
            P("narrow"),
            P("narrow"),
            P("narrow", None),
            P("narrow"),
            P("narrow", None),
            P("narrow"),
        ),
        check_vma=False,
    )
```

profile of v0, /device:TPU:0, one launch (start us, length us, event | category | flops | bytes accessed | tf_op | source)
XLA Modules:
  0.0 1105.8 jit_solution(2112300342162239540)
XLA Ops:
  21.6 4.2 reshape.323
  25.8 4.1 copy.90
  30.6 3.7 reshape.324
  34.3 4.1 copy.88
  38.4 3.7 reshape.325
  42.1 4.1 copy.89
  55.0 3.6 convert_element_type.137
  67.4 5.8 fusion.25
  73.3 18.9 %convert_reduce_fusion = (f32[3072]{0:T(1024)}, bf16[504,3072]{1,0:T(8,128)(2,1)S(1)}, f32[504,3072]{1,0:T(8,128)}) fusion(f32[504,3072]{1,0:T(8,128)S(1)} %fusion.25, f32[3072]{0:T(1024)S(1)} %convert_element_type.142, bf16[504,768]{1,0:T(8,128)(2,1)S(1)} %fusion.10, bf16[3072,768]{1,0:T(8,128)(2,1)S(1)} %bitcast.84), kind=kOutput, calls=%fused_computation.2 | convolution fusion | flops 2494288896 | bytes 21000192 | tf_op jit(solution)/shard_map/dot_general | solution.py:29
  92.3 3.4 multiply_reduce_fusion.1
  101.1 3.7 reshape.326
  104.8 4.3 copy.94
  109.1 4.4 multiply_reduce_fusion
  122.7 3.5 reshape.287
  128.2 3.5 copy.101
  131.7 3.5 reshape.288
  135.2 3.5 copy.104
  138.7 3.9 reshape.289
  146.9 6.0 multiply_reduce_fusion.3
  152.9 4.9 fusion.34
  162.8 5.5 fusion.24
  168.3 3.2 multiply_convert_fusion
  171.5 9.4 reshape.291
  180.8 6.4 constant_dynamic-update-slice_fusion.5
  201.4 13.9 %reshape.329 = f32[2363136]{0:T(1024)} reshape(f32[4,590784]{1,0:T(4,128)} %constant_dynamic-update-slice_fusion.3) | data formatting | bytes 18905088
  215.4 13.3 %reshape.298 = f32[4,8,73848]{2,1,0:T(8,128)} reshape(f32[2363136]{0:T(1024)} %reshape.329) | data formatting | bytes 18905088 | tf_op jit(solution)/shard_map/reshape | solution.py:54
  228.7 9.8 copy.105
  238.4 9.0 reshape.299
  247.5 6.2 fusion.36
  253.7 12.1 %reshape.303 = f32[4,589824]{1,0:T(4,128)} reshape(f32[3072,768]{1,0:T(8,128)} %fusion.36) | data formatting | bytes 18874368 | tf_op jit(solution)/shard_map/reshape | solution.py:45
  265.7 9.0 constant_dynamic-update-slice_fusion.7
  274.9 13.8 %reshape.305 = f32[4,589824]{1,0:T(4,128)} reshape(f32[768,3072]{1,0:T(8,128)} %fusion.24) | data formatting | bytes 18874368 | tf_op jit(solution)/shard_map/reshape | solution.py:45
  290.2 49.3 %dynamic-update-slice.2 = f32[4,1180992]{1,0:T(4,128)} dynamic-update-slice(f32[4,1180992]{1,0:T(4,128)} %dynamic-update-slice.1, f32[4,589824]{1,0:T(4,128)} %reshape.305, s32[]{} %constant.96, s32[]{} %constant.98) | dynamic-update-slice | bytes 18874372
  343.3 56.3 %reshape.331 = f32[4723968]{0:T(1024)} reshape(f32[4,1180992]{1,0:T(4,128)} %constant_dynamic-update-slice_fusion.6) | data formatting | bytes 37791744
  399.6 24.7 %reshape.309 = f32[4,8,147624]{2,1,0:T(8,128)} reshape(f32[4723968]{0:T(1024)} %reshape.331) | data formatting | bytes 37791744 | tf_op jit(solution)/shard_map/reshape | solution.py:54
  424.3 19.4 %copy.106 = f32[8,4,147624]{2,1,0:T(4,128)} copy(f32[8,4,147624]{2,0,1:T(8,128)} %bitcast.72) | data formatting | bytes 37791744 | tf_op jit(solution)/shard_map/transpose | solution.py:54
  443.6 24.4 %reshape.310 = f32[32,147624]{1,0:T(8,128)} reshape(f32[8,4,147624]{2,1,0:T(4,128)} %copy.106) | data formatting | bytes 37791744 | tf_op jit(solution)/shard_map/reshape | solution.py:55
  468.2 437.2 %all-reduce.5.cloned.1.call-done = (f32[32,73848]{1,0:T(8,128)}, f32[32,147624]{1,0:T(8,128)}) async-done(((f32[32,73848]{1,0:T(8,128)}, f32[32,147624]{1,0:T(8,128)}), (f32[32,73848]{1,0:T(8,128)}, f32[32,147624]{1,0:T(8,128)})) %all-reduce.5.cloned.1.call-update) | async-done | bytes 28348432
  908.1 3.5 dynamic-slice_bitcast_fusion
  916.8 5.9 multiply_convert_fusion.4
  922.7 36.6 %all-gather.5.cloned.1.call-done = f32[8,1,73848]{2,1,0:T(1,128)} async-done(((f32[1,1,73848]{2,1,0:T(1,128)}), f32[8,1,73848]{2,1,0:T(1,128)}) %all-gather.5.cloned.1.call-update) | async-done | bytes 2363152 | tf_op jit(solution)/shard_map/all_gather | solution.py:98
  959.3 8.7 reduce.3
  976.7 63.3 %all-gather.7.cloned.1.call-done = f32[8,1,147624]{2,1,0:T(1,128)} async-done(((f32[1,1,147624]{2,1,0:T(1,128)}), f32[8,1,147624]{2,1,0:T(1,128)}) %all-gather.7.cloned.1.call-update) | async-done | bytes 4723984 | tf_op jit(solution)/shard_map/all_gather | solution.py:78
  1040.0 36.6 %reduce.4 = f32[8,147624]{1,0:T(8,128)} reduce(f32[8,1,147624]{2,1,0:T(1,128)} %all-gather.7.cloned.1.call-done, f32[]{:T(128)} %constant.94), dimensions={1}, to_apply=%all-gather.1.reduce_sub_computation | reduce | bytes 9447940 | tf_op jit(solution)/shard_map/all_gather | solution.py:78
  1076.6 7.2 reshape.311
  1085.2 5.3 fusion.30
  1091.8 3.9 reshape.312
  1095.7 3.4 reshape.313
  (249 shorter events, 96.8 us)
Async XLA Ops:
  7.2 10.0 copy-start
  7.2 898.2 %all-reduce.5.cloned.1.call-start = ((), (), s32[]{:S(2)}) async-start(), calls=%async_computation.2 | async-start | bytes 56721408
  10.3 8.9 copy-start.36
  13.0 6.3 copy-start.30
  14.4 4.9 copy-start.47
  21.6 8.3 copy-start.66
  52.7 5.9 copy-start.62
  52.8 6.5 copy-start.63
  52.8 7.1 copy-start.57
  59.8 4.7 copy-start.55
  65.9 7.4 slice-start.6
  67.3 5.9 copy-start.28
  67.3 5.9 slice-start.7
  67.4 24.9 %slice-start.4 = ((s8[4718592]{0:T(1024)(128)(4,1)}), s8[4194304]{0:T(1024)(128)(4,1)S(1)}, s32[]{:S(2)}) async-start(s8[4718592]{0:T(1024)(128)(4,1)} %bitcast.81), calls=%async_computation.7 | async-start | bytes 8388608
  73.3 19.0 %copy-start.14 = (f32[504,3072]{1,0:T(8,128)}, f32[504,3072]{1,0:T(8,128)S(1)}, u32[]{:S(2)}) copy-start(f32[504,3072]{1,0:T(8,128)S(1)} %fusion.25) | copy-start | bytes 18579460
  73.3 19.0 %copy-start.16 = (f32[504,768]{1,0:T(8,128)S(1)}, f32[504,768]{1,0:T(8,128)}, u32[]{:S(2)}) copy-start(f32[504,768]{1,0:T(8,128)} %copy-done.15) | copy-start | bytes 4644868
  73.3 19.0 %copy-start.43 = (f32[504]{0:T(512)S(1)}, f32[504]{0:T(512)}, u32[]{:S(2)}) copy-start(f32[504]{0:T(512)} %copy-done.42) | copy-start | bytes 6052
  73.3 19.0 %copy-start.50 = (f32[768]{0:T(1024)S(1)}, f32[768]{0:T(1024)}, u32[]{:S(2)}) copy-start(f32[768]{0:T(1024)} %convert_element_type.139) | copy-start | bytes 9220
  73.3 19.0 %copy-start.53 = (f32[504]{0:T(512)S(1)}, f32[504]{0:T(512)}, u32[]{:S(2)}) copy-start(f32[504]{0:T(512)} %fusion.19) | copy-start | bytes 6052
  73.3 19.0 %slice-start.5 = ((s8[4718592]{0:T(1024)(128)(4,1)}), s8[524288]{0:T(1024)(128)(4,1)S(1)}, s32[]{:S(2)}) async-start(s8[4718592]{0:T(1024)(128)(4,1)} %bitcast.81), calls=%async_computation.8 | async-start | bytes 1048576
  109.1 4.4 copy-start.3
  109.1 4.4 copy-start.27
  138.7 8.1 copy-start.31
  142.6 4.2 copy-start.13
  146.8 6.0 copy-start.6
  146.9 6.0 copy-start.25
  157.8 4.9 copy-start.17
  157.8 4.9 copy-start.44
  157.8 4.9 copy-start.51
  157.8 4.9 copy-start.54
  157.8 4.9 copy-start.56
  157.8 4.9 copy-start.69
  160.9 7.3 slice-start
  160.9 7.3 slice-start.2
  162.8 5.5 slice-start.1
  162.8 5.5 slice-start.3
  238.4 9.1 copy-start.20
  274.9 13.8 %copy-start.52 = (f32[3072]{0:T(1024)S(1)}, f32[3072]{0:T(1024)}, u32[]{:S(2)}) copy-start(f32[3072]{0:T(1024)} %get-tuple-element.25) | copy-start | bytes 36868
  274.9 13.8 %copy-start.59 = (f32[768]{0:T(1024)S(1)}, f32[768]{0:T(1024)}, u32[]{:S(2)}) copy-start(f32[768]{0:T(1024)} %get-tuple-element.17) | copy-start | bytes 9220
  274.9 13.9 %copy-start.58 = (f32[768]{0:T(1024)S(1)}, f32[768]{0:T(1024)}, u32[]{:S(2)}) copy-start(f32[768]{0:T(1024)} %get-tuple-element.21) | copy-start | bytes 9220
  468.1 443.5 %copy-start.64 = (bf16[768]{0:T(1024)(128)(2,1)S(1)}, bf16[768]{0:T(1024)(128)(2,1)}, u32[]{:S(2)}) copy-start(bf16[768]{0:T(1024)(128)(2,1)} %param.30) | copy-start | bytes 4612
  468.1 443.5 %copy-start.48 = (f32[504]{0:T(512)S(1)}, f32[504]{0:T(512)}, u32[]{:S(2)}) copy-start(f32[504]{0:T(512)} %copy-done.47) | copy-start | bytes 6052
  468.1 443.6 %copy-start.65 = (f32[504]{0:T(512)S(1)}, f32[504]{0:T(512)}, u32[]{:S(2)}) copy-start(f32[504]{0:T(512)} %get-tuple-element.20) | copy-start | bytes 6052
  468.1 443.6 %copy-start.38 = (f32[504]{0:T(512)S(1)}, f32[504]{0:T(512)}, u32[]{:S(2)}) copy-start(f32[504]{0:T(512)} %copy-done.36) | copy-start | bytes 6052
  468.1 443.6 %copy-start.41 = (f32[504]{0:T(512)S(1)}, f32[504]{0:T(512)}, u32[]{:S(2)}) copy-start(f32[504]{0:T(512)} %copy-done.39) | copy-start | bytes 6052
  468.1 491.2 %all-gather.5.cloned.1.call-start = ((), (), s32[]{:S(2)}) async-start(), calls=%async_computation | async-start | bytes 2658816 | tf_op jit(solution)/shard_map/all_gather | solution.py:98
  908.0 132.0 %all-gather.7.cloned.1.call-start = ((), (), s32[]{:S(2)}) async-start(), calls=%async_computation.1 | async-start | bytes 5317632 | tf_op jit(solution)/shard_map/all_gather | solution.py:78
  1091.8 7.2 copy-start.1
  (33 other events, 78.4 us)
Sparse Core Ops, SparseCore 0:
  468.2 437.1 all-reduce.4
  908.2 51.0 all-gather.4
  961.5 78.4 all-gather.6
where the time goes:
time: 1110 us
  waiting for transfers between devices  537 us (48%)
  local copies, waits for them, and re-layouts  399 us (36%)
  other arithmetic  77.3 us (7%)
  matrix products  77.2 us (7%)
  between operations  15 us (1%)
    unnamed x4, waiting for transfers between devices  437 us
    unnamed x173, local copies, waits for them, and re-layouts  165 us
    all_gather x1, waiting for transfers between devices, sum_feedforward(): own_row = lax.all_gather(share, 'wide', axis=0, tiled=True).reshape(-1)  63.3 us
    reshape x13, local copies, waits for them, and re-layouts, pack_rows(): piece.reshape(narrow_count, -1)  38.5 us
    reshape x2, local copies, waits for them, and re-layouts, arrange_flat(): joined.reshape(narrow_count, wide_count, width_each).transpose(1, 0, 2)  38 us
    all_gather x1, waiting for transfers between devices, sum_attention(): own_row = lax.all_gather(share, 'wide', axis=0, tiled=True).reshape(-1)  36.6 us
    all_gather x1, other arithmetic, sum_feedforward(): own_row = lax.all_gather(share, 'wide', axis=0, tiled=True).reshape(-1)  36.6 us
    reshape x2, local copies, waits for them, and re-layouts, arrange_flat(): return arranged.reshape(wide_count * narrow_count, width_each)  33.5 us
  transfers between devices with their start and end apart: 3, of which 3 were waited for; matrix products, arithmetic and copies ran while one was open for 3% of the time, Pallas kernels for 0%

commit v1 on v0

--- a/solution.py
+++ b/solution.py
@@ -1,9 +1,16 @@
+import functools
+
 import jax
 import jax.numpy as jnp
 from jax import lax
+from jax.experimental import pallas as pl
+from jax.experimental.pallas import tpu as pltpu
 from jax.sharding import PartitionSpec as P
 
 HEAD_DIM = 64
+SUB = 8
+DEPTH = 6
+MESH = pl.DeviceIdType.MESH
 
 
 EPSILON = 1e-06
@@ -19,12 +26,6 @@
     return jax.nn.gelu(pre_act, approximate=False)
 
 
-def contract_rows(left_mat, right_mat):
-    return lax.dot_general(
-        left_mat, right_mat, (((0,), (0,)), ((), ())), preferred_element_type=jnp.float32
-    )
-
-
 def contract_cols(left_mat, right_mat):
     return lax.dot_general(
         left_mat, right_mat, (((1,), (1,)), ((), ())), preferred_element_type=jnp.float32
@@ -39,64 +40,243 @@
     return jnp.where(key_live, logits, -1000000000.0)
 
 
-def pack_rows(pieces):
-    narrow_count = lax.axis_size("narrow")
-    wide_count = lax.axis_size("wide")
-    joined = jnp.concatenate([piece.reshape(narrow_count, -1) for piece in pieces], axis=1)
-    padding = -joined.shape[1] % wide_count
-    return jnp.concatenate([joined, jnp.zeros((narrow_count, padding), jnp.float32)], axis=1)
-
-
-def arrange_flat(joined):
-    narrow_count = lax.axis_size("narrow")
-    wide_count = lax.axis_size("wide")
-    width_each = joined.shape[1] // wide_count
-    arranged = joined.reshape(narrow_count, wide_count, width_each).transpose(1, 0, 2)
-    return arranged.reshape(wide_count * narrow_count, width_each)
-
-
-def unpack_rows(own_row, pieces):
-    narrow_count = lax.axis_size("narrow")
-    result = []
-    offset = 0
-    for piece in pieces:
-        length = piece.size // narrow_count
-        shard_shape = (piece.shape[0] // narrow_count,) + piece.shape[1:]
-        result.append(own_row[offset : offset + length].reshape(shard_shape))
-        offset = offset + length
-    return tuple(result)
-
-
-def sum_feedforward(
-    shrink_grad, shrink_bias_grad, expand_grad, expand_bias_grad, gain_grad, shift_grad
-):
-    pieces = (shrink_grad, shrink_bias_grad, expand_grad, expand_bias_grad, gain_grad, shift_grad)
-    joined = pack_rows(pieces)
-    share = lax.psum_scatter(
-        arrange_flat(joined), ("wide", "narrow"), scatter_dimension=0, tiled=True
-    )
-    own_row = lax.all_gather(share, "wide", axis=0, tiled=True).reshape(-1)
-    return unpack_rows(own_row, pieces)
-
-
-def sum_attention(
-    joint_grad, query_grad, value_grad, mixer_grad, mixer_bias_grad, gain_grad, shift_grad
-):
-    pieces = (
-        joint_grad,
-        query_grad,
-        value_grad,
-        mixer_grad,
-        mixer_bias_grad,
-        gain_grad,
-        shift_grad,
-    )
-    joined = pack_rows(pieces)
-    share = lax.psum_scatter(
-        arrange_flat(joined), ("wide", "narrow"), scatter_dimension=0, tiled=True
-    )
-    own_row = lax.all_gather(share, "wide", axis=0, tiled=True).reshape(-1)
-    return unpack_rows(own_row, pieces)
+def flip(index, place):
+    return index + (1 - 2 * lax.rem(lax.div(index, 2**place), 2)) * 2**place
+
+
+def bit_of(index, place):
+    return lax.rem(lax.div(index, 2**place), 2)
+
+
+def reversed_bits(value, count):
+    out = 0
+    for place in range(count):
+        out = out * 2 + (value >> place) % 2
+    return out
+
+
+class Plan:
+    def __init__(self, narrow, wide, width, ff):
+        self.narrow, self.wide, self.width, self.ff = narrow, wide, width, ff
+        self.narrow_bits = narrow.bit_length() - 1
+        self.wide_bits = wide.bit_length() - 1
+        rows = width // narrow
+        chunk = SUB
+        while rows % (2 * chunk) == 0 and chunk < SUB * wide:
+            chunk *= 2
+        self.chunk = chunk
+        split_bits = (chunk // SUB).bit_length() - 1
+        self.sums = []
+        length = narrow * chunk
+        for place in range(self.narrow_bits):
+            length //= 2
+            self.sums.append(("narrow", place, length, True))
+        for place in range(self.wide_bits):
+            halve = place < split_bits
+            length = length // 2 if halve else length
+            self.sums.append(("wide", place, length, halve))
+        self.gathers = []
+        for place in reversed(range(split_bits)):
+            self.gathers.append(("wide", place, length))
+            length *= 2
+        self.split_bits = split_bits
+        self.depth = len(self.sums) + len(self.gathers)
+        self.phases = []
+        start = 0
+        for rows_block, windows in (
+            (ff // narrow, 1),
+            (rows, ff // width),
+            (rows, 1),
+            (rows, 3),
+        ):
+            count = rows_block // chunk * windows
+            self.phases.append((start, count, rows_block, windows))
+            start += count
+        self.small_at = start
+        self.chunks = start + 1
+
+
+def gradient_kernel(plan, *refs):
+    lefts = (refs[0], refs[2], refs[4], refs[6])
+    rights = (refs[1], refs[3], refs[5], refs[7])
+    small = refs[8]
+    outs = refs[9:13]
+    small_out = refs[13]
+    scratch = refs[14:]
+    part = scratch[0]
+    landed = scratch[1 : 1 + len(plan.sums)]
+    whole = scratch[1 + len(plan.sums)]
+    send_sems, recv_sems = scratch[2 + len(plan.sums) :]
+    width, chunk, narrow = plan.width, plan.chunk, plan.narrow
+    spots = {"narrow": lax.axis_index("narrow"), "wide": lax.axis_index("wide")}
+
+    def partner(axis, place):
+        return {
+            "wide": flip(spots["wide"], place) if axis == "wide" else spots["wide"],
+            "narrow": flip(spots["narrow"], place) if axis == "narrow" else spots["narrow"],
+        }
+
+    barrier = pltpu.get_barrier_semaphore()
+    for axis, place, _, _ in plan.sums:
+        pl.semaphore_signal(barrier, inc=1, device_id=partner(axis, place), device_id_type=MESH)
+    pl.semaphore_wait(barrier, len(plan.sums))
+
+    def source(stage, item):
+        if stage == 0:
+            return part.at[lax.rem(item, 2)]
+        return landed[stage - 1].at[lax.rem(item, DEPTH)]
+
+    def piece_start(bits):
+        start = 0
+        for place in range(bits):
+            start = start + bit_of(spots["wide"], place) * (chunk // 2 ** (place + 1))
+        return start
+
+    def exchange(stage, item):
+        slot = lax.rem(item, DEPTH)
+        if stage < len(plan.sums):
+            axis, place, length, halve = plan.sums[stage]
+            there = (1 - bit_of(spots[axis], place)) * length if halve else 0
+            src = source(stage, item).at[pl.ds(pl.multiple_of(there, SUB), length)]
+            dst = landed[stage].at[slot]
+        else:
+            axis, place, length = plan.gathers[stage - len(plan.sums)]
+            window = pl.ds(pl.multiple_of(piece_start(place + 1), SUB), length)
+            src = whole.at[item, window]
+            dst = src
+        return pltpu.make_async_remote_copy(
+            src_ref=src,
+            dst_ref=dst,
+            send_sem=send_sems.at[stage, slot],
+            recv_sem=recv_sems.at[stage, slot],
+            device_id=partner(axis, place),
+            device_id_type=MESH,
+        )
+
+    def produce(item):
+        slot = lax.rem(item, 2)
+        for (start, count, rows_block, windows), left, right in zip(plan.phases, lefts, rights):
+
+            @pl.when((item >= start) & (item < start + count))
+            def _():
+                local = item - start
+                row = lax.div(local, windows) * chunk
+                col = lax.rem(local, windows) * width
+                rows = [
+                    left[
+                        pl.ds(
+                            pl.multiple_of(
+                                reversed_bits(spot, plan.narrow_bits) * rows_block + row, chunk
+                            ),
+                            chunk,
+                        ),
+                        :,
+                    ]
+                    for spot in range(narrow)
+                ]
+                part[slot] = jnp.dot(
+                    jnp.concatenate(rows, axis=0),
+                    right[:, pl.ds(pl.multiple_of(col, width), width)],
+                    preferred_element_type=jnp.float32,
+                )
+
+        @pl.when(item == plan.small_at)
+        def _():
+            part[slot] = small[...]
+
+    def absorb(stage, item):
+        axis, place, length, halve = plan.sums[stage]
+        here = bit_of(spots[axis], place) * length if halve else 0
+        slot = lax.rem(item, DEPTH)
+        landed[stage][slot] += source(stage, item)[pl.ds(pl.multiple_of(here, SUB), length)]
+
+    def finish(item):
+        for (start, count, _, windows), out in zip(plan.phases, outs):
+
+            @pl.when((item >= start) & (item < start + count))
+            def _():
+                local = item - start
+                row = lax.div(local, windows) * chunk
+                col = lax.rem(local, windows) * width
+                out[
+                    pl.ds(pl.multiple_of(row, chunk), chunk),
+                    pl.ds(pl.multiple_of(col, width), width),
+                ] = whole[item]
+
+        @pl.when(item == plan.small_at)
+        def _():
+            small_out[...] = whole[item]
+
+    def step(tick, carry):
+        @pl.when(tick < plan.chunks)
+        def _():
+            produce(tick)
+            exchange(0, tick).start()
+
+        for stage in range(plan.depth):
+            item = tick - 1 - stage
+
+            @pl.when((item >= 0) & (item < plan.chunks))
+            def _():
+                exchange(stage, item).wait()
+                if stage < len(plan.sums):
+                    absorb(stage, item)
+                if stage == len(plan.sums) - 1:
+                    whole[
+                        item, pl.ds(pl.multiple_of(piece_start(plan.split_bits), SUB), SUB)
+                    ] = landed[stage][lax.rem(item, DEPTH)]
+                if stage + 1 < plan.depth:
+                    exchange(stage + 1, item).start()
+                else:
+                    finish(item)
+
+        return carry
+
+    lax.fori_loop(0, plan.chunks + plan.depth, step, 0)
+
+
+def reduce_gradients(pairs, vectors, ff, width):
+    narrow, wide = lax.axis_size("narrow"), lax.axis_size("wide")
+    plan = Plan(narrow, wide, width, ff)
+    chunk = plan.chunk
+    joined = jnp.concatenate([vector.reshape(narrow, -1) for vector in vectors], axis=1)
+    joined = jnp.pad(joined, ((0, 0), (0, chunk * width - joined.shape[1])))
+    order = [reversed_bits(spot, plan.narrow_bits) for spot in range(narrow)]
+    small = jnp.stack([joined[spot] for spot in order]).reshape(narrow * chunk, width)
+    operands = []
+    for left, right in pairs:
+        extra = -left.shape[0] % 256
+        operands.append(jnp.pad(left, ((0, extra), (0, 0))).T)
+        operands.append(jnp.pad(right, ((0, extra), (0, 0))))
+    shapes = [
+        jax.ShapeDtypeStruct((left.shape[1] // narrow, right.shape[1]), jnp.float32)
+        for left, right in pairs
+    ] + [jax.ShapeDtypeStruct((chunk, width), jnp.float32)]
+    scratch = [pltpu.VMEM((2, narrow * chunk, width), jnp.float32)]
+    scratch += [pltpu.VMEM((DEPTH, length, width), jnp.float32) for _, _, length, _ in plan.sums]
+    scratch += [
+        pltpu.VMEM((plan.chunks, chunk, width), jnp.float32),
+        pltpu.SemaphoreType.DMA((plan.depth, DEPTH)),
+        pltpu.SemaphoreType.DMA((plan.depth, DEPTH)),
+    ]
+    results = pl.pallas_call(
+        functools.partial(gradient_kernel, plan),
+        out_shape=shapes,
+        in_specs=[pl.BlockSpec(memory_space=pltpu.VMEM)] * (len(operands) + 1),
+        out_specs=[pl.BlockSpec(memory_space=pltpu.VMEM)] * len(shapes),
+        scratch_shapes=scratch,
+        compiler_params=pltpu.CompilerParams(
+            collective_id=0, has_side_effects=True, vmem_limit_bytes=60 * 2**20
+        ),
+        name="gradients",
+    )(*operands, small)
+    flat = results[-1].reshape(-1)
+    sums, offset = [], 0
+    for vector in vectors:
+        length = vector.size // narrow
+        sums.append(flat[offset : offset + length])
+        offset += length
+    return results[:-1], sums
 
 
 def shards(
@@ -176,32 +356,14 @@
     grad_out = cotangent.reshape(row_count, model_width).astype(jnp.float32) * live_rows
     grad_out_low = grad_out.astype(jnp.bfloat16)
     shrink_bias_grad = jnp.sum(grad_out, axis=0)
-    shrink_grad = contract_rows(active_low, grad_out_low)
     grad_active = contract_cols(grad_out_low, shrink_weight)
     grad_hidden = gelu_back(grad_active)[0].astype(jnp.bfloat16)
     expand_bias_grad = jnp.sum(grad_hidden.astype(jnp.float32), axis=0)
-    expand_grad = contract_rows(second_low, grad_hidden)
     grad_second = contract_cols(grad_hidden, expand_weight)
     grad_norm_two, second_gain_grad, second_shift_grad = second_back(grad_second)
     grad_middle = grad_out + grad_norm_two
-    (
-        total_shrink,
-        total_shrink_bias,
-        total_expand,
-        total_expand_bias,
-        total_second_gain,
-        total_second_shift,
-    ) = sum_feedforward(
-        shrink_grad,
-        shrink_bias_grad,
-        expand_grad,
-        expand_bias_grad,
-        second_gain_grad,
-        second_shift_grad,
-    )
     grad_branch = grad_middle.astype(jnp.bfloat16)
     mixer_bias_grad = jnp.sum(grad_branch.astype(jnp.float32), axis=0)
-    mixer_grad = contract_rows(mixed_low, grad_branch)
     grad_mixed = contract_cols(grad_branch, mixer_weight).astype(jnp.bfloat16).reshape(head_shape)
     attend_again = jnp.exp(attention_logits(query_low, key_part, key_live, score_scale) - log_total)
     grad_attend = jnp.einsum(
@@ -236,7 +398,6 @@
     grad_joint_float = grad_joint.astype(jnp.float32)
     query_grad = jnp.sum(grad_joint_float[:, :model_width], axis=0)
     value_grad = jnp.sum(grad_joint_float[:, 2 * model_width :], axis=0)
-    joint_grad = contract_rows(first_low, grad_joint)
     grad_first = contract_cols(grad_joint, joint_weight)
     grad_norm_one, first_gain_grad, first_shift_grad = first_back(grad_first)
     input_grad = (
@@ -244,23 +405,38 @@
         .astype(jnp.bfloat16)
         .reshape(item_count, slot_count, model_width)
     )
+    (total_shrink, total_expand, total_mixer, total_joint), vectors = reduce_gradients(
+        (
+            (active_low, grad_out_low),
+            (second_low, grad_hidden),
+            (mixed_low, grad_branch),
+            (first_low, grad_joint),
+        ),
+        (
+            first_gain_grad,
+            first_shift_grad,
+            query_grad,
+            value_grad,
+            mixer_bias_grad,
+            second_gain_grad,
+            second_shift_grad,
+            expand_bias_grad,
+            shrink_bias_grad,
+        ),
+        active_low.shape[1],
+        model_width,
+    )
     (
-        total_joint,
+        total_first_gain,
+        total_first_shift,
         total_query,
         total_value,
-        total_mixer,
         total_mixer_bias,
-        total_first_gain,
-        total_first_shift,
-    ) = sum_attention(
-        joint_grad,
-        query_grad,
-        value_grad,
-        mixer_grad,
-        mixer_bias_grad,
-        first_gain_grad,
-        first_shift_grad,
-    )
+        total_second_gain,
+        total_second_shift,
+        total_expand_bias,
+        total_shrink_bias,
+    ) = vectors
     return (
         layer_out,
         input_grad,

time: 1110 us -> 460 us (0.41)
  waiting for transfers between devices: 537 us -> 0 us
  local copies, waits for them, and re-layouts: 399 us -> 150 us
  Pallas kernels: 0 us -> 197 us
  other arithmetic: 77.3 us -> 33.9 us
  between operations: 15 us -> 1.6 us
    unnamed x4 -> x0, waiting for transfers between devices: 437 us -> none
    pallas_call x0 -> x1, Pallas kernels: none -> 197 us  [reduce_gradients(): pl.pallas_call(functools.partial(gradient_kernel, plan), out_shape=shapes...]
    unnamed x173 -> x128, local copies, waits for them, and re-layouts: 165 us -> 27.3 us
    reshape x23 -> x11, local copies, waits for them, and re-layouts: 131 us -> 11.7 us  [the longest x9 7.51 us: reduce_gradients(): vector.reshape(narrow, -1)]
    all_gather x2 -> x0, waiting for transfers between devices: 99.9 us -> none  [the longest x1 63.3 us: sum_feedforward(): own_row = lax.all_gather(share, 'wide', axis=0, tiled=True).reshape(-1)]
    all_gather x2 -> x0, other arithmetic: 45.3 us -> none  [the longest x1 36.6 us: sum_feedforward(): own_row = lax.all_gather(share, 'wide', axis=0, tiled=True).reshape(-1)]
    transpose x3 -> x4, local copies, waits for them, and re-layouts: 32.6 us -> 11.9 us  [reduce_gradients(): operands.append(jnp.pad(left, ((0, extra), (0, 0))).T)]
    dot_general x4 -> x0, matrix products: 17.4 us -> none  [contract_rows(): lax.dot_general(left_mat, right_mat, (((0,), (0,)), ((), ())), preferred_...]
  transfers between devices with their start and end apart: 3 -> 0, of which waited for: 3 -> 0; matrix products, arithmetic and copies ran while one was open for 3% -> 0% of each run, Pallas kernels for 0% -> 0%
where the time goes in v1:
time: 460 us; the launch traced here: 454 us
  Pallas kernels  197 us (43%)
  local copies, waits for them, and re-layouts  150 us (33%)
  matrix products  72.4 us (16%)
  other arithmetic  33.9 us (7%)
    pallas_call x1, Pallas kernels, reduce_gradients(): pl.pallas_call(functools.partial(gradient_kernel, plan), out_shape=shapes...  197 us
    dot_general x4, matrix products, contract_cols(): lax.dot_general(left_mat, right_mat, (((1,), (1,)), ((), ())), preferred_...  35.5 us
    unnamed x128, local copies, waits for them, and re-layouts  27.3 us
    transpose x4, local copies, waits for them, and re-layouts, reduce_gradients(): operands.append(jnp.pad(left, ((0, extra), (0, 0))).T)  11.9 us
    pad x4, local copies, waits for them, and re-layouts, reduce_gradients(): operands.append(jnp.pad(right, ((0, extra), (0, 0))))  9.43 us

profile of v1, /device:TPU:0, one launch (start us, length us, event | category | flops | bytes accessed | tf_op | source)
XLA Modules:
  0.0 454.4 jit_solution(18373690127569670294)
XLA Ops:
  0.7 2.7 copy.70
  11.3 2.1 fusion.31
  16.9 4.0 reshape.272
  20.9 4.1 copy.66
  25.6 3.7 reshape.273
  29.3 4.1 copy.64
  33.4 2.3 slice.100
  35.8 3.7 reshape.274
  39.5 4.1 copy.65
  43.5 3.0 fusion.6
  50.2 2.2 copy.68
  52.4 4.0 convert_element_type.150
  56.4 2.9 fusion.28
  61.3 7.9 %fusion.32 = f32[504,3072]{1,0:T(8,128)} fusion(bf16[504,768]{0,1:T(8,128)(2,1)S(1)} %add_convert_fusion.2, bf16[768,3072]{1,0:T(8,128)(2,1)} %param.27), kind=kOutput, calls=%fused_computation.96 | convolution fusion | flops 2378170368 | bytes 11685888 | tf_op jit(solution)/shard_map/dot_general | solution.py:343
  69.9 2.6 copy.73
  75.4 20.8 %convert_reduce_fusion = (f32[3072]{0:T(1024)}, bf16[504,3072]{1,0:T(8,128)(2,1)}, f32[504,3072]{1,0:T(8,128)}) fusion(f32[504,3072]{1,0:T(8,128)} %fusion.32, f32[3072]{0:T(1024)S(1)} %copy-done.34, bf16[504,768]{0,1:T(8,128)(2,1)S(1)} %multiply_convert_fusion.5, bf16[3072,768]{1,0:T(8,128)(2,1)} %param.29), kind=kOutput, calls=%fused_computation.2 | convolution fusion | flops 2494288896 | bytes 21000192 | tf_op jit(solution)/shard_map/dot_general | solution.py:30
  96.2 4.3 multiply_convert_fusion
  102.1 5.9 %multiply_convert_fusion.4 = bf16[504,768]{0,1:T(8,128)(2,1)} fusion(f32[504,768]{0,1:T(8,128)S(1)} %copy-done.8, bf16[504,3072]{1,0:T(8,128)(2,1)S(1)} %multiply_convert_fusion, bf16[3072,768]{1,0:T(8,128)(2,1)} %param.29, f32[504]{0:T(512)S(1)} %copy-done.38, f32[768]{0:T(1024)S(1)} %convert_element_type.157), kind=kOutput, calls=%fused_computation.43 | convolution fusion | flops 2379718656 | bytes 10142688 | tf_op jit(solution)/shard_map/dot_general | solution.py:348
  108.0 2.3 copy.72
  110.3 7.6 %fusion.30 = (f32[768]{0:T(1024)}, f32[504,768]{1,0:T(8,128)}) fusion(bf16[504,3072]{1,0:T(8,128)(2,1)} %get-tuple-element.47, bf16[768,3072]{1,0:T(8,128)(2,1)} %param.27), kind=kOutput, calls=%fused_computation.94 | convolution fusion | flops 2378556672 | bytes 9366528 | tf_op jit(solution)/shard_map/dot_general | solution.py:30
  117.9 3.0 copy.74
  120.9 3.2 multiply_reduce_fusion.1
  129.2 3.7 reshape.275
  132.9 4.3 copy.76
  137.2 4.4 multiply_reduce_fusion
  145.7 4.2 copy.103
  149.9 3.8 reshape.269
  153.7 2.2 constant_dynamic-update-slice_fusion.2
  155.9 3.4 fusion.13
  159.3 4.2 copy.104
  163.5 3.8 reshape.270
  169.4 4.4 fusion.11
  173.7 4.2 copy.105
  177.9 4.1 reshape.271
  184.1 5.4 %fusion.29 = (f32[768]{0:T(1024)}, f32[504,768]{1,0:T(8,128)}) fusion(bf16[504,2304]{1,0:T(8,128)(2,1)} %constant_dynamic-update-slice_fusion, bf16[768,2304]{1,0:T(8,128)(2,1)S(1)} %copy-done), kind=kOutput, calls=%fused_computation.93 | convolution fusion | flops 1784014080 | bytes 7412736 | tf_op jit(solution)/shard_map/dot_general | solution.py:30
  189.5 3.0 copy.90
  192.5 2.3 multiply_reduce_fusion.3
  198.3 2.3 copy.91
  200.6 3.8 pad_bitcast_fusion
  204.4 4.7 %copy.94.refs_0_ = bf16[3072,512]{1,0:T(8,128)(2,1)} copy(bf16[3072,512]{0,1:T(8,128)(2,1)} %pad_bitcast_fusion) | data formatting | bytes 6291456 | tf_op jit(solution)/shard_map/transpose | solution.py:249
  209.1 2.3 copy.117
  211.3 2.2 pad.32.clone.refs_1_
  213.5 2.1 pad_bitcast_fusion.3.refs_2_
  219.0 2.3 copy.118
  223.3 3.2 pad.38.refs_7_
  242.6 2.6 reshape.264.refs_8_
  245.2 196.7 %gradients.1 = (f32[768,768]{1,0:T(8,128)}, f32[192,3072]{1,0:T(8,128)}, f32[192,768]{1,0:T(8,128)}, f32[192,2304]{1,0:T(8,128)}, f32[64,768]{1,0:T(8,128)}) custom-call(bf16[3072,512]{1,0:T(8,128)(2,1)} %copy.94.refs_0_, bf16[512,768]{1,0:T(8,128)(2,1)} %pad.32.clone.refs_1_, bf16[768,512]{1,0:T(8,128)(2,1)} %pad_bitcast_fusion.3.refs_2_, ...), custom_call_target="tpu_custom_call" | custom-call | tf_op jit(solution)/shard_map/gradients/pallas_call | solution.py:262
  446.4 2.9 copy.125
  (185 shorter events, 70.0 us)
Async XLA Ops:
  0.6 10.6 %copy-start = (bf16[768,2304]{1,0:T(8,128)(2,1)S(1)}, bf16[768,2304]{1,0:T(8,128)(2,1)}, u32[]{:S(2)}) copy-start(bf16[768,2304]{1,0:T(8,128)(2,1)} %param.20) | copy-start | bytes 10616836
  0.7 5.3 %copy-start.52 = (bf16[768]{0:T(1024)(128)(2,1)S(1)}, bf16[768]{0:T(1024)(128)(2,1)}, u32[]{:S(2)}) copy-start(bf16[768]{0:T(1024)(128)(2,1)} %param.18) | copy-start | bytes 4612
  9.4 3.9 copy-start.36
  11.2 2.1 copy-start.20
  11.2 2.1 copy-start.53
  11.3 2.1 copy-start.54
  13.4 2.1 copy-start.11
  20.9 4.1 copy-start.58
  25.6 22.0 %copy-start.32 = (pred[7,72]{1,0:T(8,128)(4,1)}, pred[7,72]{1,0:T(8,128)(4,1)S(1)}, u32[]{:S(2)}) copy-start(pred[7,72]{1,0:T(8,128)(4,1)S(1)} %get-tuple-element.68) | copy-start | bytes 1516
  46.5 3.6 copy-start.1
  46.5 2.4 copy-start.17
  50.2 6.2 %copy-start.50 = (f32[768]{0:T(1024)S(1)}, f32[768]{0:T(1024)}, u32[]{:S(2)}) copy-start(f32[768]{0:T(1024)} %convert_element_type.151) | copy-start | bytes 9220
  56.4 2.9 copy-start.55
  56.4 2.9 copy-start.56
  61.3 7.9 %copy-start.22 = (bf16[504,768]{0,1:T(8,128)(2,1)}, bf16[504,768]{0,1:T(8,128)(2,1)S(1)}, u32[]{:S(2)}) copy-start(bf16[504,768]{0,1:T(8,128)(2,1)S(1)} %add_convert_fusion.2) | copy-start | bytes 2322436
  61.3 7.9 %copy-start.49 = (bf16[3072]{0:T(1024)(128)(2,1)S(1)}, bf16[3072]{0:T(1024)(128)(2,1)}, u32[]{:S(2)}) copy-start(bf16[3072]{0:T(1024)(128)(2,1)} %param.28) | copy-start | bytes 18436
  75.4 20.8 %copy-start.23 = (bf16[504,768]{0,1:T(8,128)(2,1)}, bf16[504,768]{0,1:T(8,128)(2,1)S(1)}, u32[]{:S(2)}) copy-start(bf16[504,768]{0,1:T(8,128)(2,1)S(1)} %multiply_convert_fusion.5) | copy-start | bytes 2322436
  75.4 20.8 %copy-start.10 = (f32[504,3072]{1,0:T(8,128)S(1)}, f32[504,3072]{1,0:T(8,128)}, u32[]{:S(2)}) copy-start(f32[504,3072]{1,0:T(8,128)} %fusion.32) | copy-start | bytes 18579460
  96.1 4.4 copy-start.57
  96.1 6.0 %copy-start.8 = (f32[504,768]{0,1:T(8,128)S(1)}, f32[504,768]{0,1:T(8,128)}, u32[]{:S(2)}) copy-start(f32[504,768]{0,1:T(8,128)} %copy-done.7) | copy-start | bytes 4644868
  96.2 6.0 %copy-start.38 = (f32[504]{0:T(512)S(1)}, f32[504]{0:T(512)}, u32[]{:S(2)}) copy-start(f32[504]{0:T(512)} %reshape.267) | copy-start | bytes 6052
  120.9 3.2 copy-start.44
  120.9 3.2 copy-start.9
  120.9 3.2 copy-start.14
  120.9 3.2 copy-start.42
  124.6 1.9 copy-start.12
  124.6 2.8 copy-start.59
  132.9 4.3 copy-start.33
  137.2 4.4 copy-start.2
  137.2 4.4 copy-start.30
  141.6 2.3 copy-start.19
  153.7 2.2 copy-start.16
  192.5 2.3 copy-start.46
  192.5 2.4 copy-start.3
  192.5 2.8 copy-start.6
  192.5 2.8 copy-start.37
  194.8 2.0 copy-start.13
  194.8 2.0 copy-start.40
  211.3 4.3 copy-start.26
  215.7 1.9 copy-start.21
  215.7 1.9 copy-start.24
  223.3 3.2 copy-start.48
  223.3 3.9 copy-start.51
  229.9 2.9 copy-start.47
  229.9 5.6 %copy-start.35 = (f32[7,72]{1,0:T(8,128)S(1)}, f32[7,72]{1,0:T(8,128)}, u32[]{:S(2)}) copy-start(f32[7,72]{1,0:T(8,128)} %get-tuple-element.67) | copy-start | bytes 6052
  443.5 5.9 %copy-start.31 = (f32[192,768]{1,0:T(8,128)S(1)}, f32[192,768]{1,0:T(8,128)}, u32[]{:S(2)}) copy-start(f32[192,768]{1,0:T(8,128)} %get-tuple-element.103) | copy-start | bytes 1769476
  446.4 3.8 copy-start.28
  450.2 2.5 copy-start.27
  (12 other events, 14.3 us)

commit v2 on v1

v2 whole, which is shorter than its diff:
```python
import functools
import types

import jax
import jax.numpy as jnp
from jax import lax
from jax.experimental import pallas as pl
from jax.experimental.pallas import tpu as pltpu
from jax.sharding import PartitionSpec as P

HEAD_DIM = 64
EPSILON = 1e-06
SUB = 8
DEPTH = 6
TILE = 256
MESH = pl.DeviceIdType.MESH
ROOT_HALF = 0.5**0.5
PEAK = 0.3989422804014327
BF16 = jnp.bfloat16
F32 = jnp.float32


def flip(index, place):
    return index + (1 - 2 * lax.rem(lax.div(index, 2**place), 2)) * 2**place


def bit_of(index, place):
    return lax.rem(lax.div(index, 2**place), 2)


def reversed_bits(value, count):
    out = 0
    for place in range(count):
        out = out * 2 + (value >> place) % 2
    return out


def aligned(start, size, unit):
    return pl.ds(pl.multiple_of(start, unit), size)


def matmul(left, right, contract=((1,), (0,))):
    return lax.dot_general(left, right, (contract, ((), ())), preferred_element_type=F32)


class Plan:
    def __init__(self, narrow, wide, items, slots, width, ff, least=SUB):
        self.narrow, self.wide, self.width, self.ff = narrow, wide, width, ff
        self.items, self.slots = items, slots
        self.rows = items * slots
        self.padded = self.rows + -self.rows % 256
        self.pairs = width // (2 * HEAD_DIM)
        self.narrow_bits = narrow.bit_length() - 1
        self.wide_bits = wide.bit_length() - 1
        rows = width // narrow
        chunk = least
        while rows % (2 * chunk) == 0 and chunk < SUB * wide:
            chunk *= 2
        self.chunk = chunk
        split_bits = (chunk // SUB).bit_length() - 1 if wide > 1 else 0
        self.sums = []
        length = narrow * chunk
        for place in range(self.narrow_bits):
            length //= 2
            self.sums.append(("narrow", place, length, True))
        for place in range(self.wide_bits):
            halve = place < split_bits
            length = length // 2 if halve else length
            self.sums.append(("wide", place, length, halve))
        self.last = length
        self.gathers = []
        for place in reversed(range(split_bits)):
            self.gathers.append(("wide", place, length))
            length *= 2
        self.split_bits = split_bits
        self.depth = len(self.sums) + len(self.gathers)
        self.phases = []
        start = 0
        for rows_block, windows in (
            (ff // narrow, 1),
            (rows, ff // width),
            (rows, 1),
            (rows, 3),
        ):
            count = rows_block // chunk * windows
            self.phases.append((start, count, rows_block, windows))
            start += count
        self.chunks = start
        self.ff_jobs = ff // TILE
        self.norm_job = self.ff_jobs
        self.mix_job = self.norm_job + 1
        self.item_job = self.mix_job + 1
        self.pack_job = self.item_job + items
        self.first_job = self.pack_job + 1
        self.input_job = self.first_job + 1
        self.vector_tick = self.input_job + 1
        assert self.phases[1][0] >= self.norm_job
        assert self.phases[2][0] >= self.mix_job
        assert self.phases[3][0] >= self.first_job
        self.vector_rows = 8 + ff // width
        self.vector_rows += -self.vector_rows % SUB
        self.ticks = self.chunks + self.depth + 1
        assert self.vector_tick + len(self.sums) < self.ticks


def gelu_parts(hidden):
    normal = 0.5 + 0.5 * lax.erf(hidden * ROOT_HALF)
    return normal


def layer_kernel(plan, names, *refs):
    r = types.SimpleNamespace(**dict(zip(names, refs)))
    width, chunk, narrow, slots = plan.width, plan.chunk, plan.narrow, plan.slots
    rows, padded, pairs = plan.rows, plan.padded, plan.pairs
    landed = [getattr(r, f"land{stage}") for stage in range(len(plan.sums))]
    score_scale = HEAD_DIM ** (-0.5)
    spots = {"narrow": lax.axis_index("narrow"), "wide": lax.axis_index("wide")}

    def partner(axis, place):
        return {
            "wide": flip(spots["wide"], place) if axis == "wide" else spots["wide"],
            "narrow": flip(spots["narrow"], place) if axis == "narrow" else spots["narrow"],
        }

    loads = {}
    for number, name in enumerate(("tok", "jw", "mw", "ew", "sw", "cot")):
        loads[name] = pltpu.make_async_copy(
            getattr(r, name + "_in"), getattr(r, name), r.load_sems.at[number]
        )
        loads[name].start()

    barrier = pltpu.get_barrier_semaphore() if plan.sums else None
    for axis, place, _, _ in plan.sums:
        pl.semaphore_signal(barrier, inc=1, device_id=partner(axis, place), device_id_type=MESH)

    def vector(row):
        return r.vec[row : row + 1, :]

    def item_rows(item):
        return aligned(item * slots, slots, SUB)

    def row_live(item):
        return lax.broadcasted_iota(jnp.int32, (slots, 1), 0) < r.visible[item]

    lanes = lax.broadcasted_iota(jnp.int32, (slots, 2 * HEAD_DIM), 1)
    first_head = lanes < HEAD_DIM

    def both_heads(value):
        zero = jnp.zeros_like(value)
        return jnp.concatenate(
            [jnp.where(first_head, value, zero), jnp.where(first_head, zero, value)], axis=0
        ).astype(BF16)

    def one_head_each(value):
        return jnp.where(first_head, value[:slots], value[slots:])

    def normalized(values):
        center = values - jnp.mean(values, axis=-1, keepdims=True)
        spread = lax.rsqrt(jnp.mean(center * center, axis=-1, keepdims=True) + EPSILON)
        return center * spread, spread

    def norm_backward(grad, unit, spread):
        return spread * (
            grad
            - jnp.mean(grad, axis=-1, keepdims=True)
            - unit * jnp.mean(grad * unit, axis=-1, keepdims=True)
        )

    def each_item(body):
        lax.fori_loop(0, plan.items, lambda item, carry: (body(item), carry)[1], 0)

    def each_tile(count, body):
        lax.fori_loop(0, count, lambda tile, carry: (body(tile), carry)[1], 0)

    def pair_lanes(part, pair):
        start = part * width + pair * 2 * HEAD_DIM
        return slice(start, start + 2 * HEAD_DIM)

    r.stage[rows:, :] = jnp.zeros((padded - rows, width), F32)
    r.sums[...] = jnp.zeros_like(r.sums)
    loads["tok"].wait()

    def first_norm(item):
        unit, _ = normalized(r.tok[item].astype(F32))
        r.stage[item_rows(item), :] = unit * vector(0) + vector(1)

    each_item(first_norm)
    r.rowb[...] = r.stage[...].astype(BF16)
    loads["jw"].wait()
    for part, bias in enumerate((2, None, 3)):

        def joint_tile(tile):
            cols = aligned(part * width + tile * TILE, TILE, TILE)
            value = matmul(r.rowb[...], r.jw[:, cols])
            if bias is not None:
                value = value + r.vec[bias : bias + 1, aligned(tile * TILE, TILE, TILE)]
            r.qkv[:, cols] = value.astype(BF16).astype(F32)

        each_tile(width // TILE, joint_tile)
    r.first_t[...] = r.stage[...].T.astype(BF16)
    r.qkv[rows:, :] = jnp.zeros((padded - rows, 3 * width), F32)

    def attend_item(item):
        here = item_rows(item)
        key_live = (
            lax.broadcasted_iota(jnp.int32, (2 * slots, slots), 1) < r.visible[item]
        )
        for pair in range(pairs):
            query = both_heads(r.qkv[here, pair_lanes(0, pair)])
            keys = r.qkv[here, pair_lanes(1, pair)].astype(BF16)
            values = r.qkv[here, pair_lanes(2, pair)].astype(BF16)
            logits = matmul(query, keys, ((1,), (1,))) * score_scale
            logits = jnp.where(key_live, logits, -1000000000.0)
            expo = jnp.exp(logits - jnp.max(logits, axis=-1, keepdims=True))
            attend = expo * (1.0 / jnp.sum(expo, axis=-1, keepdims=True))
            r.attend[item * pairs + pair] = attend
            mixed = one_head_each(matmul(attend.astype(BF16), values))
            r.stage[here, pair_lanes(0, pair)] = mixed

    each_item(attend_item)
    r.rowb[...] = r.stage[...].astype(BF16)
    loads["mw"].wait()

    def mixer_tile(tile):
        cols = aligned(tile * TILE, TILE, TILE)
        r.middle[:, cols] = matmul(r.rowb[...], r.mw[:, cols]) + r.vec[4:5, cols]

    each_tile(width // TILE, mixer_tile)
    r.mixed_t[...] = r.stage[...].T.astype(BF16)

    def second_norm(item):
        here = item_rows(item)
        middle = r.middle[here, :] + r.tok[item].astype(F32)
        r.middle[here, :] = middle
        unit, _ = normalized(middle)
        r.stage[here, :] = unit * vector(5) + vector(6)

    each_item(second_norm)
    r.second[...] = r.stage[...].astype(BF16)
    loads["ew"].wait()

    def expand_bias(tile):
        per_row = width // TILE
        return r.vec[
            pl.ds(8 + lax.div(tile, per_row), 1),
            aligned(lax.rem(tile, per_row) * TILE, TILE, TILE),
        ]

    def expand_tile(tile):
        cols = aligned(tile * TILE, TILE, TILE)
        hidden = matmul(r.second[...], r.ew[:, cols]) + expand_bias(tile)
        active = hidden * gelu_parts(hidden)
        r.wide_rows[:, cols] = active.astype(BF16)
        r.active_t[cols, :] = active.T.astype(BF16)

    each_tile(plan.ff_jobs, expand_tile)
    r.second_t[...] = r.stage[...].T.astype(BF16)
    loads["cot"].wait()

    def mask_cotangent(item):
        grad = r.cot[item].astype(F32)
        r.stage[item_rows(item), :] = jnp.where(row_live(item), grad, 0.0)

    each_item(mask_cotangent)
    r.grad_out[...] = r.stage[...].astype(BF16)
    loads["sw"].wait()

    def ff_job(tile):
        cols = aligned(tile * TILE, TILE, TILE)
        output = matmul(r.wide_rows[:, cols], r.sw[cols, :])
        hidden = matmul(r.second[...], r.ew[:, cols]) + expand_bias(tile)
        grad = matmul(r.grad_out[...], r.sw[cols, :], ((1,), (1,)))
        slope = gelu_parts(hidden) + hidden * (PEAK * jnp.exp(-0.5 * hidden * hidden))
        grad_hidden = (grad * slope).astype(BF16)
        r.wide_rows[:, cols] = grad_hidden
        r.expand_sums[tile] = jnp.sum(grad_hidden.astype(F32), axis=0, keepdims=True)
        grad_second = matmul(grad_hidden, r.ew[:, cols], ((1,), (1,)))

        @pl.when(tile == 0)
        def _():
            r.acc_out[...] = output
            r.acc_grad[...] = grad_second

        @pl.when(tile > 0)
        def _():
            r.acc_out[...] += output
            r.acc_grad[...] += grad_second

    def norm_job():
        def one(item):
            here = item_rows(item)
            live = row_live(item)
            middle = r.middle[here, :]
            grad_out = jnp.where(live, r.cot[item].astype(F32), 0.0)
            layer_out = jnp.where(live, middle + (r.acc_out[here, :] + vector(7)), 0.0)
            r.cot[item] = layer_out.astype(BF16)
            unit, spread = normalized(middle)
            grad = r.acc_grad[here, :]
            r.sums[5:6, :] += jnp.sum(grad * unit, axis=0, keepdims=True)
            r.sums[6:7, :] += jnp.sum(grad, axis=0, keepdims=True)
            r.sums[7:8, :] += jnp.sum(grad_out, axis=0, keepdims=True)
            grad_middle = grad_out + norm_backward(grad * vector(5), unit, spread)
            r.acc_out[here, :] = grad_middle
            r.sums[4:5, :] += jnp.sum(
                grad_middle.astype(BF16).astype(F32), axis=0, keepdims=True
            )

        each_item(one)
        r.grad_branch[:rows_full, :] = r.acc_out[:rows_full, :].astype(BF16)
        tail = jnp.concatenate(
            [r.acc_out[rows_full:rows, :], jnp.zeros((padded - rows, width), F32)], axis=0
        )
        r.grad_branch[rows_full:, :] = tail.astype(BF16)
        layer_copy().start()

    rows_full = rows // 16 * 16

    def layer_copy():
        return pltpu.make_async_copy(r.cot, r.layer_out, r.load_sems.at[0])

    def input_copy():
        return pltpu.make_async_copy(r.tok, r.input_grad, r.load_sems.at[1])

    def mix_job():
        def one(tile):
            cols = aligned(tile * TILE, TILE, TILE)
            value = matmul(r.grad_branch[...], r.mw[cols, :], ((1,), (1,)))
            r.stage[:, cols] = value.astype(BF16).astype(F32)

        each_tile(width // TILE, one)

    def item_job(item):
        here = item_rows(item)
        for pair in range(pairs):
            query = both_heads(r.qkv[here, pair_lanes(0, pair)])
            keys = r.qkv[here, pair_lanes(1, pair)].astype(BF16)
            values = r.qkv[here, pair_lanes(2, pair)].astype(BF16)
            grad_mixed = both_heads(r.stage[here, pair_lanes(0, pair)])
            attend = r.attend[item * pairs + pair]
            grad_attend = matmul(grad_mixed, values, ((1,), (1,)))
            grad_value = matmul(attend.astype(BF16), grad_mixed, ((0,), (0,)))
            inner = jnp.sum(attend * grad_attend, axis=-1, keepdims=True)
            grad_logits = (attend * (grad_attend - inner)).astype(BF16)
            grad_query = one_head_each(matmul(grad_logits, keys)) * score_scale
            grad_key = matmul(grad_logits, query, ((0,), (0,))) * score_scale
            r.qkv[here, pair_lanes(0, pair)] = grad_query
            r.qkv[here, pair_lanes(1, pair)] = grad_key
            r.qkv[here, pair_lanes(2, pair)] = grad_value

    def joint_rows(part):
        return slice(part * padded, (part + 1) * padded)

    def pack_job():
        for part in range(3):
            value = r.qkv[:, part * width : (part + 1) * width].astype(BF16)
            r.sw[joint_rows(part), :] = value
            if part != 1:
                row = 2 if part == 0 else 3
                r.sums[row : row + 1, :] = jnp.sum(value.astype(F32), axis=0, keepdims=True)

    def first_job():
        def one(tile):
            cols = aligned(tile * TILE, TILE, TILE)
            total = None
            for part in range(3):
                value = matmul(
                    r.sw[joint_rows(part), :],
                    r.jw[cols, part * width : (part + 1) * width],
                    ((1,), (1,)),
                )
                total = value if total is None else total + value
            r.acc_grad[:, cols] = total

        each_tile(width // TILE, one)

    def input_job():
        def one(item):
            here = item_rows(item)
            unit, spread = normalized(r.tok[item].astype(F32))
            grad = r.acc_grad[here, :]
            r.sums[0:1, :] += jnp.sum(grad * unit, axis=0, keepdims=True)
            r.sums[1:2, :] += jnp.sum(grad, axis=0, keepdims=True)
            total = r.acc_out[here, :] + norm_backward(grad * vector(0), unit, spread)
            r.tok[item] = total.astype(BF16)

        each_item(one)
        per_row = width // TILE
        for tile in range(plan.ff_jobs):
            row, start = 8 + tile // per_row, tile % per_row * TILE
            r.sums[row : row + 1, start : start + TILE] = r.expand_sums[tile]
        input_copy().start()

    def source(stage, item):
        if stage == 0:
            return r.part.at[lax.rem(item, 2)]
        return landed[stage - 1].at[lax.rem(item, DEPTH)]

    def piece_start(bits):
        start = 0
        for place in range(bits):
            start = start + bit_of(spots["wide"], place) * (chunk // 2 ** (place + 1))
        return start

    def exchange(stage, item):
        slot = lax.rem(item, DEPTH)
        if stage < len(plan.sums):
            axis, place, length, halve = plan.sums[stage]
            there = (1 - bit_of(spots[axis], place)) * length if halve else 0
            src = source(stage, item).at[aligned(there, length, SUB)]
            dst = landed[stage].at[slot]
        else:
            axis, place, length = plan.gathers[stage - len(plan.sums)]
            src = r.whole.at[item, aligned(piece_start(place + 1), length, SUB)]
            dst = src
        return pltpu.make_async_remote_copy(
            src_ref=src,
            dst_ref=dst,
            send_sem=r.send_sems.at[stage, slot],
            recv_sem=r.recv_sems.at[stage, slot],
            device_id=partner(axis, place),
            device_id_type=MESH,
        )

    def produce(item):
        slot = lax.rem(item, 2)
        lefts = (r.active_t, r.second_t, r.mixed_t, r.first_t)
        rights = (r.grad_out, r.wide_rows, r.grad_branch, r.sw)
        for number, (start, count, rows_block, windows) in enumerate(plan.phases):
            left, right = lefts[number], rights[number]

            @pl.when((item >= start) & (item < start + count))
            def _():
                local = item - start
                row = lax.div(local, windows) * chunk
                window = lax.rem(local, windows)
                picked = [
                    left[
                        aligned(
                            reversed_bits(spot, plan.narrow_bits) * rows_block + row, chunk, chunk
                        ),
                        :,
                    ]
                    for spot in range(narrow)
                ]
                if number == 3:
                    other = right[aligned(window * padded, padded, 256), :]
                else:
                    other = right[:, aligned(window * width, width, 128)]
                r.part[slot] = matmul(jnp.concatenate(picked, axis=0), other)

    def absorb(stage, item):
        axis, place, length, halve = plan.sums[stage]
        here = bit_of(spots[axis], place) * length if halve else 0
        slot = lax.rem(item, DEPTH)
        landed[stage][slot] += source(stage, item)[aligned(here, length, SUB)]

    def result_copy(item, act):
        outs = (r.out_shrink, r.out_expand, r.out_mixer, r.out_joint)
        for (start, count, _, windows), out in zip(plan.phases, outs):

            @pl.when((item >= start) & (item < start + count))
            def _():
                local = item - start
                row = lax.div(local, windows) * chunk
                col = lax.rem(local, windows) * width
                copy = pltpu.make_async_copy(
                    r.whole.at[item],
                    out.at[aligned(row, chunk, chunk), aligned(col, width, 128)],
                    r.out_sems.at[lax.rem(item, 2)],
                )
                if act == "start":
                    copy.start()
                else:
                    copy.wait()

    def vector_exchange(stage):
        axis, place, _, _ = plan.sums[stage]
        return pltpu.make_async_remote_copy(
            src_ref=r.sums if stage == 0 else r.vector_land.at[stage - 1],
            dst_ref=r.vector_land.at[stage],
            send_sem=r.vector_sems.at[0, stage],
            recv_sem=r.vector_sems.at[1, stage],
            device_id=partner(axis, place),
            device_id_type=MESH,
        )

    def vector_step(tick):
        count = len(plan.sums)
        for stage in range(count + 1):

            @pl.when(tick == plan.vector_tick + stage)
            def _():
                if stage > 0:
                    vector_exchange(stage - 1).wait()
                    before = r.sums if stage == 1 else r.vector_land.at[stage - 2]
                    r.vector_land[stage - 1] += before[...]
                if stage < count:
                    vector_exchange(stage).start()

    if plan.sums:
        pl.semaphore_wait(barrier, len(plan.sums))

    def step(tick, carry):
        @pl.when(tick < plan.chunks)
        def _():
            produce(tick)
            if plan.depth:
                exchange(0, tick).start()
            else:
                r.whole[tick] = r.part[lax.rem(tick, 2)]
                result_copy(tick, "start")

        for stage in range(plan.depth):
            item = tick - 1 - stage

            @pl.when((item >= 0) & (item < plan.chunks))
            def _():
                exchange(stage, item).wait()
                if stage < len(plan.sums):
                    absorb(stage, item)
                if stage == len(plan.sums) - 1:
                    r.whole[item, aligned(piece_start(plan.split_bits), plan.last, SUB)] = landed[
                        stage
                    ][lax.rem(item, DEPTH)]
                if stage + 1 < plan.depth:
                    exchange(stage + 1, item).start()
                else:
                    result_copy(item, "start")

        done = tick - 1 - plan.depth

        @pl.when(done >= 0)
        def _():
            result_copy(done, "wait")

        vector_step(tick)
        pl.when(tick < plan.ff_jobs)(lambda: ff_job(tick))
        pl.when(tick == plan.norm_job)(norm_job)
        pl.when(tick == plan.mix_job)(mix_job)
        pl.when((tick >= plan.item_job) & (tick < plan.pack_job))(
            lambda: item_job(tick - plan.item_job)
        )
        pl.when(tick == plan.pack_job)(pack_job)
        pl.when(tick == plan.first_job)(first_job)
        pl.when(tick == plan.input_job)(input_job)
        return carry

    lax.fori_loop(0, plan.ticks, step, 0)
    r.vector_out[...] = r.vector_land[len(plan.sums) - 1] if plan.sums else r.sums[...]
    layer_copy().wait()
    input_copy().wait()


def shards(
    tokens,
    visible,
    first_gain,
    first_shift,
    joint_weight,
    query_bias,
    value_bias,
    mixer_weight,
    mixer_bias,
    second_gain,
    second_shift,
    expand_weight,
    expand_bias,
    shrink_weight,
    shrink_bias,
    cotangent,
):
    items, slots, width = tokens.shape
    ff = expand_weight.shape[1]
    narrow, wide = lax.axis_size("narrow"), lax.axis_size("wide")
    plan = Plan(narrow, wide, items, slots, width, ff, SUB if wide > 1 else TILE)
    padded, chunk = plan.padded, plan.chunk
    vectors = jnp.stack(
        [
            first_gain,
            first_shift,
            query_bias,
            value_bias,
            mixer_bias,
            second_gain,
            second_shift,
            shrink_bias,
            *expand_bias.reshape(ff // width, width),
        ]
    ).astype(F32)
    hbm = pl.BlockSpec(memory_space=pl.ANY)
    vmem = pl.BlockSpec(memory_space=pltpu.VMEM)
    smem = pl.BlockSpec(memory_space=pltpu.SMEM)
    inputs = {
        "visible": (visible, smem),
        "vec": (vectors, vmem),
        "tok_in": (tokens, hbm),
        "cot_in": (cotangent, hbm),
        "jw_in": (joint_weight, hbm),
        "mw_in": (mixer_weight, hbm),
        "ew_in": (expand_weight, hbm),
        "sw_in": (shrink_weight, hbm),
    }
    block = width // narrow
    outputs = {
        "layer_out": (tokens.shape, BF16, hbm),
        "input_grad": (tokens.shape, BF16, hbm),
        "out_shrink": ((ff // narrow, width), F32, hbm),
        "out_expand": ((block, ff), F32, hbm),
        "out_mixer": ((block, width), F32, hbm),
        "out_joint": ((block, 3 * width), F32, hbm),
        "vector_out": ((plan.vector_rows, width), F32, vmem),
    }
    scratch = {
        "tok": pltpu.VMEM(tokens.shape, BF16),
        "cot": pltpu.VMEM(tokens.shape, BF16),
        "jw": pltpu.VMEM(joint_weight.shape, BF16),
        "mw": pltpu.VMEM(mixer_weight.shape, BF16),
        "ew": pltpu.VMEM(expand_weight.shape, BF16),
        "sw": pltpu.VMEM(shrink_weight.shape, BF16),
        "stage": pltpu.VMEM((padded, width), F32),
        "rowb": pltpu.VMEM((padded, width), BF16),
        "qkv": pltpu.VMEM((padded, 3 * width), F32),
        "attend": pltpu.VMEM((items * plan.pairs, 2 * slots, slots), F32),
        "first_t": pltpu.VMEM((width, padded), BF16),
        "mixed_t": pltpu.VMEM((width, padded), BF16),
        "second": pltpu.VMEM((padded, width), BF16),
        "second_t": pltpu.VMEM((width, padded), BF16),
        "middle": pltpu.VMEM((padded, width), F32),
        "wide_rows": pltpu.VMEM((padded, ff), BF16),
        "active_t": pltpu.VMEM((ff, padded), BF16),
        "grad_out": pltpu.VMEM((padded, width), BF16),
        "acc_out": pltpu.VMEM((padded, width), F32),
        "acc_grad": pltpu.VMEM((padded, width), F32),
        "grad_branch": pltpu.VMEM((padded, width), BF16),
        "sums": pltpu.VMEM((plan.vector_rows, width), F32),
        "expand_sums": pltpu.VMEM((plan.ff_jobs, 1, TILE), F32),
        "part": pltpu.VMEM((2, narrow * chunk, width), F32),
        "whole": pltpu.VMEM((plan.chunks, chunk, width), F32),
        "load_sems": pltpu.SemaphoreType.DMA((6,)),
        "out_sems": pltpu.SemaphoreType.DMA((2,)),
    }
    if plan.sums:
        for stage, (_, _, length, _) in enumerate(plan.sums):
            scratch[f"land{stage}"] = pltpu.VMEM((DEPTH, length, width), F32)
        scratch["vector_land"] = pltpu.VMEM((len(plan.sums), plan.vector_rows, width), F32)
        scratch["vector_sems"] = pltpu.SemaphoreType.DMA((2, len(plan.sums)))
        scratch["send_sems"] = pltpu.SemaphoreType.DMA((plan.depth, DEPTH))
        scratch["recv_sems"] = pltpu.SemaphoreType.DMA((plan.depth, DEPTH))
    remote = {"collective_id": 0} if plan.sums else {}
    results = pl.pallas_call(
        functools.partial(layer_kernel, plan, (*inputs, *outputs, *scratch)),
        out_shape=[jax.ShapeDtypeStruct(shape, kind) for shape, kind, _ in outputs.values()],
        in_specs=[spec for _, spec in inputs.values()],
        out_specs=[spec for _, _, spec in outputs.values()],
        scratch_shapes=list(scratch.values()),
        compiler_params=pltpu.CompilerParams(
            has_side_effects=True, vmem_limit_bytes=61 * 2**20, **remote
        ),
        name="layer",
    )(*(value for value, _ in inputs.values()))
    layer_out, input_grad, shrink, expand, mixer, joint, sums = results
    own = lax.axis_index("narrow")
    mine = lax.dynamic_slice_in_dim(sums[:8], own * block, block, axis=1)
    wide_sums = sums[8 : 8 + ff // width].reshape(ff)
    expand_sum = lax.dynamic_slice_in_dim(wide_sums, own * (ff // narrow), ff // narrow)
    return (
        layer_out,
        input_grad,
        mine[0],
        mine[1],
        joint,
        mine[2],
        mine[3],
        mixer,
        mine[4],
        mine[5],
        mine[6],
        expand,
        expand_sum,
        shrink,
        mine[7],
    )


def solution(mesh):
    return jax.shard_map(
        shards,
        mesh=mesh,
        in_specs=(
            P(("wide", "narrow"), None, None),
            P(("wide", "narrow")),
            P(),
            P(),
            P(),
            P(),
            P(),
            P(),
            P(),
            P(),
            P(),
            P(),
            P(),
            P(),
            P(),
            P(("wide", "narrow"), None, None),
        ),
        out_specs=(
            P(("wide", "narrow"), None, None),
            P(("wide", "narrow"), None, None),
            P("narrow"),
            P("narrow"),
            P("narrow", None),
            P("narrow"),
            P("narrow"),
            P("narrow", None),
            P("narrow"),
            P("narrow"),
            P("narrow"),
            P("narrow", None),
            P("narrow"),
            P("narrow", None),
            P("narrow"),
        ),
        check_vma=False,
    )
```

time: 460 us -> 240 us (0.52); the launches traced: 454 us -> 239 us
  local copies, waits for them, and re-layouts: 150 us -> 19.9 us
  matrix products: 72.4 us -> 0 us
  other arithmetic: 33.9 us -> 0.63 us
  Pallas kernels: 197 us -> 218 us
    dot_general x14 -> x0, matrix products: 72.4 us -> none  [the longest x4 35.5 us: contract_cols(): lax.dot_general(left_mat, right_mat, (((1,), (1,)), ((), ())), preferred_...]
    reshape x25 -> x1, local copies, waits for them, and re-layouts: 67.6 us -> 0.01 us  [shards(): wide_sums = sums[8:8 + ff // width].reshape(ff)]
    pallas_call x1, Pallas kernels: 197 us -> 218 us  [shards(): pl.pallas_call(functools.partial(layer_kernel, plan, (*inputs, *outputs,...]
    convert_element_type x7 -> x0, local copies, waits for them, and re-layouts: 17.3 us -> none  [the longest x2 6.19 us: shards(): mixed_low = mixed_low.reshape(row_count, model_width).astype(jnp.bfloat16)]
    convert_element_type x18 -> x1, other arithmetic: 17.9 us -> 0.63 us  [shards(): vectors = jnp.stack([first_gain, first_shift, query_bias, value_bias, mix...]
    unnamed x128 -> x14, local copies, waits for them, and re-layouts: 27.3 us -> 10.6 us
    reduce_sum x11 -> x0, other arithmetic: 14.3 us -> none  [the longest x3 6.77 us: normalize(): return center * lax.rsqrt(spread + EPSILON) * gain_vec + shift_vec]
    transpose x4 -> x0, local copies, waits for them, and re-layouts: 11.9 us -> none  [reduce_gradients(): operands.append(jnp.pad(left, ((0, extra), (0, 0))).T)]
where the time goes in v2:
time: 240 us; the launch traced here: 239 us
  Pallas kernels  218 us (91%)
  local copies, waits for them, and re-layouts  19.9 us (8%)
    pallas_call x1, Pallas kernels, shards(): pl.pallas_call(functools.partial(layer_kernel, plan, (*inputs, *outputs,...  218 us
    unnamed x14, local copies, waits for them, and re-layouts  10.6 us
    another operation x9, local copies, waits for them, and re-layouts, shards(): jnp.stack([first_gain, first_shift, query_bias, value_bias, mixer_bias, s...  5.56 us

profile of v2, /device:TPU:0, one launch (start us, length us, event | category | flops | bytes accessed | tf_op | source)
XLA Modules:
  0.0 239.3 jit_solution(15923392055724418168)
XLA Ops:
  0.6 0.7 stack.27
  1.3 0.7 stack.28
  2.0 0.7 stack.29
  2.7 0.7 stack.30
  3.4 0.7 stack.31
  4.1 0.7 stack.32
  4.8 0.7 stack.33
  5.4 0.7 stack.34
  6.1 0.8 fusion.1
  6.9 0.1 stack.35
  7.0 0.6 convert_element_type.3.refs_1_
  7.7 218.0 %layer.1 = (bf16[7,72,768]{2,1,0:T(8,128)(2,1)}, bf16[7,72,768]{2,1,0:T(8,128)(2,1)}, f32[768,768]{1,0:T(8,128)}, f32[192,3072]{1,0:T(8,128)}, f32[192,768]{1,0:...) custom-call(s32[7]{0:T(128)} %refs_0_.1, f32[12,768]{1,0:T(8,128)} %convert_element_type.3.refs_1_, ...), custom_call_target="tpu_custom_call" | custom-call | tf_op jit(solution)/shard_map/layer/pallas_call | solution.py:650
  225.7 0.0 copy-start.2
  225.7 0.9 slice.42
  226.6 0.7 slice.34
  227.3 0.7 fusion
  228.0 0.7 dynamic_slice.7
  228.7 2.1 copy.37
  230.7 0.0 copy-start.3
  230.7 2.1 copy.38
  232.9 0.0 copy-done.2
  232.9 0.0 copy-start.1
  232.9 1.2 copy.39
  234.1 0.0 copy-done.3
  234.1 0.8 copy.40
  234.9 0.5 copy-done.1
  235.4 0.0 copy-start
  235.4 1.4 copy.41
  236.8 1.1 copy-done
  237.9 1.4 copy.42
  (5 shorter events, 0.0 us)
Async XLA Ops:
  225.7 7.1 %copy-start.2 = (f32[192,2304]{1,0:T(8,128)S(1)}, f32[192,2304]{1,0:T(8,128)}, u32[]{:S(2)}) copy-start(f32[192,2304]{1,0:T(8,128)} %get-tuple-element.60) | copy-start | bytes 5308420
  230.7 3.3 %copy-start.3 = (f32[192,768]{1,0:T(8,128)S(1)}, f32[192,768]{1,0:T(8,128)}, u32[]{:S(2)}) copy-start(f32[192,768]{1,0:T(8,128)} %get-tuple-element.63) | copy-start | bytes 1769476
  232.9 2.5 %copy-start.1 = (f32[192,3072]{1,0:T(8,128)S(1)}, f32[192,3072]{1,0:T(8,128)}, u32[]{:S(2)}) copy-start(f32[192,3072]{1,0:T(8,128)} %get-tuple-element.67) | copy-start | bytes 7077892
  235.4 2.5 %copy-start = (f32[768,768]{1,0:T(8,128)S(1)}, f32[768,768]{1,0:T(8,128)}, u32[]{:S(2)}) copy-start(f32[768,768]{1,0:T(8,128)} %get-tuple-element.69) | copy-start | bytes 7077892

commit v3 on v2

--- a/solution.py
+++ b/solution.py
@@ -11,7 +11,8 @@
 HEAD_DIM = 64
 EPSILON = 1e-06
 SUB = 8
-DEPTH = 6
+LAGS = ([1, 2, 2, 2, 2, 2, 2, 2], [1, 2, 2, 2, 2, 2, 2, 2])
+MOST = 32
 TILE = 256
 MESH = pl.DeviceIdType.MESH
 ROOT_HALF = 0.5**0.5
@@ -20,10 +21,6 @@
 F32 = jnp.float32
 
 
-def flip(index, place):
-    return index + (1 - 2 * lax.rem(lax.div(index, 2**place), 2)) * 2**place
-
-
 def bit_of(index, place):
     return lax.rem(lax.div(index, 2**place), 2)
 
@@ -43,37 +40,111 @@
     return lax.dot_general(left, right, (contract, ((), ())), preferred_element_type=F32)
 
 
+class Move:
+    def __init__(self, kind, flips, length, select=None, inner=False):
+        self.kind, self.flips, self.length = kind, flips, length
+        self.select, self.inner = select, inner
+
+
+class Part:
+    def __init__(self, column, columns, picks, sums, gathers, selects):
+        self.column, self.columns, self.picks = column, columns, picks
+        self.sums, self.moves = sums, sums + gathers
+        self.selects = selects
+        self.lags = LAGS[column > 0] if len(self.moves) == 8 else [1] + [2] * (len(self.moves) - 1)
+        self.due = [sum(self.lags[: stage + 1]) for stage in range(len(self.moves))]
+
+    def slots(self, stage):
+        after = self.lags[stage + 1] if stage + 1 < len(self.sums) else 0
+        count = 2 * self.lags[stage] + after + 2
+        if self.moves[stage].kind in ("fold", "unfold"):
+            kinds = [move.kind for move in self.moves]
+            ahead = self.due[kinds.index("unfold")] - self.due[kinds.index("fold") - 1]
+            count = max(count, ahead + 2)
+        return count
+
+
 class Plan:
-    def __init__(self, narrow, wide, items, slots, width, ff, least=SUB):
+    def __init__(self, narrow, wide, items, slots, width, ff):
         self.narrow, self.wide, self.width, self.ff = narrow, wide, width, ff
         self.items, self.slots = items, slots
         self.rows = items * slots
         self.padded = self.rows + -self.rows % 256
         self.pairs = width // (2 * HEAD_DIM)
-        self.narrow_bits = narrow.bit_length() - 1
-        self.wide_bits = wide.bit_length() - 1
+        narrow_bits = self.narrow_bits = narrow.bit_length() - 1
+        wide_bits = self.wide_bits = wide.bit_length() - 1
         rows = width // narrow
-        chunk = least
-        while rows % (2 * chunk) == 0 and chunk < SUB * wide:
+        chunk = SUB
+        while rows % (2 * chunk) == 0 and chunk < MOST:
             chunk *= 2
         self.chunk = chunk
-        split_bits = (chunk // SUB).bit_length() - 1 if wide > 1 else 0
-        self.sums = []
-        length = narrow * chunk
-        for place in range(self.narrow_bits):
-            length //= 2
-            self.sums.append(("narrow", place, length, True))
-        for place in range(self.wide_bits):
-            halve = place < split_bits
-            length = length // 2 if halve else length
-            self.sums.append(("wide", place, length, halve))
-        self.last = length
-        self.gathers = []
-        for place in reversed(range(split_bits)):
-            self.gathers.append(("wide", place, length))
-            length *= 2
-        self.split_bits = split_bits
-        self.depth = len(self.sums) + len(self.gathers)
+        near, mirror = (("wide", 1),), (("wide", 1), ("wide", 2))
+        x, y, core = (("wide", 0),), (("narrow", 1),), (("narrow", 0),)
+        if (narrow, wide) == (4, 8):
+            self.links = (core, y, x, near, mirror)
+            half, quarter = chunk // 2, chunk // 4
+            z_bit, x_bit, y_bit, core_bit = ("wide", 2), x[0], y[0], core[0]
+            one = Part(
+                0,
+                width // 3 * 2,
+                [(spot % 2 * 2 + spot // 2, 0, chunk) for spot in range(4)],
+                [
+                    Move("halve", core, 2 * chunk, core_bit),
+                    Move("halve", y, chunk, y_bit),
+                    Move("fold", near, chunk),
+                    Move("halve", mirror, half, z_bit, True),
+                    Move("halve", x, quarter, x_bit, True),
+                ],
+                [
+                    Move("double", x, quarter, inner=True),
+                    Move("double", mirror, half, inner=True),
+                    Move("unfold", near, chunk),
+                ],
+                [(z_bit, half), (x_bit, quarter)],
+            )
+            two = Part(
+                width // 3 * 2,
+                width // 3,
+                [
+                    (2 * (spot % 2) + spot // 4, spot // 2 % 2 * half, half)
+                    for spot in range(8)
+                ],
+                [
+                    Move("halve", core, 2 * chunk, core_bit),
+                    Move("halve", x, chunk, x_bit),
+                    Move("halve", y, half, y_bit),
+                    Move("fold", near, half),
+                    Move("halve", mirror, quarter, z_bit, True),
+                ],
+                [
+                    Move("double", mirror, quarter, inner=True),
+                    Move("unfold", near, half),
+                    Move("double", x, half),
+                ],
+                [(x_bit, half), (z_bit, quarter)],
+            )
+            self.parts = (one, two)
+        else:
+            self.links = tuple((("narrow", place),) for place in range(narrow_bits))
+            self.links += tuple((("wide", place),) for place in range(wide_bits))
+            sums, gathers, selects = [], [], []
+            length = narrow * chunk
+            for (axis, place), in self.links:
+                if length > SUB:
+                    length //= 2
+                    sums.append(Move("halve", ((axis, place),), length, (axis, place)))
+                    if axis == "wide":
+                        selects.append(((axis, place), length))
+                        gathers.insert(0, Move("double", ((axis, place),), length))
+                else:
+                    sums.append(Move("add", ((axis, place),), length))
+            picks = [(reversed_bits(spot, narrow_bits), 0, chunk) for spot in range(narrow)]
+            self.parts = (Part(0, width, picks, sums, gathers, selects),)
+        self.stages = max(len(part.moves) for part in self.parts)
+        self.depth = max(part.due[-1] for part in self.parts)
+        self.slots_most = max(
+            part.slots(stage) for part in self.parts for stage in range(len(part.moves))
+        )
         self.phases = []
         start = 0
         for rows_block, windows in (
@@ -93,14 +164,16 @@
         self.pack_job = self.item_job + items
         self.first_job = self.pack_job + 1
         self.input_job = self.first_job + 1
-        self.vector_tick = self.input_job + 1
-        assert self.phases[1][0] >= self.norm_job
-        assert self.phases[2][0] >= self.mix_job
-        assert self.phases[3][0] >= self.first_job
+        self.stride = self.phases[1][0] // self.ff_jobs
+        self.vector_tick = (self.input_job + 1) * self.stride
+        assert self.stride >= 1
+        assert self.phases[2][0] > self.mix_job * self.stride
+        assert self.phases[3][0] > self.first_job * self.stride
         self.vector_rows = 8 + ff // width
         self.vector_rows += -self.vector_rows % SUB
         self.ticks = self.chunks + self.depth + 1
-        assert self.vector_tick + len(self.sums) < self.ticks
+        self.vector_every = (self.ticks - 1 - self.vector_tick) // len(self.links)
+        assert self.vector_every > 0
 
 
 def gelu_parts(hidden):
@@ -112,15 +185,22 @@
     r = types.SimpleNamespace(**dict(zip(names, refs)))
     width, chunk, narrow, slots = plan.width, plan.chunk, plan.narrow, plan.slots
     rows, padded, pairs = plan.rows, plan.padded, plan.pairs
-    landed = [getattr(r, f"land{stage}") for stage in range(len(plan.sums))]
     score_scale = HEAD_DIM ** (-0.5)
     spots = {"narrow": lax.axis_index("narrow"), "wide": lax.axis_index("wide")}
-
-    def partner(axis, place):
-        return {
-            "wide": flip(spots["wide"], place) if axis == "wide" else spots["wide"],
-            "narrow": flip(spots["narrow"], place) if axis == "narrow" else spots["narrow"],
-        }
+    inner = bit_of(spots["wide"], 1) != bit_of(spots["wide"], 2)
+    outer = bit_of(spots["wide"], 1) == bit_of(spots["wide"], 2)
+
+    bits = {
+        (axis, place): bit_of(spots[axis], place)
+        for axis, count in (("narrow", plan.narrow_bits), ("wide", plan.wide_bits))
+        for place in range(count)
+    }
+    partners = {}
+    for flips in plan.links:
+        there = dict(spots)
+        for axis, place in flips:
+            there[axis] = there[axis] + (1 - 2 * bits[axis, place]) * 2**place
+        partners[flips] = there
 
     loads = {}
     for number, name in enumerate(("tok", "jw", "mw", "ew", "sw", "cot")):
@@ -129,9 +209,9 @@
         )
         loads[name].start()
 
-    barrier = pltpu.get_barrier_semaphore() if plan.sums else None
-    for axis, place, _, _ in plan.sums:
-        pl.semaphore_signal(barrier, inc=1, device_id=partner(axis, place), device_id_type=MESH)
+    barrier = pltpu.get_barrier_semaphore()
+    for flips in plan.links:
+        pl.semaphore_signal(barrier, inc=1, device_id=partners[flips], device_id_type=MESH)
 
     def vector(row):
         return r.vec[row : row + 1, :]
@@ -390,69 +470,130 @@
             r.sums[row : row + 1, start : start + TILE] = r.expand_sums[tile]
         input_copy().start()
 
-    def source(stage, item):
+    def when(condition, action):
+        if condition is True:
+            action()
+        else:
+            pl.when(condition)(action)
+
+    def roles(move):
+        if move.kind == "fold":
+            return outer, inner
+        if move.kind == "unfold":
+            return inner, outer
+        return (inner, inner) if move.inner else (True, True)
+
+    def land(number, stage, item):
+        ref = getattr(r, f"land{number}_{stage}")
+        return ref.at[lax.rem(item, plan.parts[number].slots(stage))]
+
+    def source(number, stage, item):
         if stage == 0:
-            return r.part.at[lax.rem(item, 2)]
-        return landed[stage - 1].at[lax.rem(item, DEPTH)]
-
-    def piece_start(bits):
-        start = 0
-        for place in range(bits):
-            start = start + bit_of(spots["wide"], place) * (chunk // 2 ** (place + 1))
-        return start
-
-    def exchange(stage, item):
-        slot = lax.rem(item, DEPTH)
-        if stage < len(plan.sums):
-            axis, place, length, halve = plan.sums[stage]
-            there = (1 - bit_of(spots[axis], place)) * length if halve else 0
-            src = source(stage, item).at[aligned(there, length, SUB)]
-            dst = landed[stage].at[slot]
+            return getattr(r, f"part{number}").at[lax.rem(item, 2)]
+        return land(number, stage - 1, item)
+
+    kept, given, regions = {}, {}, {}
+    for number, part in enumerate(plan.parts):
+        for stage, move in enumerate(part.moves):
+            bit = bits[move.select] if move.select else 0
+            kept[number, stage] = bit * move.length
+            given[number, stage] = (1 - bit) * move.length if move.select else 0
+            regions[number, stage] = sum(
+                bits[select] * size for select, size in part.selects if size >= move.length
+            )
+
+    def in_whole(number, stage, item):
+        part = plan.parts[number]
+        return (
+            item,
+            aligned(regions[number, stage], part.moves[stage].length, SUB),
+            pl.ds(part.column, part.columns),
+        )
+
+    def transfer(number, stage, item):
+        part = plan.parts[number]
+        move = part.moves[stage]
+        slot = lax.rem(item, part.slots(stage))
+        if stage < len(part.sums):
+            src = source(number, stage, item).at[
+                aligned(given[number, stage], move.length, SUB)
+            ]
+            dst = land(number, stage, item)
         else:
-            axis, place, length = plan.gathers[stage - len(plan.sums)]
-            src = r.whole.at[item, aligned(piece_start(place + 1), length, SUB)]
+            src = r.whole.at[in_whole(number, stage, item)]
             dst = src
         return pltpu.make_async_remote_copy(
             src_ref=src,
             dst_ref=dst,
-            send_sem=r.send_sems.at[stage, slot],
-            recv_sem=r.recv_sems.at[stage, slot],
-            device_id=partner(axis, place),
+            send_sem=r.send_sems.at[number, stage, slot],
+            recv_sem=r.recv_sems.at[number, stage, slot],
+            device_id=partners[move.flips],
             device_id_type=MESH,
         )
+
+    def begin(number, stage, item):
+        sender, _ = roles(plan.parts[number].moves[stage])
+        when(sender, lambda: transfer(number, stage, item).start())
+
+    def settle(number, stage, item):
+        part = plan.parts[number]
+        move = part.moves[stage]
+        sender, receiver = roles(move)
+
+        def receive():
+            if stage < len(part.sums):
+                land(number, stage, item)[...] += source(number, stage, item)[
+                    aligned(kept[number, stage], move.length, SUB)
+                ]
+            if stage == len(part.sums) - 1:
+                r.whole[in_whole(number, stage, item)] = land(number, stage, item)[...]
+
+        if move.kind in ("fold", "unfold"):
+            when(sender, lambda: transfer(number, stage, item).wait_send())
+
+            def arrive():
+                transfer(number, stage, item).wait_recv()
+                receive()
+
+        else:
+
+            def arrive():
+                transfer(number, stage, item).wait()
+                receive()
+
+        when(receiver, arrive)
+        if stage + 1 < len(part.moves):
+            begin(number, stage + 1, item)
 
     def produce(item):
         slot = lax.rem(item, 2)
         lefts = (r.active_t, r.second_t, r.mixed_t, r.first_t)
         rights = (r.grad_out, r.wide_rows, r.grad_branch, r.sw)
-        for number, (start, count, rows_block, windows) in enumerate(plan.phases):
-            left, right = lefts[number], rights[number]
+        for phase, (start, count, rows_block, windows) in enumerate(plan.phases):
+            left, right = lefts[phase], rights[phase]
 
             @pl.when((item >= start) & (item < start + count))
             def _():
                 local = item - start
                 row = lax.div(local, windows) * chunk
                 window = lax.rem(local, windows)
-                picked = [
-                    left[
-                        aligned(
-                            reversed_bits(spot, plan.narrow_bits) * rows_block + row, chunk, chunk
-                        ),
-                        :,
+                for number, part in enumerate(plan.parts):
+                    picked = [
+                        left[aligned(block * rows_block + row + offset, size, size), :]
+                        for block, offset, size in part.picks
                     ]
-                    for spot in range(narrow)
-                ]
-                if number == 3:
-                    other = right[aligned(window * padded, padded, 256), :]
-                else:
-                    other = right[:, aligned(window * width, width, 128)]
-                r.part[slot] = matmul(jnp.concatenate(picked, axis=0), other)
-
-    def absorb(stage, item):
-        axis, place, length, halve = plan.sums[stage]
-        here = bit_of(spots[axis], place) * length if halve else 0
-        slot = lax.rem(item, DEPTH)
-        landed[stage][slot] += source(stage, item)[aligned(here, length, SUB)]
+                    if phase == 3:
+                        other = right[
+                            aligned(window * padded, padded, 256),
+                            part.column : part.column + part.columns,
+                        ]
+                    else:
+                        other = right[
+                            :, aligned(window * width + part.column, part.columns, 128)
+                        ]
+                    getattr(r, f"part{number}")[slot] = matmul(
+                        jnp.concatenate(picked, axis=0), other
+                    )
 
     def result_copy(item, act):
         outs = (r.out_shrink, r.out_expand, r.out_mixer, r.out_joint)
@@ -474,21 +615,20 @@
                     copy.wait()
 
     def vector_exchange(stage):
-        axis, place, _, _ = plan.sums[stage]
         return pltpu.make_async_remote_copy(
             src_ref=r.sums if stage == 0 else r.vector_land.at[stage - 1],
             dst_ref=r.vector_land.at[stage],
             send_sem=r.vector_sems.at[0, stage],
             recv_sem=r.vector_sems.at[1, stage],
-            device_id=partner(axis, place),
+            device_id=partners[plan.links[stage]],
             device_id_type=MESH,
         )
 
     def vector_step(tick):
-        count = len(plan.sums)
+        count = len(plan.links)
         for stage in range(count + 1):
 
-            @pl.when(tick == plan.vector_tick + stage)
+            @pl.when(tick == plan.vector_tick + stage * plan.vector_every)
             def _():
                 if stage > 0:
                     vector_exchange(stage - 1).wait()
@@ -497,35 +637,29 @@
                 if stage < count:
                     vector_exchange(stage).start()
 
-    if plan.sums:
-        pl.semaphore_wait(barrier, len(plan.sums))
+    pl.semaphore_wait(barrier, len(plan.links))
 
     def step(tick, carry):
         @pl.when(tick < plan.chunks)
         def _():
             produce(tick)
-            if plan.depth:
-                exchange(0, tick).start()
-            else:
-                r.whole[tick] = r.part[lax.rem(tick, 2)]
-                result_copy(tick, "start")
-
-        for stage in range(plan.depth):
-            item = tick - 1 - stage
-
-            @pl.when((item >= 0) & (item < plan.chunks))
-            def _():
-                exchange(stage, item).wait()
-                if stage < len(plan.sums):
-                    absorb(stage, item)
-                if stage == len(plan.sums) - 1:
-                    r.whole[item, aligned(piece_start(plan.split_bits), plan.last, SUB)] = landed[
-                        stage
-                    ][lax.rem(item, DEPTH)]
-                if stage + 1 < plan.depth:
-                    exchange(stage + 1, item).start()
-                else:
-                    result_copy(item, "start")
+            for number in range(len(plan.parts)):
+                begin(number, 0, tick)
+
+        for stage in range(plan.stages):
+            for number, part in enumerate(plan.parts):
+                if stage < len(part.moves):
+                    item = tick - part.due[stage]
+
+                    @pl.when((item >= 0) & (item < plan.chunks))
+                    def _():
+                        settle(number, stage, item)
+
+        ready = tick - plan.depth
+
+        @pl.when((ready >= 0) & (ready < plan.chunks))
+        def _():
+            result_copy(ready, "start")
 
         done = tick - 1 - plan.depth
 
@@ -534,19 +668,24 @@
             result_copy(done, "wait")
 
         vector_step(tick)
-        pl.when(tick < plan.ff_jobs)(lambda: ff_job(tick))
-        pl.when(tick == plan.norm_job)(norm_job)
-        pl.when(tick == plan.mix_job)(mix_job)
-        pl.when((tick >= plan.item_job) & (tick < plan.pack_job))(
-            lambda: item_job(tick - plan.item_job)
-        )
-        pl.when(tick == plan.pack_job)(pack_job)
-        pl.when(tick == plan.first_job)(first_job)
-        pl.when(tick == plan.input_job)(input_job)
+        job = lax.div(tick, plan.stride)
+
+        @pl.when(lax.rem(tick, plan.stride) == 0)
+        def _():
+            pl.when(job < plan.ff_jobs)(lambda: ff_job(job))
+            pl.when(job == plan.norm_job)(norm_job)
+            pl.when(job == plan.mix_job)(mix_job)
+            pl.when((job >= plan.item_job) & (job < plan.pack_job))(
+                lambda: item_job(job - plan.item_job)
+            )
+            pl.when(job == plan.pack_job)(pack_job)
+            pl.when(job == plan.first_job)(first_job)
+            pl.when(job == plan.input_job)(input_job)
+
         return carry
 
     lax.fori_loop(0, plan.ticks, step, 0)
-    r.vector_out[...] = r.vector_land[len(plan.sums) - 1] if plan.sums else r.sums[...]
+    r.vector_out[...] = r.vector_land[len(plan.links) - 1]
     layer_copy().wait()
     input_copy().wait()
 
@@ -572,7 +711,7 @@
     items, slots, width = tokens.shape
     ff = expand_weight.shape[1]
     narrow, wide = lax.axis_size("narrow"), lax.axis_size("wide")
-    plan = Plan(narrow, wide, items, slots, width, ff, SUB if wide > 1 else TILE)
+    plan = Plan(narrow, wide, items, slots, width, ff)
     padded, chunk = plan.padded, plan.chunk
     vectors = jnp.stack(
         [
@@ -634,19 +773,20 @@
         "grad_branch": pltpu.VMEM((padded, width), BF16),
         "sums": pltpu.VMEM((plan.vector_rows, width), F32),
         "expand_sums": pltpu.VMEM((plan.ff_jobs, 1, TILE), F32),
-        "part": pltpu.VMEM((2, narrow * chunk, width), F32),
         "whole": pltpu.VMEM((plan.chunks, chunk, width), F32),
+        "vector_land": pltpu.VMEM((len(plan.links), plan.vector_rows, width), F32),
         "load_sems": pltpu.SemaphoreType.DMA((6,)),
         "out_sems": pltpu.SemaphoreType.DMA((2,)),
+        "vector_sems": pltpu.SemaphoreType.DMA((2, len(plan.links))),
+        "send_sems": pltpu.SemaphoreType.DMA((len(plan.parts), plan.stages, plan.slots_most)),
+        "recv_sems": pltpu.SemaphoreType.DMA((len(plan.parts), plan.stages, plan.slots_most)),
     }
-    if plan.sums:
-        for stage, (_, _, length, _) in enumerate(plan.sums):
-            scratch[f"land{stage}"] = pltpu.VMEM((DEPTH, length, width), F32)
-        scratch["vector_land"] = pltpu.VMEM((len(plan.sums), plan.vector_rows, width), F32)
-        scratch["vector_sems"] = pltpu.SemaphoreType.DMA((2, len(plan.sums)))
-        scratch["send_sems"] = pltpu.SemaphoreType.DMA((plan.depth, DEPTH))
-        scratch["recv_sems"] = pltpu.SemaphoreType.DMA((plan.depth, DEPTH))
-    remote = {"collective_id": 0} if plan.sums else {}
+    for number, part in enumerate(plan.parts):
+        scratch[f"part{number}"] = pltpu.VMEM((2, narrow * chunk, part.columns), F32)
+        for stage, move in enumerate(part.sums):
+            scratch[f"land{number}_{stage}"] = pltpu.VMEM(
+                (part.slots(stage), move.length, part.columns), F32
+            )
     results = pl.pallas_call(
         functools.partial(layer_kernel, plan, (*inputs, *outputs, *scratch)),
         out_shape=[jax.ShapeDtypeStruct(shape, kind) for shape, kind, _ in outputs.values()],
@@ -654,7 +794,7 @@
         out_specs=[spec for _, _, spec in outputs.values()],
         scratch_shapes=list(scratch.values()),
         compiler_params=pltpu.CompilerParams(
-            has_side_effects=True, vmem_limit_bytes=61 * 2**20, **remote
+            has_side_effects=True, vmem_limit_bytes=61 * 2**20, collective_id=0
         ),
         name="layer",
     )(*(value for value, _ in inputs.values()))

time: 240 us -> 218 us (0.908)
  Pallas kernels: 218 us -> 196 us
    pallas_call x1, Pallas kernels: 218 us -> 196 us  [shards(): pl.pallas_call(functools.partial(layer_kernel, plan, (*inputs, *outputs,...]
where the time goes in v3:
time: 218 us
  Pallas kernels  196 us (90%)
  local copies, waits for them, and re-layouts  19.9 us (9%)
    pallas_call x1, Pallas kernels, shards(): pl.pallas_call(functools.partial(layer_kernel, plan, (*inputs, *outputs,...  196 us
    unnamed x14, local copies, waits for them, and re-layouts  10.6 us
    another operation x9, local copies, waits for them, and re-layouts, shards(): jnp.stack([first_gain, first_shift, query_bias, value_bias, mixer_bias, s...  5.56 us

profile of v3, /device:TPU:0, one launch (start us, length us, event | category | flops | bytes accessed | tf_op | source)
XLA Modules:
  0.0 217.7 jit_solution(13936353055877795705)
XLA Ops:
  0.6 0.7 stack.27
  1.3 0.7 stack.28
  2.0 0.7 stack.29
  2.7 0.7 stack.30
  3.4 0.7 stack.31
  4.1 0.7 stack.32
  4.8 0.7 stack.33
  5.4 0.7 stack.34
  6.1 0.8 fusion.1
  6.9 0.1 stack.35
  7.0 0.6 convert_element_type.3.refs_1_
  7.7 196.4 %layer.1 = (bf16[7,72,768]{2,1,0:T(8,128)(2,1)}, bf16[7,72,768]{2,1,0:T(8,128)(2,1)}, f32[768,768]{1,0:T(8,128)}, f32[192,3072]{1,0:T(8,128)}, f32[192,768]{1,0:...) custom-call(s32[7]{0:T(128)} %refs_0_.1, f32[12,768]{1,0:T(8,128)} %convert_element_type.3.refs_1_, ...), custom_call_target="tpu_custom_call" | custom-call | tf_op jit(solution)/shard_map/layer/pallas_call | solution.py:790
  204.1 0.0 copy-start.2
  204.1 0.9 slice.42
  205.0 0.7 slice.34
  205.7 0.7 fusion
  206.4 0.7 dynamic_slice.7
  207.1 2.1 copy.37
  209.1 0.0 copy-start.3
  209.1 2.1 copy.38
  211.2 0.0 copy-done.2
  211.3 0.0 copy-start.1
  211.3 1.2 copy.39
  212.5 0.0 copy-done.3
  212.5 0.8 copy.40
  213.3 0.5 copy-done.1
  213.8 0.0 copy-start
  213.8 1.4 copy.41
  215.2 1.1 copy-done
  216.3 1.4 copy.42
  (5 shorter events, 0.0 us)
Async XLA Ops:
  204.1 7.1 %copy-start.2 = (f32[192,2304]{1,0:T(8,128)S(1)}, f32[192,2304]{1,0:T(8,128)}, u32[]{:S(2)}) copy-start(f32[192,2304]{1,0:T(8,128)} %get-tuple-element.60) | copy-start | bytes 5308420
  209.1 3.3 %copy-start.3 = (f32[192,768]{1,0:T(8,128)S(1)}, f32[192,768]{1,0:T(8,128)}, u32[]{:S(2)}) copy-start(f32[192,768]{1,0:T(8,128)} %get-tuple-element.63) | copy-start | bytes 1769476
  211.3 2.5 %copy-start.1 = (f32[192,3072]{1,0:T(8,128)S(1)}, f32[192,3072]{1,0:T(8,128)}, u32[]{:S(2)}) copy-start(f32[192,3072]{1,0:T(8,128)} %get-tuple-element.67) | copy-start | bytes 7077892
  213.8 2.5 %copy-start = (f32[768,768]{1,0:T(8,128)S(1)}, f32[768,768]{1,0:T(8,128)}, u32[]{:S(2)}) copy-start(f32[768,768]{1,0:T(8,128)} %get-tuple-element.69) | copy-start | bytes 7077892

commit v4 on v3

--- a/solution.py
+++ b/solution.py
@@ -171,7 +171,7 @@
         assert self.phases[3][0] > self.first_job * self.stride
         self.vector_rows = 8 + ff // width
         self.vector_rows += -self.vector_rows % SUB
-        self.ticks = self.chunks + self.depth + 1
+        self.ticks = self.chunks + self.depth
         self.vector_every = (self.ticks - 1 - self.vector_tick) // len(self.links)
         assert self.vector_every > 0
 
@@ -256,6 +256,12 @@
         start = part * width + pair * 2 * HEAD_DIM
         return slice(start, start + 2 * HEAD_DIM)
 
+    small = (r.g1, r.s1, r.qb, r.vb, r.mb, r.g2, r.s2, r.sb)
+    for row, ref in enumerate(small):
+        r.vec[row : row + 1, :] = ref[...].astype(F32).reshape(1, width)
+    for row in range(plan.ff // width):
+        value = r.eb[row * width : (row + 1) * width].astype(F32)
+        r.vec[8 + row : 9 + row, :] = value.reshape(1, width)
     r.stage[rows:, :] = jnp.zeros((padded - rows, width), F32)
     r.sums[...] = jnp.zeros_like(r.sums)
     loads["tok"].wait()
@@ -391,15 +397,8 @@
             [r.acc_out[rows_full:rows, :], jnp.zeros((padded - rows, width), F32)], axis=0
         )
         r.grad_branch[rows_full:, :] = tail.astype(BF16)
-        layer_copy().start()
 
     rows_full = rows // 16 * 16
-
-    def layer_copy():
-        return pltpu.make_async_copy(r.cot, r.layer_out, r.load_sems.at[0])
-
-    def input_copy():
-        return pltpu.make_async_copy(r.tok, r.input_grad, r.load_sems.at[1])
 
     def mix_job():
         def one(tile):
@@ -468,7 +467,6 @@
         for tile in range(plan.ff_jobs):
             row, start = 8 + tile // per_row, tile % per_row * TILE
             r.sums[row : row + 1, start : start + TILE] = r.expand_sums[tile]
-        input_copy().start()
 
     def when(condition, action):
         if condition is True:
@@ -565,6 +563,10 @@
         if stage + 1 < len(part.moves):
             begin(number, stage + 1, item)
 
+    def rows_of(phase):
+        _, count, _, windows = plan.phases[phase]
+        return count // windows
+
     def produce(item):
         slot = lax.rem(item, 2)
         lefts = (r.active_t, r.second_t, r.mixed_t, r.first_t)
@@ -575,8 +577,9 @@
             @pl.when((item >= start) & (item < start + count))
             def _():
                 local = item - start
-                row = lax.div(local, windows) * chunk
-                window = lax.rem(local, windows)
+                tall = rows_of(phase)
+                row = lax.rem(local, tall) * chunk
+                window = lax.div(local, tall)
                 for number, part in enumerate(plan.parts):
                     picked = [
                         left[aligned(block * rows_block + row + offset, size, size), :]
@@ -595,25 +598,6 @@
                         jnp.concatenate(picked, axis=0), other
                     )
 
-    def result_copy(item, act):
-        outs = (r.out_shrink, r.out_expand, r.out_mixer, r.out_joint)
-        for (start, count, _, windows), out in zip(plan.phases, outs):
-
-            @pl.when((item >= start) & (item < start + count))
-            def _():
-                local = item - start
-                row = lax.div(local, windows) * chunk
-                col = lax.rem(local, windows) * width
-                copy = pltpu.make_async_copy(
-                    r.whole.at[item],
-                    out.at[aligned(row, chunk, chunk), aligned(col, width, 128)],
-                    r.out_sems.at[lax.rem(item, 2)],
-                )
-                if act == "start":
-                    copy.start()
-                else:
-                    copy.wait()
-
     def vector_exchange(stage):
         return pltpu.make_async_remote_copy(
             src_ref=r.sums if stage == 0 else r.vector_land.at[stage - 1],
@@ -654,18 +638,6 @@
                     @pl.when((item >= 0) & (item < plan.chunks))
                     def _():
                         settle(number, stage, item)
-
-        ready = tick - plan.depth
-
-        @pl.when((ready >= 0) & (ready < plan.chunks))
-        def _():
-            result_copy(ready, "start")
-
-        done = tick - 1 - plan.depth
-
-        @pl.when(done >= 0)
-        def _():
-            result_copy(done, "wait")
 
         vector_step(tick)
         job = lax.div(tick, plan.stride)
@@ -686,8 +658,37 @@
 
     lax.fori_loop(0, plan.ticks, step, 0)
     r.vector_out[...] = r.vector_land[len(plan.links) - 1]
-    layer_copy().wait()
-    input_copy().wait()
+
+
+def write_kernel(plan, tok, cot, whole, sums, *refs):
+    outs, sems = refs[:-1], refs[-1]
+    copies = [(tok, outs[0]), (cot, outs[1])]
+    for (start, count, _, windows), out in zip(plan.phases, outs[2:6]):
+        tall = count // windows
+        for window in range(windows):
+            first = start + window * tall
+            cols = pl.ds(window * plan.width, plan.width)
+            copies.append((whole.at[first : first + tall], out.at[:, :, cols]))
+    copies = [
+        pltpu.make_async_copy(source, target, sems.at[number])
+        for number, (source, target) in enumerate(copies)
+    ]
+    for copy in copies:
+        copy.start()
+    own = lax.axis_index("narrow")
+    for place in range(plan.narrow):
+
+        @pl.when(own == place)
+        def _():
+            for row, out in enumerate(outs[6:14]):
+                size = out.shape[0]
+                out[...] = sums[row : row + 1, place * size : (place + 1) * size].reshape(size)
+            size = outs[14].shape[0]
+            row, start = 8 + place * size // plan.width, place * size % plan.width
+            outs[14][...] = sums[row : row + 1, start : start + size].reshape(size)
+
+    for copy in copies:
+        copy.wait()
 
 
 def shards(
@@ -713,25 +714,20 @@
     narrow, wide = lax.axis_size("narrow"), lax.axis_size("wide")
     plan = Plan(narrow, wide, items, slots, width, ff)
     padded, chunk = plan.padded, plan.chunk
-    vectors = jnp.stack(
-        [
-            first_gain,
-            first_shift,
-            query_bias,
-            value_bias,
-            mixer_bias,
-            second_gain,
-            second_shift,
-            shrink_bias,
-            *expand_bias.reshape(ff // width, width),
-        ]
-    ).astype(F32)
     hbm = pl.BlockSpec(memory_space=pl.ANY)
     vmem = pl.BlockSpec(memory_space=pltpu.VMEM)
     smem = pl.BlockSpec(memory_space=pltpu.SMEM)
     inputs = {
         "visible": (visible, smem),
-        "vec": (vectors, vmem),
+        "g1": (first_gain, vmem),
+        "s1": (first_shift, vmem),
+        "qb": (query_bias, vmem),
+        "vb": (value_bias, vmem),
+        "mb": (mixer_bias, vmem),
+        "g2": (second_gain, vmem),
+        "s2": (second_shift, vmem),
+        "sb": (shrink_bias, vmem),
+        "eb": (expand_bias, vmem),
         "tok_in": (tokens, hbm),
         "cot_in": (cotangent, hbm),
         "jw_in": (joint_weight, hbm),
@@ -741,17 +737,12 @@
     }
     block = width // narrow
     outputs = {
-        "layer_out": (tokens.shape, BF16, hbm),
-        "input_grad": (tokens.shape, BF16, hbm),
-        "out_shrink": ((ff // narrow, width), F32, hbm),
-        "out_expand": ((block, ff), F32, hbm),
-        "out_mixer": ((block, width), F32, hbm),
-        "out_joint": ((block, 3 * width), F32, hbm),
-        "vector_out": ((plan.vector_rows, width), F32, vmem),
+        "tok": (tokens.shape, BF16),
+        "cot": (tokens.shape, BF16),
+        "whole": ((plan.chunks, chunk, width), F32),
+        "vector_out": ((plan.vector_rows, width), F32),
     }
     scratch = {
-        "tok": pltpu.VMEM(tokens.shape, BF16),
-        "cot": pltpu.VMEM(tokens.shape, BF16),
         "jw": pltpu.VMEM(joint_weight.shape, BF16),
         "mw": pltpu.VMEM(mixer_weight.shape, BF16),
         "ew": pltpu.VMEM(expand_weight.shape, BF16),
@@ -771,12 +762,11 @@
         "acc_out": pltpu.VMEM((padded, width), F32),
         "acc_grad": pltpu.VMEM((padded, width), F32),
         "grad_branch": pltpu.VMEM((padded, width), BF16),
+        "vec": pltpu.VMEM((plan.vector_rows, width), F32),
         "sums": pltpu.VMEM((plan.vector_rows, width), F32),
         "expand_sums": pltpu.VMEM((plan.ff_jobs, 1, TILE), F32),
-        "whole": pltpu.VMEM((plan.chunks, chunk, width), F32),
         "vector_land": pltpu.VMEM((len(plan.links), plan.vector_rows, width), F32),
         "load_sems": pltpu.SemaphoreType.DMA((6,)),
-        "out_sems": pltpu.SemaphoreType.DMA((2,)),
         "vector_sems": pltpu.SemaphoreType.DMA((2, len(plan.links))),
         "send_sems": pltpu.SemaphoreType.DMA((len(plan.parts), plan.stages, plan.slots_most)),
         "recv_sems": pltpu.SemaphoreType.DMA((len(plan.parts), plan.stages, plan.slots_most)),
@@ -789,36 +779,54 @@
             )
     results = pl.pallas_call(
         functools.partial(layer_kernel, plan, (*inputs, *outputs, *scratch)),
-        out_shape=[jax.ShapeDtypeStruct(shape, kind) for shape, kind, _ in outputs.values()],
+        out_shape=[pltpu.VMEM(shape, kind) for shape, kind in outputs.values()],
         in_specs=[spec for _, spec in inputs.values()],
-        out_specs=[spec for _, _, spec in outputs.values()],
+        out_specs=[vmem] * len(outputs),
         scratch_shapes=list(scratch.values()),
         compiler_params=pltpu.CompilerParams(
-            has_side_effects=True, vmem_limit_bytes=61 * 2**20, collective_id=0
+            has_side_effects=True, vmem_limit_bytes=51 * 2**20, collective_id=0
         ),
         name="layer",
     )(*(value for value, _ in inputs.values()))
-    layer_out, input_grad, shrink, expand, mixer, joint, sums = results
-    own = lax.axis_index("narrow")
-    mine = lax.dynamic_slice_in_dim(sums[:8], own * block, block, axis=1)
-    wide_sums = sums[8 : 8 + ff // width].reshape(ff)
-    expand_sum = lax.dynamic_slice_in_dim(wide_sums, own * (ff // narrow), ff // narrow)
+    row_counts = [count // windows for _, count, _, windows in plan.phases]
+    shapes = [jax.ShapeDtypeStruct(tokens.shape, BF16)] * 2
+    shapes += [
+        jax.ShapeDtypeStruct((tall, chunk, windows * width), F32)
+        for tall, (_, _, _, windows) in zip(row_counts, plan.phases)
+    ]
+    shapes += [jax.ShapeDtypeStruct((block,), F32)] * 8
+    shapes += [jax.ShapeDtypeStruct((ff // narrow,), F32)]
+    copies = 2 + sum(windows for _, _, _, windows in plan.phases)
+    outs = pl.pallas_call(
+        functools.partial(write_kernel, plan),
+        out_shape=shapes,
+        in_specs=[vmem] * len(results),
+        out_specs=[hbm] * 6 + [vmem] * 9,
+        scratch_shapes=[pltpu.SemaphoreType.DMA((copies,))],
+        compiler_params=pltpu.CompilerParams(vmem_limit_bytes=4 * 2**20),
+        name="write",
+    )(*(pltpu.with_memory_space_constraint(value, pltpu.VMEM) for value in results))
+    input_grad, layer_out = outs[:2]
+    shrink, expand, mixer, joint = (
+        out.reshape(-1, out.shape[-1]) for out in outs[2:6]
+    )
+    vectors = outs[6:]
     return (
         layer_out,
         input_grad,
-        mine[0],
-        mine[1],
+        vectors[0],
+        vectors[1],
         joint,
-        mine[2],
-        mine[3],
+        vectors[2],
+        vectors[3],
         mixer,
-        mine[4],
-        mine[5],
-        mine[6],
+        vectors[4],
+        vectors[5],
+        vectors[6],
         expand,
-        expand_sum,
+        vectors[8],
         shrink,
-        mine[7],
+        vectors[7],
     )
 
 

time: 218 us -> 200 us (0.917)
  local copies, waits for them, and re-layouts: 19.9 us -> 0 us
  Pallas kernels: 196 us -> 199 us
    unnamed x14 -> x0, local copies, waits for them, and re-layouts: 10.6 us -> none
    another operation x14 -> x0, local copies, waits for them, and re-layouts: 6.35 us -> none  [the longest x9 5.56 us: shards(): jnp.stack([first_gain, first_shift, query_bias, value_bias, mixer_bias, s...]
    pallas_call x0 -> x1, Pallas kernels: none -> 4.08 us  [shards(): pl.pallas_call(functools.partial(write_kernel, plan), out_shape=shapes, i...]
    slice x3 -> x0, local copies, waits for them, and re-layouts: 2.28 us -> none  [the longest x1 0.87 us: shards(): wide_sums = sums[8:8 + ff // width].reshape(ff)]
where the time goes in v4:
time: 200 us
  Pallas kernels  199 us (100%)
    pallas_call x1, Pallas kernels, shards(): pl.pallas_call(functools.partial(layer_kernel, plan, (*inputs, *outputs,...  195 us
    pallas_call x1, Pallas kernels, shards(): pl.pallas_call(functools.partial(write_kernel, plan), out_shape=shapes, i...  4.08 us

profile of v4, /device:TPU:0, one launch (start us, length us, event | category | flops | bytes accessed | tf_op | source)
XLA Modules:
  0.0 199.8 jit_solution(3499326694108152033)
XLA Ops:
  0.7 195.0 %layer.1 = (bf16[7,72,768]{2,1,0:T(8,128)(2,1)S(1)}, bf16[7,72,768]{2,1,0:T(8,128)(2,1)S(1)}, f32[72,32,768]{2,1,0:T(8,128)S(1)}, f32[16,768]{1,0:T(8,128)S(1)}) custom-call(s32[7]{0:T(128)} %refs_0_.1, bf16[768]{0:T(1024)(128)(2,1)} %refs_1_.1, bf16[768]{0:T(1024)(128)(2,1)} %refs_2_.1, bf16[768]{0:T(1024)(128)(2,1)} %refs_3_.1, bf16[768]{0:T(1024)(128)(2,1)} %refs_4_.1, ...), custom_call_target="tpu_custom_call" | custom-call | tf_op jit(solution)/shard_map/layer/pallas_call | solution.py:780
  195.7 4.1 %write.1 = (bf16[7,72,768]{2,1,0:T(8,128)(2,1)}, bf16[7,72,768]{2,1,0:T(8,128)(2,1)}, f32[24,32,768]{2,1,0:T(8,128)}, f32[6,32,3072]{2,1,0:T(8,128)}, f32[6,32,7...) custom-call(bf16[7,72,768]{2,1,0:T(8,128)(2,1)S(1)} %get-tuple-eleme, ...), custom_call_target="tpu_custom_call" | custom-call | tf_op jit(solution)/shard_map/write/pallas_call | solution.py:800

commit v5 on v4

--- a/solution.py
+++ b/solution.py
@@ -157,28 +157,33 @@
             self.phases.append((start, count, rows_block, windows))
             start += count
         self.chunks = start
-        self.ff_jobs = ff // TILE
-        self.norm_job = self.ff_jobs
-        self.mix_job = self.norm_job + 1
-        self.item_job = self.mix_job + 1
-        self.pack_job = self.item_job + items
-        self.first_job = self.pack_job + 1
-        self.input_job = self.first_job + 1
-        self.stride = self.phases[1][0] // self.ff_jobs
-        self.vector_tick = (self.input_job + 1) * self.stride
-        assert self.stride >= 1
-        assert self.phases[2][0] > self.mix_job * self.stride
-        assert self.phases[3][0] > self.first_job * self.stride
+        self.ff_tiles = ff // TILE
+        self.split = self.phases[1][0] // self.ff_tiles
+        assert self.split >= 1
+        tall = ff // narrow
+        self.groups = tall // TILE if tall % TILE == 0 else 1
+        self.blocks = self.ff_tiles // self.groups
+        self.jobs = {}
+        tick = 0
+        for name, count in (
+            ("ff", self.ff_tiles * self.split),
+            ("norm", self.split),
+            ("mix", 1),
+            ("item", items * self.split),
+            ("pack", 1),
+            ("first", self.split),
+            ("input", self.split),
+        ):
+            self.jobs[name] = (tick, count)
+            tick += count
+        self.vector_tick = tick
+        assert self.phases[2][0] >= self.jobs["item"][0]
+        assert self.phases[3][0] >= self.jobs["first"][0]
         self.vector_rows = 8 + ff // width
         self.vector_rows += -self.vector_rows % SUB
         self.ticks = self.chunks + self.depth
         self.vector_every = (self.ticks - 1 - self.vector_tick) // len(self.links)
         assert self.vector_every > 0
-
-
-def gelu_parts(hidden):
-    normal = 0.5 + 0.5 * lax.erf(hidden * ROOT_HALF)
-    return normal
 
 
 def layer_kernel(plan, names, *refs):
@@ -203,11 +208,12 @@
         partners[flips] = there
 
     loads = {}
-    for number, name in enumerate(("tok", "jw", "mw", "ew", "sw", "cot")):
+    for number, name in enumerate(("tok", "jw", "mw", "ew", "cot", "sw")):
         loads[name] = pltpu.make_async_copy(
             getattr(r, name + "_in"), getattr(r, name), r.load_sems.at[number]
         )
-        loads[name].start()
+    loads["tok"].start()
+    loads["jw"].start()
 
     barrier = pltpu.get_barrier_semaphore()
     for flips in plan.links:
@@ -264,6 +270,7 @@
         r.vec[8 + row : 9 + row, :] = value.reshape(1, width)
     r.stage[rows:, :] = jnp.zeros((padded - rows, width), F32)
     r.sums[...] = jnp.zeros_like(r.sums)
+    r.expand_sums[...] = jnp.zeros_like(r.expand_sums)
     loads["tok"].wait()
 
     def first_norm(item):
@@ -271,6 +278,8 @@
         r.stage[item_rows(item), :] = unit * vector(0) + vector(1)
 
     each_item(first_norm)
+    for name in ("mw", "ew", "cot", "sw"):
+        loads[name].start()
     r.rowb[...] = r.stage[...].astype(BF16)
     loads["jw"].wait()
     for part, bias in enumerate((2, None, 3)):
@@ -332,14 +341,24 @@
             aligned(lax.rem(tile, per_row) * TILE, TILE, TILE),
         ]
 
-    def expand_tile(tile):
+    every_row = slice(0, padded)
+
+    def hidden_tile(tile, some):
         cols = aligned(tile * TILE, TILE, TILE)
-        hidden = matmul(r.second[...], r.ew[:, cols]) + expand_bias(tile)
-        active = hidden * gelu_parts(hidden)
-        r.wide_rows[:, cols] = active.astype(BF16)
-        r.active_t[cols, :] = active.T.astype(BF16)
-
-    each_tile(plan.ff_jobs, expand_tile)
+        hidden = matmul(r.second[some, :], r.ew[:, cols]) + expand_bias(tile)
+        return hidden, 0.5 + 0.5 * lax.erf(hidden * ROOT_HALF)
+
+    def activate(tile, some, hidden, normal):
+        cols = aligned(tile * TILE, TILE, TILE)
+        active = hidden * normal
+        r.wide_rows[some, cols] = active.astype(BF16)
+        r.active_t[cols, some] = active.T.astype(BF16)
+
+    def expand_tile(place):
+        tile = place * plan.groups
+        activate(tile, every_row, *hidden_tile(tile, every_row))
+
+    each_tile(plan.blocks, expand_tile)
     r.second_t[...] = r.stage[...].T.astype(BF16)
     loads["cot"].wait()
 
@@ -351,28 +370,46 @@
     r.grad_out[...] = r.stage[...].astype(BF16)
     loads["sw"].wait()
 
-    def ff_job(tile):
+    rows_full = rows // 16 * 16
+
+    def share(count, turn, body):
+        size = -(-count // plan.split)
+        first = turn * size
+        last = jnp.minimum(first + size, count)
+        lax.fori_loop(first, last, lambda place, carry: (body(place), carry)[1], 0)
+
+    def ff_job(turn):
+        step_number, half = lax.div(turn, plan.split), lax.rem(turn, plan.split)
+        group = lax.rem(lax.div(step_number, plan.blocks) + 1, plan.groups)
+        tile = lax.rem(step_number, plan.blocks) * plan.groups + group
+        size = padded // plan.split
+        some = aligned(half * size, size, size)
         cols = aligned(tile * TILE, TILE, TILE)
-        output = matmul(r.wide_rows[:, cols], r.sw[cols, :])
-        hidden = matmul(r.second[...], r.ew[:, cols]) + expand_bias(tile)
-        grad = matmul(r.grad_out[...], r.sw[cols, :], ((1,), (1,)))
-        slope = gelu_parts(hidden) + hidden * (PEAK * jnp.exp(-0.5 * hidden * hidden))
+        hidden, normal = hidden_tile(tile, some)
+
+        @pl.when(step_number < plan.ff_tiles - plan.blocks)
+        def _():
+            activate(tile, some, hidden, normal)
+
+        grad = matmul(r.grad_out[some, :], r.sw[cols, :], ((1,), (1,)))
+        slope = normal + hidden * (PEAK * jnp.exp(-0.5 * hidden * hidden))
         grad_hidden = (grad * slope).astype(BF16)
-        r.wide_rows[:, cols] = grad_hidden
-        r.expand_sums[tile] = jnp.sum(grad_hidden.astype(F32), axis=0, keepdims=True)
+        output = matmul(r.wide_rows[some, cols], r.sw[cols, :])
+        r.wide_rows[some, cols] = grad_hidden
+        r.expand_sums[tile] += jnp.sum(grad_hidden.astype(F32), axis=0, keepdims=True)
         grad_second = matmul(grad_hidden, r.ew[:, cols], ((1,), (1,)))
 
-        @pl.when(tile == 0)
+        @pl.when(step_number == 0)
         def _():
-            r.acc_out[...] = output
-            r.acc_grad[...] = grad_second
-
-        @pl.when(tile > 0)
+            r.acc_out[some, :] = output
+            r.acc_grad[some, :] = grad_second
+
+        @pl.when(step_number > 0)
         def _():
-            r.acc_out[...] += output
-            r.acc_grad[...] += grad_second
-
-    def norm_job():
+            r.acc_out[some, :] += output
+            r.acc_grad[some, :] += grad_second
+
+    def norm_job(turn):
         def one(item):
             here = item_rows(item)
             live = row_live(item)
@@ -391,16 +428,15 @@
                 grad_middle.astype(BF16).astype(F32), axis=0, keepdims=True
             )
 
-        each_item(one)
+        share(plan.items, turn, one)
+
+    def mix_job(turn):
         r.grad_branch[:rows_full, :] = r.acc_out[:rows_full, :].astype(BF16)
         tail = jnp.concatenate(
             [r.acc_out[rows_full:rows, :], jnp.zeros((padded - rows, width), F32)], axis=0
         )
         r.grad_branch[rows_full:, :] = tail.astype(BF16)
 
-    rows_full = rows // 16 * 16
-
-    def mix_job():
         def one(tile):
             cols = aligned(tile * TILE, TILE, TILE)
             value = matmul(r.grad_branch[...], r.mw[cols, :], ((1,), (1,)))
@@ -408,28 +444,35 @@
 
         each_tile(width // TILE, one)
 
-    def item_job(item):
+    def item_job(turn):
+        item, half = lax.div(turn, plan.split), lax.rem(turn, plan.split)
         here = item_rows(item)
-        for pair in range(pairs):
-            query = both_heads(r.qkv[here, pair_lanes(0, pair)])
-            keys = r.qkv[here, pair_lanes(1, pair)].astype(BF16)
-            values = r.qkv[here, pair_lanes(2, pair)].astype(BF16)
-            grad_mixed = both_heads(r.stage[here, pair_lanes(0, pair)])
-            attend = r.attend[item * pairs + pair]
+        size = pairs // plan.split
+
+        def lanes_of(part, pair):
+            start = part * width + (half * size + pair) * 2 * HEAD_DIM
+            return aligned(start, 2 * HEAD_DIM, 2 * HEAD_DIM)
+
+        for pair in range(size):
+            query = both_heads(r.qkv[here, lanes_of(0, pair)])
+            keys = r.qkv[here, lanes_of(1, pair)].astype(BF16)
+            values = r.qkv[here, lanes_of(2, pair)].astype(BF16)
+            grad_mixed = both_heads(r.stage[here, lanes_of(0, pair)])
+            attend = r.attend[item * pairs + half * size + pair]
             grad_attend = matmul(grad_mixed, values, ((1,), (1,)))
             grad_value = matmul(attend.astype(BF16), grad_mixed, ((0,), (0,)))
-            inner = jnp.sum(attend * grad_attend, axis=-1, keepdims=True)
-            grad_logits = (attend * (grad_attend - inner)).astype(BF16)
+            inner_sum = jnp.sum(attend * grad_attend, axis=-1, keepdims=True)
+            grad_logits = (attend * (grad_attend - inner_sum)).astype(BF16)
             grad_query = one_head_each(matmul(grad_logits, keys)) * score_scale
             grad_key = matmul(grad_logits, query, ((0,), (0,))) * score_scale
-            r.qkv[here, pair_lanes(0, pair)] = grad_query
-            r.qkv[here, pair_lanes(1, pair)] = grad_key
-            r.qkv[here, pair_lanes(2, pair)] = grad_value
+            r.qkv[here, lanes_of(0, pair)] = grad_query
+            r.qkv[here, lanes_of(1, pair)] = grad_key
+            r.qkv[here, lanes_of(2, pair)] = grad_value
 
     def joint_rows(part):
         return slice(part * padded, (part + 1) * padded)
 
-    def pack_job():
+    def pack_job(turn):
         for part in range(3):
             value = r.qkv[:, part * width : (part + 1) * width].astype(BF16)
             r.sw[joint_rows(part), :] = value
@@ -437,7 +480,7 @@
                 row = 2 if part == 0 else 3
                 r.sums[row : row + 1, :] = jnp.sum(value.astype(F32), axis=0, keepdims=True)
 
-    def first_job():
+    def first_job(turn):
         def one(tile):
             cols = aligned(tile * TILE, TILE, TILE)
             total = None
@@ -450,9 +493,9 @@
                 total = value if total is None else total + value
             r.acc_grad[:, cols] = total
 
-        each_tile(width // TILE, one)
-
-    def input_job():
+        share(width // TILE, turn, one)
+
+    def input_job(turn):
         def one(item):
             here = item_rows(item)
             unit, spread = normalized(r.tok[item].astype(F32))
@@ -462,11 +505,14 @@
             total = r.acc_out[here, :] + norm_backward(grad * vector(0), unit, spread)
             r.tok[item] = total.astype(BF16)
 
-        each_item(one)
-        per_row = width // TILE
-        for tile in range(plan.ff_jobs):
-            row, start = 8 + tile // per_row, tile % per_row * TILE
-            r.sums[row : row + 1, start : start + TILE] = r.expand_sums[tile]
+        share(plan.items, turn, one)
+
+        @pl.when(turn == 0)
+        def _():
+            per_row = width // TILE
+            for tile in range(plan.ff_tiles):
+                row, start = 8 + tile // per_row, tile % per_row * TILE
+                r.sums[row : row + 1, start : start + TILE] = r.expand_sums[tile]
 
     def when(condition, action):
         if condition is True:
@@ -640,19 +686,18 @@
                         settle(number, stage, item)
 
         vector_step(tick)
-        job = lax.div(tick, plan.stride)
-
-        @pl.when(lax.rem(tick, plan.stride) == 0)
-        def _():
-            pl.when(job < plan.ff_jobs)(lambda: ff_job(job))
-            pl.when(job == plan.norm_job)(norm_job)
-            pl.when(job == plan.mix_job)(mix_job)
-            pl.when((job >= plan.item_job) & (job < plan.pack_job))(
-                lambda: item_job(job - plan.item_job)
-            )
-            pl.when(job == plan.pack_job)(pack_job)
-            pl.when(job == plan.first_job)(first_job)
-            pl.when(job == plan.input_job)(input_job)
+        run = {
+            "ff": ff_job,
+            "norm": norm_job,
+            "mix": mix_job,
+            "item": item_job,
+            "pack": pack_job,
+            "first": first_job,
+            "input": input_job,
+        }
+        for name, (start, count) in plan.jobs.items():
+            job = functools.partial(run[name], tick - start)
+            pl.when((tick >= start) & (tick < start + count))(job)
 
         return carry
 
@@ -764,7 +809,7 @@
         "grad_branch": pltpu.VMEM((padded, width), BF16),
         "vec": pltpu.VMEM((plan.vector_rows, width), F32),
         "sums": pltpu.VMEM((plan.vector_rows, width), F32),
-        "expand_sums": pltpu.VMEM((plan.ff_jobs, 1, TILE), F32),
+        "expand_sums": pltpu.VMEM((plan.ff_tiles, 1, TILE), F32),
         "vector_land": pltpu.VMEM((len(plan.links), plan.vector_rows, width), F32),
         "load_sems": pltpu.SemaphoreType.DMA((6,)),
         "vector_sems": pltpu.SemaphoreType.DMA((2, len(plan.links))),

time: 200 us -> 195 us (0.975)
  Pallas kernels: 199 us -> 194 us
    pallas_call x1, Pallas kernels: 195 us -> 190 us  [shards(): pl.pallas_call(functools.partial(layer_kernel, plan, (*inputs, *outputs,...]
where the time goes in v5:
time: 195 us
  Pallas kernels  194 us (99%)
    pallas_call x1, Pallas kernels, shards(): pl.pallas_call(functools.partial(layer_kernel, plan, (*inputs, *outputs,...  190 us
    pallas_call x1, Pallas kernels, shards(): pl.pallas_call(functools.partial(write_kernel, plan), out_shape=shapes, i...  4.08 us

profile of v5, /device:TPU:0, one launch (start us, length us, event | category | flops | bytes accessed | tf_op | source)
XLA Modules:
  0.0 194.5 jit_solution(12944839511286723579)
XLA Ops:
  0.7 189.8 %layer.1 = (bf16[7,72,768]{2,1,0:T(8,128)(2,1)S(1)}, bf16[7,72,768]{2,1,0:T(8,128)(2,1)S(1)}, f32[72,32,768]{2,1,0:T(8,128)S(1)}, f32[16,768]{1,0:T(8,128)S(1)}) custom-call(s32[7]{0:T(128)} %refs_0_.1, bf16[768]{0:T(1024)(128)(2,1)} %refs_1_.1, bf16[768]{0:T(1024)(128)(2,1)} %refs_2_.1, bf16[768]{0:T(1024)(128)(2,1)} %refs_3_.1, bf16[768]{0:T(1024)(128)(2,1)} %refs_4_.1, ...), custom_call_target="tpu_custom_call" | custom-call | tf_op jit(solution)/shard_map/layer/pallas_call | solution.py:825
  190.4 4.1 %write.1 = (bf16[7,72,768]{2,1,0:T(8,128)(2,1)}, bf16[7,72,768]{2,1,0:T(8,128)(2,1)}, f32[24,32,768]{2,1,0:T(8,128)}, f32[6,32,3072]{2,1,0:T(8,128)}, f32[6,32,7...) custom-call(bf16[7,72,768]{2,1,0:T(8,128)(2,1)S(1)} %get-tuple-eleme, ...), custom_call_target="tpu_custom_call" | custom-call | tf_op jit(solution)/shard_map/write/pallas_call | solution.py:845

commit v6 on v5

--- a/solution.py
+++ b/solution.py
@@ -159,7 +159,7 @@
         self.chunks = start
         self.ff_tiles = ff // TILE
         self.split = self.phases[1][0] // self.ff_tiles
-        assert self.split >= 1
+        assert self.split in (1, 2)
         tall = ff // narrow
         self.groups = tall // TILE if tall % TILE == 0 else 1
         self.blocks = self.ff_tiles // self.groups
@@ -269,8 +269,8 @@
         value = r.eb[row * width : (row + 1) * width].astype(F32)
         r.vec[8 + row : 9 + row, :] = value.reshape(1, width)
     r.stage[rows:, :] = jnp.zeros((padded - rows, width), F32)
-    r.sums[...] = jnp.zeros_like(r.sums)
-    r.expand_sums[...] = jnp.zeros_like(r.expand_sums)
+    for ref in (r.sums, r.acc_out, r.acc_grad):
+        ref[...] = jnp.zeros_like(ref)
     loads["tok"].wait()
 
     def first_norm(item):
@@ -278,21 +278,17 @@
         r.stage[item_rows(item), :] = unit * vector(0) + vector(1)
 
     each_item(first_norm)
+    r.first_rows[...] = r.stage[...].astype(BF16)
     for name in ("mw", "ew", "cot", "sw"):
         loads[name].start()
-    r.rowb[...] = r.stage[...].astype(BF16)
     loads["jw"].wait()
     for part, bias in enumerate((2, None, 3)):
 
-        def joint_tile(tile):
-            cols = aligned(part * width + tile * TILE, TILE, TILE)
-            value = matmul(r.rowb[...], r.jw[:, cols])
-            if bias is not None:
-                value = value + r.vec[bias : bias + 1, aligned(tile * TILE, TILE, TILE)]
-            r.qkv[:, cols] = value.astype(BF16).astype(F32)
-
-        each_tile(width // TILE, joint_tile)
-    r.first_t[...] = r.stage[...].T.astype(BF16)
+        cols = slice(part * width, (part + 1) * width)
+        value = matmul(r.first_rows[...], r.jw[:, cols])
+        if bias is not None:
+            value = value + vector(bias)
+        r.qkv[:, cols] = value.astype(BF16).astype(F32)
     r.qkv[rows:, :] = jnp.zeros((padded - rows, 3 * width), F32)
 
     def attend_item(item):
@@ -300,28 +296,26 @@
         key_live = (
             lax.broadcasted_iota(jnp.int32, (2 * slots, slots), 1) < r.visible[item]
         )
-        for pair in range(pairs):
-            query = both_heads(r.qkv[here, pair_lanes(0, pair)])
-            keys = r.qkv[here, pair_lanes(1, pair)].astype(BF16)
-            values = r.qkv[here, pair_lanes(2, pair)].astype(BF16)
-            logits = matmul(query, keys, ((1,), (1,))) * score_scale
-            logits = jnp.where(key_live, logits, -1000000000.0)
-            expo = jnp.exp(logits - jnp.max(logits, axis=-1, keepdims=True))
-            attend = expo * (1.0 / jnp.sum(expo, axis=-1, keepdims=True))
-            r.attend[item * pairs + pair] = attend
-            mixed = one_head_each(matmul(attend.astype(BF16), values))
-            r.stage[here, pair_lanes(0, pair)] = mixed
+        every = range(pairs)
+        queries = [both_heads(r.qkv[here, pair_lanes(0, pair)]) for pair in every]
+        keys = [r.qkv[here, pair_lanes(1, pair)].astype(BF16) for pair in every]
+        values = [r.qkv[here, pair_lanes(2, pair)].astype(BF16) for pair in every]
+        logits = [matmul(queries[pair], keys[pair], ((1,), (1,))) for pair in every]
+        logits = [jnp.where(key_live, value * score_scale, -1000000000.0) for value in logits]
+        tops = [jnp.max(value, axis=-1, keepdims=True) for value in logits]
+        expos = [jnp.exp(logits[pair] - tops[pair]) for pair in every]
+        totals = [jnp.sum(value, axis=-1, keepdims=True) for value in expos]
+        attends = [expos[pair] * (1.0 / totals[pair]) for pair in every]
+        mixed = [matmul(attends[pair].astype(BF16), values[pair]) for pair in every]
+        for pair in every:
+            r.attend[item * pairs + pair] = attends[pair]
+            r.stage[here, pair_lanes(0, pair)] = one_head_each(mixed[pair])
 
     each_item(attend_item)
-    r.rowb[...] = r.stage[...].astype(BF16)
+    r.mixed_rows[...] = r.stage[...].astype(BF16)
     loads["mw"].wait()
 
-    def mixer_tile(tile):
-        cols = aligned(tile * TILE, TILE, TILE)
-        r.middle[:, cols] = matmul(r.rowb[...], r.mw[:, cols]) + r.vec[4:5, cols]
-
-    each_tile(width // TILE, mixer_tile)
-    r.mixed_t[...] = r.stage[...].T.astype(BF16)
+    r.middle[...] = matmul(r.mixed_rows[...], r.mw[...]) + vector(4)
 
     def second_norm(item):
         here = item_rows(item)
@@ -341,25 +335,17 @@
             aligned(lax.rem(tile, per_row) * TILE, TILE, TILE),
         ]
 
-    every_row = slice(0, padded)
-
-    def hidden_tile(tile, some):
+    def hidden_tile(tile):
         cols = aligned(tile * TILE, TILE, TILE)
-        hidden = matmul(r.second[some, :], r.ew[:, cols]) + expand_bias(tile)
+        hidden = matmul(r.second[...], r.ew[:, cols]) + expand_bias(tile)
         return hidden, 0.5 + 0.5 * lax.erf(hidden * ROOT_HALF)
-
-    def activate(tile, some, hidden, normal):
-        cols = aligned(tile * TILE, TILE, TILE)
-        active = hidden * normal
-        r.wide_rows[some, cols] = active.astype(BF16)
-        r.active_t[cols, some] = active.T.astype(BF16)
 
     def expand_tile(place):
         tile = place * plan.groups
-        activate(tile, every_row, *hidden_tile(tile, every_row))
+        hidden, normal = hidden_tile(tile)
+        r.active_t[aligned(tile * TILE, TILE, TILE), :] = (hidden * normal).astype(BF16).T
 
     each_tile(plan.blocks, expand_tile)
-    r.second_t[...] = r.stage[...].T.astype(BF16)
     loads["cot"].wait()
 
     def mask_cotangent(item):
@@ -378,36 +364,46 @@
         last = jnp.minimum(first + size, count)
         lax.fori_loop(first, last, lambda place, carry: (body(place), carry)[1], 0)
 
+    def in_turns(turn, first_half, second_half):
+        number = lax.div(turn, plan.split)
+        if plan.split == 1:
+            first_half(number)
+            second_half(number)
+        else:
+            half = lax.rem(turn, plan.split)
+            pl.when(half == 0)(lambda: first_half(number))
+            pl.when(half == 1)(lambda: second_half(number))
+
     def ff_job(turn):
-        step_number, half = lax.div(turn, plan.split), lax.rem(turn, plan.split)
-        group = lax.rem(lax.div(step_number, plan.blocks) + 1, plan.groups)
-        tile = lax.rem(step_number, plan.blocks) * plan.groups + group
-        size = padded // plan.split
-        some = aligned(half * size, size, size)
-        cols = aligned(tile * TILE, TILE, TILE)
-        hidden, normal = hidden_tile(tile, some)
-
-        @pl.when(step_number < plan.ff_tiles - plan.blocks)
-        def _():
-            activate(tile, some, hidden, normal)
-
-        grad = matmul(r.grad_out[some, :], r.sw[cols, :], ((1,), (1,)))
-        slope = normal + hidden * (PEAK * jnp.exp(-0.5 * hidden * hidden))
-        grad_hidden = (grad * slope).astype(BF16)
-        output = matmul(r.wide_rows[some, cols], r.sw[cols, :])
-        r.wide_rows[some, cols] = grad_hidden
-        r.expand_sums[tile] += jnp.sum(grad_hidden.astype(F32), axis=0, keepdims=True)
-        grad_second = matmul(grad_hidden, r.ew[:, cols], ((1,), (1,)))
-
-        @pl.when(step_number == 0)
-        def _():
-            r.acc_out[some, :] = output
-            r.acc_grad[some, :] = grad_second
-
-        @pl.when(step_number > 0)
-        def _():
-            r.acc_out[some, :] += output
-            r.acc_grad[some, :] += grad_second
+        def tile_job(number):
+            group = lax.rem(lax.div(number, plan.blocks) + 1, plan.groups)
+            tile = lax.rem(number, plan.blocks) * plan.groups + group
+            cols = aligned(tile * TILE, TILE, TILE)
+            hidden, normal = hidden_tile(tile)
+            active = (hidden * normal).astype(BF16)
+            r.active_t[cols, :] = active.T
+            slope = normal + hidden * (PEAK * jnp.exp(-0.5 * hidden * hidden))
+            grad = matmul(r.grad_out[...], r.sw[cols, :], ((1,), (1,)))
+            grad_hidden = (grad * slope).astype(BF16)
+            r.grad_hidden[:, cols] = grad_hidden
+            r.expand_sums[tile] = jnp.sum(grad_hidden.astype(F32), axis=0, keepdims=True)
+            r.acc_out[...] += matmul(active, r.sw[cols, :])
+            r.acc_grad[...] += matmul(grad_hidden, r.ew[:, cols], ((1,), (1,)))
+
+        def turn_rows(number):
+            for place, (rows_ref, turned) in enumerate(
+                (
+                    (r.second, r.second_t),
+                    (r.mixed_rows, r.mixed_t),
+                    (r.first_rows, r.first_t),
+                )
+            ):
+
+                @pl.when(number == place)
+                def _():
+                    turned[...] = rows_ref[...].T
+
+        in_turns(turn, tile_job, turn_rows)
 
     def norm_job(turn):
         def one(item):
@@ -445,29 +441,31 @@
         each_tile(width // TILE, one)
 
     def item_job(turn):
-        item, half = lax.div(turn, plan.split), lax.rem(turn, plan.split)
-        here = item_rows(item)
-        size = pairs // plan.split
-
-        def lanes_of(part, pair):
-            start = part * width + (half * size + pair) * 2 * HEAD_DIM
-            return aligned(start, 2 * HEAD_DIM, 2 * HEAD_DIM)
-
-        for pair in range(size):
-            query = both_heads(r.qkv[here, lanes_of(0, pair)])
-            keys = r.qkv[here, lanes_of(1, pair)].astype(BF16)
-            values = r.qkv[here, lanes_of(2, pair)].astype(BF16)
-            grad_mixed = both_heads(r.stage[here, lanes_of(0, pair)])
-            attend = r.attend[item * pairs + half * size + pair]
-            grad_attend = matmul(grad_mixed, values, ((1,), (1,)))
-            grad_value = matmul(attend.astype(BF16), grad_mixed, ((0,), (0,)))
-            inner_sum = jnp.sum(attend * grad_attend, axis=-1, keepdims=True)
-            grad_logits = (attend * (grad_attend - inner_sum)).astype(BF16)
-            grad_query = one_head_each(matmul(grad_logits, keys)) * score_scale
-            grad_key = matmul(grad_logits, query, ((0,), (0,))) * score_scale
-            r.qkv[here, lanes_of(0, pair)] = grad_query
-            r.qkv[here, lanes_of(1, pair)] = grad_key
-            r.qkv[here, lanes_of(2, pair)] = grad_value
+        def scores(item):
+            here = item_rows(item)
+            for pair in range(pairs):
+                values = r.qkv[here, pair_lanes(2, pair)].astype(BF16)
+                grad_mixed = both_heads(r.stage[here, pair_lanes(0, pair)])
+                attend = r.attend[item * pairs + pair]
+                grad_attend = matmul(grad_mixed, values, ((1,), (1,)))
+                inner_sum = jnp.sum(attend * grad_attend, axis=-1, keepdims=True)
+                r.grad_logits[pair] = (attend * (grad_attend - inner_sum)).astype(BF16)
+                r.qkv[here, pair_lanes(2, pair)] = matmul(
+                    attend.astype(BF16), grad_mixed, ((0,), (0,))
+                )
+
+        def inputs(item):
+            here = item_rows(item)
+            for pair in range(pairs):
+                query = both_heads(r.qkv[here, pair_lanes(0, pair)])
+                keys = r.qkv[here, pair_lanes(1, pair)].astype(BF16)
+                grad_logits = r.grad_logits[pair]
+                grad_query = one_head_each(matmul(grad_logits, keys)) * score_scale
+                grad_key = matmul(grad_logits, query, ((0,), (0,))) * score_scale
+                r.qkv[here, pair_lanes(0, pair)] = grad_query
+                r.qkv[here, pair_lanes(1, pair)] = grad_key
+
+        in_turns(turn, scores, inputs)
 
     def joint_rows(part):
         return slice(part * padded, (part + 1) * padded)
@@ -616,7 +614,7 @@
     def produce(item):
         slot = lax.rem(item, 2)
         lefts = (r.active_t, r.second_t, r.mixed_t, r.first_t)
-        rights = (r.grad_out, r.wide_rows, r.grad_branch, r.sw)
+        rights = (r.grad_out, r.grad_hidden, r.grad_branch, r.sw)
         for phase, (start, count, rows_block, windows) in enumerate(plan.phases):
             left, right = lefts[phase], rights[phase]
 
@@ -793,7 +791,8 @@
         "ew": pltpu.VMEM(expand_weight.shape, BF16),
         "sw": pltpu.VMEM(shrink_weight.shape, BF16),
         "stage": pltpu.VMEM((padded, width), F32),
-        "rowb": pltpu.VMEM((padded, width), BF16),
+        "first_rows": pltpu.VMEM((padded, width), BF16),
+        "mixed_rows": pltpu.VMEM((padded, width), BF16),
         "qkv": pltpu.VMEM((padded, 3 * width), F32),
         "attend": pltpu.VMEM((items * plan.pairs, 2 * slots, slots), F32),
         "first_t": pltpu.VMEM((width, padded), BF16),
@@ -801,13 +800,14 @@
         "second": pltpu.VMEM((padded, width), BF16),
         "second_t": pltpu.VMEM((width, padded), BF16),
         "middle": pltpu.VMEM((padded, width), F32),
-        "wide_rows": pltpu.VMEM((padded, ff), BF16),
+        "grad_hidden": pltpu.VMEM((padded, ff), BF16),
         "active_t": pltpu.VMEM((ff, padded), BF16),
         "grad_out": pltpu.VMEM((padded, width), BF16),
         "acc_out": pltpu.VMEM((padded, width), F32),
         "acc_grad": pltpu.VMEM((padded, width), F32),
         "grad_branch": pltpu.VMEM((padded, width), BF16),
         "vec": pltpu.VMEM((plan.vector_rows, width), F32),
+        "grad_logits": pltpu.VMEM((plan.pairs, 2 * slots, slots), BF16),
         "sums": pltpu.VMEM((plan.vector_rows, width), F32),
         "expand_sums": pltpu.VMEM((plan.ff_tiles, 1, TILE), F32),
         "vector_land": pltpu.VMEM((len(plan.links), plan.vector_rows, width), F32),
@@ -829,7 +829,7 @@
         out_specs=[vmem] * len(outputs),
         scratch_shapes=list(scratch.values()),
         compiler_params=pltpu.CompilerParams(
-            has_side_effects=True, vmem_limit_bytes=51 * 2**20, collective_id=0
+            has_side_effects=True, vmem_limit_bytes=52 * 2**20, collective_id=0
         ),
         name="layer",
     )(*(value for value, _ in inputs.values()))

time: 195 us -> 185 us (0.949)
  Pallas kernels: 194 us -> 184 us
    pallas_call x1, Pallas kernels: 190 us -> 180 us  [shards(): pl.pallas_call(functools.partial(layer_kernel, plan, (*inputs, *outputs,...]
where the time goes in v6:
time: 185 us
  Pallas kernels  184 us (99%)
    pallas_call x1, Pallas kernels, shards(): pl.pallas_call(functools.partial(layer_kernel, plan, (*inputs, *outputs,...  180 us
    pallas_call x1, Pallas kernels, shards(): pl.pallas_call(functools.partial(write_kernel, plan), out_shape=shapes, i...  4.08 us

profile of v6, /device:TPU:0, one launch (start us, length us, event | category | flops | bytes accessed | tf_op | source)
XLA Modules:
  0.0 184.7 jit_solution(3962972582440858382)
XLA Ops:
  0.7 179.9 %layer.1 = (bf16[7,72,768]{2,1,0:T(8,128)(2,1)S(1)}, bf16[7,72,768]{2,1,0:T(8,128)(2,1)S(1)}, f32[72,32,768]{2,1,0:T(8,128)S(1)}, f32[16,768]{1,0:T(8,128)S(1)}) custom-call(s32[7]{0:T(128)} %refs_0_.1, bf16[768]{0:T(1024)(128)(2,1)} %refs_1_.1, bf16[768]{0:T(1024)(128)(2,1)} %refs_2_.1, bf16[768]{0:T(1024)(128)(2,1)} %refs_3_.1, bf16[768]{0:T(1024)(128)(2,1)} %refs_4_.1, ...), custom_call_target="tpu_custom_call" | custom-call | tf_op jit(solution)/shard_map/layer/pallas_call | solution.py:825
  180.6 4.1 %write.1 = (bf16[7,72,768]{2,1,0:T(8,128)(2,1)}, bf16[7,72,768]{2,1,0:T(8,128)(2,1)}, f32[24,32,768]{2,1,0:T(8,128)}, f32[6,32,3072]{2,1,0:T(8,128)}, f32[6,32,7...) custom-call(bf16[7,72,768]{2,1,0:T(8,128)(2,1)S(1)} %get-tuple-eleme, ...), custom_call_target="tpu_custom_call" | custom-call | tf_op jit(solution)/shard_map/write/pallas_call | solution.py:845

commit v7 on v6

--- a/solution.py
+++ b/solution.py
@@ -11,7 +11,7 @@
 HEAD_DIM = 64
 EPSILON = 1e-06
 SUB = 8
-LAGS = ([1, 2, 2, 2, 2, 2, 2, 2], [1, 2, 2, 2, 2, 2, 2, 2])
+LAGS = ([1] + [2] * 15, [1] + [2] * 15)
 MOST = 32
 TILE = 256
 MESH = pl.DeviceIdType.MESH
@@ -51,8 +51,11 @@
         self.column, self.columns, self.picks = column, columns, picks
         self.sums, self.moves = sums, sums + gathers
         self.selects = selects
-        self.lags = LAGS[column > 0] if len(self.moves) == 8 else [1] + [2] * (len(self.moves) - 1)
+        self.lags = LAGS[column > 0][: len(self.moves)]
         self.due = [sum(self.lags[: stage + 1]) for stage in range(len(self.moves))]
+
+    def flights(self, stage):
+        return self.lags[stage] + 1
 
     def slots(self, stage):
         after = self.lags[stage + 1] if stage + 1 < len(self.sums) else 0
@@ -82,7 +85,7 @@
         x, y, core = (("wide", 0),), (("narrow", 1),), (("narrow", 0),)
         if (narrow, wide) == (4, 8):
             self.links = (core, y, x, near, mirror)
-            half, quarter = chunk // 2, chunk // 4
+            half = chunk // 2
             z_bit, x_bit, y_bit, core_bit = ("wide", 2), x[0], y[0], core[0]
             one = Part(
                 0,
@@ -93,14 +96,13 @@
                     Move("halve", y, chunk, y_bit),
                     Move("fold", near, chunk),
                     Move("halve", mirror, half, z_bit, True),
-                    Move("halve", x, quarter, x_bit, True),
+                    Move("add", x, half, inner=True),
                 ],
                 [
-                    Move("double", x, quarter, inner=True),
                     Move("double", mirror, half, inner=True),
                     Move("unfold", near, chunk),
                 ],
-                [(z_bit, half), (x_bit, quarter)],
+                [(z_bit, half)],
             )
             two = Part(
                 width // 3 * 2,
@@ -114,14 +116,13 @@
                     Move("halve", x, chunk, x_bit),
                     Move("halve", y, half, y_bit),
                     Move("fold", near, half),
-                    Move("halve", mirror, quarter, z_bit, True),
+                    Move("add", mirror, half, inner=True),
                 ],
                 [
-                    Move("double", mirror, quarter, inner=True),
                     Move("unfold", near, half),
                     Move("double", x, half),
                 ],
-                [(x_bit, half), (z_bit, quarter)],
+                [(x_bit, half)],
             )
             self.parts = (one, two)
         else:
@@ -142,9 +143,13 @@
             self.parts = (Part(0, width, picks, sums, gathers, selects),)
         self.stages = max(len(part.moves) for part in self.parts)
         self.depth = max(part.due[-1] for part in self.parts)
-        self.slots_most = max(
-            part.slots(stage) for part in self.parts for stage in range(len(part.moves))
-        )
+        self.arrivals, self.sends, self.arrival_at, self.send_at = 0, 0, {}, {}
+        for number, part in enumerate(self.parts):
+            for stage in range(len(part.moves)):
+                self.arrival_at[number, stage] = self.arrivals
+                self.send_at[number, stage] = self.sends
+                self.arrivals += part.slots(stage)
+                self.sends += part.flights(stage)
         self.phases = []
         start = 0
         for rows_block, windows in (
@@ -164,7 +169,7 @@
         self.groups = tall // TILE if tall % TILE == 0 else 1
         self.blocks = self.ff_tiles // self.groups
         self.jobs = {}
-        tick = 0
+        tick = self.split - 1
         for name, count in (
             ("ff", self.ff_tiles * self.split),
             ("norm", self.split),
@@ -555,7 +560,8 @@
     def transfer(number, stage, item):
         part = plan.parts[number]
         move = part.moves[stage]
-        slot = lax.rem(item, part.slots(stage))
+        arrival = plan.arrival_at[number, stage] + lax.rem(item, part.slots(stage))
+        send = plan.send_at[number, stage] + lax.rem(item, part.flights(stage))
         if stage < len(part.sums):
             src = source(number, stage, item).at[
                 aligned(given[number, stage], move.length, SUB)
@@ -567,8 +573,8 @@
         return pltpu.make_async_remote_copy(
             src_ref=src,
             dst_ref=dst,
-            send_sem=r.send_sems.at[number, stage, slot],
-            recv_sem=r.recv_sems.at[number, stage, slot],
+            send_sem=r.send_sems.at[send],
+            recv_sem=r.recv_sems.at[arrival],
             device_id=partners[move.flips],
             device_id_type=MESH,
         )
@@ -813,8 +819,8 @@
         "vector_land": pltpu.VMEM((len(plan.links), plan.vector_rows, width), F32),
         "load_sems": pltpu.SemaphoreType.DMA((6,)),
         "vector_sems": pltpu.SemaphoreType.DMA((2, len(plan.links))),
-        "send_sems": pltpu.SemaphoreType.DMA((len(plan.parts), plan.stages, plan.slots_most)),
-        "recv_sems": pltpu.SemaphoreType.DMA((len(plan.parts), plan.stages, plan.slots_most)),
+        "send_sems": pltpu.SemaphoreType.DMA((plan.sends,)),
+        "recv_sems": pltpu.SemaphoreType.DMA((plan.arrivals,)),
     }
     for number, part in enumerate(plan.parts):
         scratch[f"part{number}"] = pltpu.VMEM((2, narrow * chunk, part.columns), F32)

time: 185 us -> 178 us (0.962)
  Pallas kernels: 184 us -> 177 us
    pallas_call x1, Pallas kernels: 180 us -> 173 us  [shards(): pl.pallas_call(functools.partial(layer_kernel, plan, (*inputs, *outputs,...]
where the time goes in v7:
time: 178 us
  Pallas kernels  177 us (99%)
    pallas_call x1, Pallas kernels, shards(): pl.pallas_call(functools.partial(layer_kernel, plan, (*inputs, *outputs,...  173 us
    pallas_call x1, Pallas kernels, shards(): pl.pallas_call(functools.partial(write_kernel, plan), out_shape=shapes, i...  4.08 us

profile of v7, /device:TPU:0, one launch (start us, length us, event | category | flops | bytes accessed | tf_op | source)
XLA Modules:
  0.0 178.1 jit_solution(15461717308651704376)
XLA Ops:
  0.7 173.4 %layer.1 = (bf16[7,72,768]{2,1,0:T(8,128)(2,1)S(1)}, bf16[7,72,768]{2,1,0:T(8,128)(2,1)S(1)}, f32[72,32,768]{2,1,0:T(8,128)S(1)}, f32[16,768]{1,0:T(8,128)S(1)}) custom-call(s32[7]{0:T(128)} %refs_0_.1, bf16[768]{0:T(1024)(128)(2,1)} %refs_1_.1, bf16[768]{0:T(1024)(128)(2,1)} %refs_2_.1, bf16[768]{0:T(1024)(128)(2,1)} %refs_3_.1, bf16[768]{0:T(1024)(128)(2,1)} %refs_4_.1, ...), custom_call_target="tpu_custom_call" | custom-call | tf_op jit(solution)/shard_map/layer/pallas_call | solution.py:831
  174.1 4.1 %write.1 = (bf16[7,72,768]{2,1,0:T(8,128)(2,1)}, bf16[7,72,768]{2,1,0:T(8,128)(2,1)}, f32[24,32,768]{2,1,0:T(8,128)}, f32[6,32,3072]{2,1,0:T(8,128)}, f32[6,32,7...) custom-call(bf16[7,72,768]{2,1,0:T(8,128)(2,1)S(1)} %get-tuple-eleme, ...), custom_call_target="tpu_custom_call" | custom-call | tf_op jit(solution)/shard_map/write/pallas_call | solution.py:851

commit v8 on v7

--- a/solution.py
+++ b/solution.py
@@ -14,6 +14,11 @@
 LAGS = ([1] + [2] * 15, [1] + [2] * 15)
 MOST = 32
 TILE = 256
+U1 = 7
+U2 = 7
+U3 = 7
+U4 = 7
+U5 = 4
 MESH = pl.DeviceIdType.MESH
 ROOT_HALF = 0.5**0.5
 PEAK = 0.3989422804014327
@@ -172,12 +177,12 @@
         tick = self.split - 1
         for name, count in (
             ("ff", self.ff_tiles * self.split),
-            ("norm", self.split),
-            ("mix", 1),
+            ("norm", 1 if self.split == 1 else 4),
+            ("mix", 1 if self.split == 1 else 3),
             ("item", items * self.split),
-            ("pack", 1),
-            ("first", self.split),
-            ("input", self.split),
+            ("pack", 1 if self.split == 1 else 3),
+            ("first", 1 if self.split == 1 else 3),
+            ("input", 1 if self.split == 1 else 4),
         ):
             self.jobs[name] = (tick, count)
             tick += count
@@ -218,6 +223,7 @@
             getattr(r, name + "_in"), getattr(r, name), r.load_sems.at[number]
         )
     loads["tok"].start()
+    loads["cot"].start()
     loads["jw"].start()
 
     barrier = pltpu.get_barrier_semaphore()
@@ -257,11 +263,15 @@
             - unit * jnp.mean(grad * unit, axis=-1, keepdims=True)
         )
 
-    def each_item(body):
-        lax.fori_loop(0, plan.items, lambda item, carry: (body(item), carry)[1], 0)
-
-    def each_tile(count, body):
-        lax.fori_loop(0, count, lambda tile, carry: (body(tile), carry)[1], 0)
+    def each_item(body, unroll=1):
+        lax.fori_loop(
+            0, plan.items, lambda item, carry: (body(item), carry)[1], 0, unroll=unroll
+        )
+
+    def each_tile(count, body, unroll=1):
+        lax.fori_loop(
+            0, count, lambda tile, carry: (body(tile), carry)[1], 0, unroll=unroll
+        )
 
     def pair_lanes(part, pair):
         start = part * width + pair * 2 * HEAD_DIM
@@ -274,18 +284,25 @@
         value = r.eb[row * width : (row + 1) * width].astype(F32)
         r.vec[8 + row : 9 + row, :] = value.reshape(1, width)
     r.stage[rows:, :] = jnp.zeros((padded - rows, width), F32)
-    for ref in (r.sums, r.acc_out, r.acc_grad):
-        ref[...] = jnp.zeros_like(ref)
+    r.sums[...] = jnp.zeros_like(r.sums)
     loads["tok"].wait()
 
     def first_norm(item):
         unit, _ = normalized(r.tok[item].astype(F32))
         r.stage[item_rows(item), :] = unit * vector(0) + vector(1)
 
-    each_item(first_norm)
+    each_item(first_norm, U1)
     r.first_rows[...] = r.stage[...].astype(BF16)
-    for name in ("mw", "ew", "cot", "sw"):
+    for name in ("mw", "ew", "sw"):
         loads[name].start()
+    loads["cot"].wait()
+
+    def mask_cotangent(item):
+        grad = r.cot[item].astype(F32)
+        r.stage[item_rows(item), :] = jnp.where(row_live(item), grad, 0.0)
+
+    each_item(mask_cotangent, U3)
+    r.grad_out[...] = r.stage[...].astype(BF16)
     loads["jw"].wait()
     for part, bias in enumerate((2, None, 3)):
 
@@ -316,7 +333,7 @@
             r.attend[item * pairs + pair] = attends[pair]
             r.stage[here, pair_lanes(0, pair)] = one_head_each(mixed[pair])
 
-    each_item(attend_item)
+    each_item(attend_item, U4)
     r.mixed_rows[...] = r.stage[...].astype(BF16)
     loads["mw"].wait()
 
@@ -329,7 +346,7 @@
         unit, _ = normalized(middle)
         r.stage[here, :] = unit * vector(5) + vector(6)
 
-    each_item(second_norm)
+    each_item(second_norm, U2)
     r.second[...] = r.stage[...].astype(BF16)
     loads["ew"].wait()
 
@@ -350,21 +367,13 @@
         hidden, normal = hidden_tile(tile)
         r.active_t[aligned(tile * TILE, TILE, TILE), :] = (hidden * normal).astype(BF16).T
 
-    each_tile(plan.blocks, expand_tile)
-    loads["cot"].wait()
-
-    def mask_cotangent(item):
-        grad = r.cot[item].astype(F32)
-        r.stage[item_rows(item), :] = jnp.where(row_live(item), grad, 0.0)
-
-    each_item(mask_cotangent)
-    r.grad_out[...] = r.stage[...].astype(BF16)
+    each_tile(plan.blocks, expand_tile, U5)
     loads["sw"].wait()
 
     rows_full = rows // 16 * 16
 
-    def share(count, turn, body):
-        size = -(-count // plan.split)
+    def share(name, count, turn, body):
+        size = -(-count // plan.jobs[name][1])
         first = turn * size
         last = jnp.minimum(first + size, count)
         lax.fori_loop(first, last, lambda place, carry: (body(place), carry)[1], 0)
@@ -395,20 +404,20 @@
             r.acc_out[...] += matmul(active, r.sw[cols, :])
             r.acc_grad[...] += matmul(grad_hidden, r.ew[:, cols], ((1,), (1,)))
 
-        def turn_rows(number):
-            for place, (rows_ref, turned) in enumerate(
-                (
-                    (r.second, r.second_t),
-                    (r.mixed_rows, r.mixed_t),
-                    (r.first_rows, r.first_t),
-                )
-            ):
-
-                @pl.when(number == place)
-                def _():
-                    turned[...] = rows_ref[...].T
-
         in_turns(turn, tile_job, turn_rows)
+
+    def turn_rows(turn):
+        for place, (rows_ref, turned) in enumerate(
+            (
+                (r.second, r.second_t),
+                (r.mixed_rows, r.mixed_t),
+                (r.first_rows, r.first_t),
+            )
+        ):
+
+            @pl.when(turn == place)
+            def _():
+                turned[...] = rows_ref[...].T
 
     def norm_job(turn):
         def one(item):
@@ -429,21 +438,24 @@
                 grad_middle.astype(BF16).astype(F32), axis=0, keepdims=True
             )
 
-        share(plan.items, turn, one)
+        share("norm", plan.items, turn, one)
 
     def mix_job(turn):
+        pl.when(turn == 0)(pack_branch)
+
+        def one(tile):
+            cols = aligned(tile * TILE, TILE, TILE)
+            value = matmul(r.grad_branch[...], r.mw[cols, :], ((1,), (1,)))
+            r.stage[:, cols] = value.astype(BF16).astype(F32)
+
+        share("mix", width // TILE, turn, one)
+
+    def pack_branch():
         r.grad_branch[:rows_full, :] = r.acc_out[:rows_full, :].astype(BF16)
         tail = jnp.concatenate(
             [r.acc_out[rows_full:rows, :], jnp.zeros((padded - rows, width), F32)], axis=0
         )
         r.grad_branch[rows_full:, :] = tail.astype(BF16)
-
-        def one(tile):
-            cols = aligned(tile * TILE, TILE, TILE)
-            value = matmul(r.grad_branch[...], r.mw[cols, :], ((1,), (1,)))
-            r.stage[:, cols] = value.astype(BF16).astype(F32)
-
-        each_tile(width // TILE, one)
 
     def item_job(turn):
         def scores(item):
@@ -477,11 +489,14 @@
 
     def pack_job(turn):
         for part in range(3):
-            value = r.qkv[:, part * width : (part + 1) * width].astype(BF16)
-            r.sw[joint_rows(part), :] = value
-            if part != 1:
-                row = 2 if part == 0 else 3
-                r.sums[row : row + 1, :] = jnp.sum(value.astype(F32), axis=0, keepdims=True)
+
+            @pl.when(turn == part * (plan.jobs["pack"][1] > 1))
+            def _():
+                value = r.qkv[:, part * width : (part + 1) * width].astype(BF16)
+                r.sw[joint_rows(part), :] = value
+                if part != 1:
+                    row = 2 if part == 0 else 3
+                    r.sums[row : row + 1, :] = jnp.sum(value.astype(F32), axis=0, keepdims=True)
 
     def first_job(turn):
         def one(tile):
@@ -496,7 +511,7 @@
                 total = value if total is None else total + value
             r.acc_grad[:, cols] = total
 
-        share(width // TILE, turn, one)
+        share("first", width // TILE, turn, one)
 
     def input_job(turn):
         def one(item):
@@ -508,7 +523,7 @@
             total = r.acc_out[here, :] + norm_backward(grad * vector(0), unit, spread)
             r.tok[item] = total.astype(BF16)
 
-        share(plan.items, turn, one)
+        share("input", plan.items, turn, one)
 
         @pl.when(turn == 0)
         def _():
@@ -690,6 +705,11 @@
                         settle(number, stage, item)
 
         vector_step(tick)
+        @pl.when(tick == 0)
+        def _():
+            for ref in (r.acc_out, r.acc_grad):
+                ref[...] = jnp.zeros_like(ref)
+
         run = {
             "ff": ff_job,
             "norm": norm_job,

time: 178 us -> 175 us (0.983)
  Pallas kernels: 177 us -> 174 us
    pallas_call x1, Pallas kernels: 173 us -> 170 us  [shards(): pl.pallas_call(functools.partial(layer_kernel, plan, (*inputs, *outputs,...]
where the time goes in v8:
time: 175 us
  Pallas kernels  174 us (99%)
    pallas_call x1, Pallas kernels, shards(): pl.pallas_call(functools.partial(layer_kernel, plan, (*inputs, *outputs,...  170 us
    pallas_call x1, Pallas kernels, shards(): pl.pallas_call(functools.partial(write_kernel, plan), out_shape=shapes, i...  4.08 us

profile of v8, /device:TPU:0, one launch (start us, length us, event | category | flops | bytes accessed | tf_op | source)
XLA Modules:
  0.0 174.8 jit_solution(6132913218376931037)
XLA Ops:
  0.7 169.9 %layer.1 = (bf16[7,72,768]{2,1,0:T(8,128)(2,1)S(1)}, bf16[7,72,768]{2,1,0:T(8,128)(2,1)S(1)}, f32[72,32,768]{2,1,0:T(8,128)S(1)}, f32[16,768]{1,0:T(8,128)S(1)}) custom-call(s32[7]{0:T(128)} %refs_0_.1, bf16[768]{0:T(1024)(128)(2,1)} %refs_1_.1, bf16[768]{0:T(1024)(128)(2,1)} %refs_2_.1, bf16[768]{0:T(1024)(128)(2,1)} %refs_3_.1, bf16[768]{0:T(1024)(128)(2,1)} %refs_4_.1, ...), custom_call_target="tpu_custom_call" | custom-call | tf_op jit(solution)/shard_map/layer/pallas_call | solution.py:851
  170.6 4.1 %write.1 = (bf16[7,72,768]{2,1,0:T(8,128)(2,1)}, bf16[7,72,768]{2,1,0:T(8,128)(2,1)}, f32[24,32,768]{2,1,0:T(8,128)}, f32[6,32,3072]{2,1,0:T(8,128)}, f32[6,32,7...) custom-call(bf16[7,72,768]{2,1,0:T(8,128)(2,1)S(1)} %get-tuple-eleme, ...), custom_call_target="tpu_custom_call" | custom-call | tf_op jit(solution)/shard_map/write/pallas_call | solution.py:871

commit v9 on v8

--- a/solution.py
+++ b/solution.py
@@ -189,9 +189,16 @@
         self.vector_tick = tick
         assert self.phases[2][0] >= self.jobs["item"][0]
         assert self.phases[3][0] >= self.jobs["first"][0]
+        self.block = rows
+        self.block_lanes = rows + -rows % 128
+        self.block_order = [reversed_bits(spot, narrow_bits) for spot in range(narrow)]
         self.vector_rows = 8 + ff // width
         self.vector_rows += -self.vector_rows % SUB
         self.ticks = self.chunks + self.depth
+        self.vector_lengths = [narrow * self.vector_rows]
+        for flips in self.links:
+            length = self.vector_lengths[-1]
+            self.vector_lengths.append(length // 2 if flips[0][0] == "narrow" else length)
         self.vector_every = (self.ticks - 1 - self.vector_tick) // len(self.links)
         assert self.vector_every > 0
 
@@ -663,26 +670,53 @@
                         jnp.concatenate(picked, axis=0), other
                     )
 
+    def vector_source(stage):
+        return getattr(r, f"vector{stage}")
+
+    def vector_part(stage, own):
+        before, after = plan.vector_lengths[stage : stage + 2]
+        if before == after:
+            return pl.ds(0, after)
+        bit = bits[plan.links[stage][0]]
+        return aligned((bit if own else 1 - bit) * after, after, SUB)
+
     def vector_exchange(stage):
         return pltpu.make_async_remote_copy(
-            src_ref=r.sums if stage == 0 else r.vector_land.at[stage - 1],
-            dst_ref=r.vector_land.at[stage],
+            src_ref=vector_source(stage).at[vector_part(stage, False)],
+            dst_ref=vector_source(stage + 1),
             send_sem=r.vector_sems.at[0, stage],
             recv_sem=r.vector_sems.at[1, stage],
             device_id=partners[plan.links[stage]],
             device_id_type=MESH,
         )
 
+    def vector_pack():
+        r.vector0[...] = jnp.zeros_like(r.vector0)
+        block = plan.block
+        for spot, owner in enumerate(plan.block_order):
+            base = spot * plan.vector_rows
+            own = slice(owner * block, (owner + 1) * block)
+            r.vector0[base : base + 8, :block] = r.sums[:8, own]
+            for piece in range(plan.ff // width):
+                place = owner * (plan.ff // narrow) + piece * block
+                row, start = 8 + place // width, place % width
+                r.vector0[base + 8 + piece : base + 9 + piece, :block] = r.sums[
+                    row : row + 1, start : start + block
+                ]
+
     def vector_step(tick):
         count = len(plan.links)
         for stage in range(count + 1):
 
             @pl.when(tick == plan.vector_tick + stage * plan.vector_every)
             def _():
-                if stage > 0:
+                if stage == 0:
+                    vector_pack()
+                else:
                     vector_exchange(stage - 1).wait()
-                    before = r.sums if stage == 1 else r.vector_land.at[stage - 2]
-                    r.vector_land[stage - 1] += before[...]
+                    vector_source(stage)[...] += vector_source(stage - 1)[
+                        vector_part(stage - 1, True)
+                    ]
                 if stage < count:
                     vector_exchange(stage).start()
 
@@ -726,7 +760,7 @@
         return carry
 
     lax.fori_loop(0, plan.ticks, step, 0)
-    r.vector_out[...] = r.vector_land[len(plan.links) - 1]
+    r.vector_out[...] = vector_source(len(plan.links))[...]
 
 
 def write_kernel(plan, tok, cot, whole, sums, *refs):
@@ -744,18 +778,12 @@
     ]
     for copy in copies:
         copy.start()
-    own = lax.axis_index("narrow")
-    for place in range(plan.narrow):
-
-        @pl.when(own == place)
-        def _():
-            for row, out in enumerate(outs[6:14]):
-                size = out.shape[0]
-                out[...] = sums[row : row + 1, place * size : (place + 1) * size].reshape(size)
-            size = outs[14].shape[0]
-            row, start = 8 + place * size // plan.width, place * size % plan.width
-            outs[14][...] = sums[row : row + 1, start : start + size].reshape(size)
-
+    for row, out in enumerate(outs[6:14]):
+        out[...] = sums[row : row + 1, : plan.block].reshape(plan.block)
+    pieces = [
+        sums[8 + piece : 9 + piece, : plan.block] for piece in range(plan.ff // plan.width)
+    ]
+    outs[14][...] = jnp.concatenate(pieces, axis=1).reshape(plan.ff // plan.narrow)
     for copy in copies:
         copy.wait()
 
@@ -809,7 +837,7 @@
         "tok": (tokens.shape, BF16),
         "cot": (tokens.shape, BF16),
         "whole": ((plan.chunks, chunk, width), F32),
-        "vector_out": ((plan.vector_rows, width), F32),
+        "vector_out": ((plan.vector_rows, plan.block_lanes), F32),
     }
     scratch = {
         "jw": pltpu.VMEM(joint_weight.shape, BF16),
@@ -836,12 +864,13 @@
         "grad_logits": pltpu.VMEM((plan.pairs, 2 * slots, slots), BF16),
         "sums": pltpu.VMEM((plan.vector_rows, width), F32),
         "expand_sums": pltpu.VMEM((plan.ff_tiles, 1, TILE), F32),
-        "vector_land": pltpu.VMEM((len(plan.links), plan.vector_rows, width), F32),
         "load_sems": pltpu.SemaphoreType.DMA((6,)),
         "vector_sems": pltpu.SemaphoreType.DMA((2, len(plan.links))),
         "send_sems": pltpu.SemaphoreType.DMA((plan.sends,)),
         "recv_sems": pltpu.SemaphoreType.DMA((plan.arrivals,)),
     }
+    for stage, length in enumerate(plan.vector_lengths):
+        scratch[f"vector{stage}"] = pltpu.VMEM((length, plan.block_lanes), F32)
     for number, part in enumerate(plan.parts):
         scratch[f"part{number}"] = pltpu.VMEM((2, narrow * chunk, part.columns), F32)
         for stage, move in enumerate(part.sums):

time: 175 us -> 172 us (0.983)
  Pallas kernels: 174 us -> 171 us
    pallas_call x1, Pallas kernels: 170 us -> 167 us  [shards(): pl.pallas_call(functools.partial(layer_kernel, plan, (*inputs, *outputs,...]
where the time goes in v9:
time: 172 us
  Pallas kernels  171 us (99%)
    pallas_call x1, Pallas kernels, shards(): pl.pallas_call(functools.partial(layer_kernel, plan, (*inputs, *outputs,...  167 us
    pallas_call x1, Pallas kernels, shards(): pl.pallas_call(functools.partial(write_kernel, plan), out_shape=shapes, i...  4.08 us

profile of v9, /device:TPU:0, one launch (start us, length us, event | category | flops | bytes accessed | tf_op | source)
XLA Modules:
  0.0 171.9 jit_solution(3408010746889378468)
XLA Ops:
  0.7 167.0 %layer.1 = (bf16[7,72,768]{2,1,0:T(8,128)(2,1)S(1)}, bf16[7,72,768]{2,1,0:T(8,128)(2,1)S(1)}, f32[72,32,768]{2,1,0:T(8,128)S(1)}, f32[16,256]{1,0:T(8,128)S(1)}) custom-call(s32[7]{0:T(128)} %refs_0_.1, bf16[768]{0:T(1024)(128)(2,1)} %refs_1_.1, bf16[768]{0:T(1024)(128)(2,1)} %refs_2_.1, bf16[768]{0:T(1024)(128)(2,1)} %refs_3_.1, bf16[768]{0:T(1024)(128)(2,1)} %refs_4_.1, ...), custom_call_target="tpu_custom_call" | custom-call | tf_op jit(solution)/shard_map/layer/pallas_call | solution.py:880
  167.6 4.1 %write.1 = (bf16[7,72,768]{2,1,0:T(8,128)(2,1)}, bf16[7,72,768]{2,1,0:T(8,128)(2,1)}, f32[24,32,768]{2,1,0:T(8,128)}, f32[6,32,3072]{2,1,0:T(8,128)}, f32[6,32,7...) custom-call(bf16[7,72,768]{2,1,0:T(8,128)(2,1)S(1)} %get-tuple-eleme, ...), custom_call_target="tpu_custom_call" | custom-call | tf_op jit(solution)/shard_map/write/pallas_call | solution.py:900

commit v10 on v9

--- a/solution.py
+++ b/solution.py
@@ -11,7 +11,7 @@
 HEAD_DIM = 64
 EPSILON = 1e-06
 SUB = 8
-LAGS = ([1] + [2] * 15, [1] + [2] * 15)
+LAGS = ([1, 2, 2, 2, 2, 2, 3] + [2] * 8, [1] + [2] * 15)
 MOST = 32
 TILE = 256
 U1 = 7
@@ -285,11 +285,12 @@
         return slice(start, start + 2 * HEAD_DIM)
 
     small = (r.g1, r.s1, r.qb, r.vb, r.mb, r.g2, r.s2, r.sb)
-    for row, ref in enumerate(small):
-        r.vec[row : row + 1, :] = ref[...].astype(F32).reshape(1, width)
-    for row in range(plan.ff // width):
-        value = r.eb[row * width : (row + 1) * width].astype(F32)
-        r.vec[8 + row : 9 + row, :] = value.reshape(1, width)
+
+    def place_small(first, last):
+        for row in range(first, last):
+            r.vec[row : row + 1, :] = small[row][...].astype(F32).reshape(1, width)
+
+    place_small(0, 2)
     r.stage[rows:, :] = jnp.zeros((padded - rows, width), F32)
     r.sums[...] = jnp.zeros_like(r.sums)
     loads["tok"].wait()
@@ -310,6 +311,10 @@
 
     each_item(mask_cotangent, U3)
     r.grad_out[...] = r.stage[...].astype(BF16)
+    place_small(2, 8)
+    for row in range(plan.ff // width):
+        value = r.eb[row * width : (row + 1) * width].astype(F32)
+        r.vec[8 + row : 9 + row, :] = value.reshape(1, width)
     loads["jw"].wait()
     for part, bias in enumerate((2, None, 3)):
 
@@ -764,7 +769,7 @@
 
 
 def write_kernel(plan, tok, cot, whole, sums, *refs):
-    outs, sems = refs[:-1], refs[-1]
+    outs, held, sems = refs[:15], refs[15:-1], refs[-1]
     copies = [(tok, outs[0]), (cot, outs[1])]
     for (start, count, _, windows), out in zip(plan.phases, outs[2:6]):
         tall = count // windows
@@ -778,12 +783,16 @@
     ]
     for copy in copies:
         copy.start()
-    for row, out in enumerate(outs[6:14]):
-        out[...] = sums[row : row + 1, : plan.block].reshape(plan.block)
+    for row, ref in enumerate(held[:8]):
+        ref[...] = sums[row : row + 1, : plan.block].reshape(plan.block)
     pieces = [
         sums[8 + piece : 9 + piece, : plan.block] for piece in range(plan.ff // plan.width)
     ]
-    outs[14][...] = jnp.concatenate(pieces, axis=1).reshape(plan.ff // plan.narrow)
+    held[8][...] = jnp.concatenate(pieces, axis=1).reshape(plan.ff // plan.narrow)
+    for source, target in zip(held, outs[6:]):
+        copy = pltpu.make_async_copy(source, target, sems.at[len(copies)])
+        copy.start()
+        copies.append(copy)
     for copy in copies:
         copy.wait()
 
@@ -901,8 +910,9 @@
         functools.partial(write_kernel, plan),
         out_shape=shapes,
         in_specs=[vmem] * len(results),
-        out_specs=[hbm] * 6 + [vmem] * 9,
-        scratch_shapes=[pltpu.SemaphoreType.DMA((copies,))],
+        out_specs=[hbm] * 15,
+        scratch_shapes=[pltpu.VMEM(shape.shape, F32) for shape in shapes[6:]]
+        + [pltpu.SemaphoreType.DMA((copies + 9,))],
         compiler_params=pltpu.CompilerParams(vmem_limit_bytes=4 * 2**20),
         name="write",
     )(*(pltpu.with_memory_space_constraint(value, pltpu.VMEM) for value in results))

time: 172 us -> 170 us (0.988)
  Pallas kernels: 171 us -> 169 us
where the time goes in v10:
time: 170 us
  Pallas kernels  169 us (99%)
    pallas_call x1, Pallas kernels, shards(): pl.pallas_call(functools.partial(layer_kernel, plan, (*inputs, *outputs,...  166 us
    pallas_call x1, Pallas kernels, shards(): pl.pallas_call(functools.partial(write_kernel, plan), out_shape=shapes, i...  3.56 us

profile of v10, /device:TPU:0, one launch (start us, length us, event | category | flops | bytes accessed | tf_op | source)
XLA Modules:
  0.0 170.2 jit_solution(11576493061760324062)
XLA Ops:
  0.7 165.8 %layer.1 = (bf16[7,72,768]{2,1,0:T(8,128)(2,1)S(1)}, bf16[7,72,768]{2,1,0:T(8,128)(2,1)S(1)}, f32[72,32,768]{2,1,0:T(8,128)S(1)}, f32[16,256]{1,0:T(8,128)S(1)}) custom-call(s32[7]{0:T(128)} %refs_0_.1, bf16[768]{0:T(1024)(128)(2,1)} %refs_1_.1, bf16[768]{0:T(1024)(128)(2,1)} %refs_2_.1, bf16[768]{0:T(1024)(128)(2,1)} %refs_3_.1, bf16[768]{0:T(1024)(128)(2,1)} %refs_4_.1, ...), custom_call_target="tpu_custom_call" | custom-call | tf_op jit(solution)/shard_map/layer/pallas_call | solution.py:889
  166.4 3.6 %write.1 = (bf16[7,72,768]{2,1,0:T(8,128)(2,1)}, bf16[7,72,768]{2,1,0:T(8,128)(2,1)}, f32[24,32,768]{2,1,0:T(8,128)}, f32[6,32,3072]{2,1,0:T(8,128)}, f32[6,32,7...) custom-call(bf16[7,72,768]{2,1,0:T(8,128)(2,1)S(1)} %get-tuple-eleme, ...), custom_call_target="tpu_custom_call" | custom-call | tf_op jit(solution)/shard_map/write/pallas_call | solution.py:909

commit v11 on v10

--- a/solution.py
+++ b/solution.py
@@ -727,14 +727,15 @@
 
     pl.semaphore_wait(barrier, len(plan.links))
 
+    def open_chunk(item):
+        produce(item)
+        for number in range(len(plan.parts)):
+            begin(number, 0, item)
+
     def step(tick, carry):
-        @pl.when(tick < plan.chunks)
-        def _():
-            produce(tick)
-            for number in range(len(plan.parts)):
-                begin(number, 0, tick)
-
         for stage in range(plan.stages):
+            if stage == 1:
+                pl.when(tick < plan.chunks)(functools.partial(open_chunk, tick))
             for number, part in enumerate(plan.parts):
                 if stage < len(part.moves):
                     item = tick - part.due[stage]

time: 170 us -> 170 us (level)
  no operation moved by 1% of the time
where the time goes in v11:
time: 170 us
  Pallas kernels  169 us (99%)
    pallas_call x1, Pallas kernels, shards(): pl.pallas_call(functools.partial(layer_kernel, plan, (*inputs, *outputs,...  165 us
    pallas_call x1, Pallas kernels, shards(): pl.pallas_call(functools.partial(write_kernel, plan), out_shape=shapes, i...  3.56 us

profile of v11, /device:TPU:0, one launch (start us, length us, event | category | flops | bytes accessed | tf_op | source)
XLA Modules:
  0.0 169.7 jit_solution(2560410248811285484)
XLA Ops:
  0.7 165.3 %layer.1 = (bf16[7,72,768]{2,1,0:T(8,128)(2,1)S(1)}, bf16[7,72,768]{2,1,0:T(8,128)(2,1)S(1)}, f32[72,32,768]{2,1,0:T(8,128)S(1)}, f32[16,256]{1,0:T(8,128)S(1)}) custom-call(s32[7]{0:T(128)} %refs_0_.1, bf16[768]{0:T(1024)(128)(2,1)} %refs_1_.1, bf16[768]{0:T(1024)(128)(2,1)} %refs_2_.1, bf16[768]{0:T(1024)(128)(2,1)} %refs_3_.1, bf16[768]{0:T(1024)(128)(2,1)} %refs_4_.1, ...), custom_call_target="tpu_custom_call" | custom-call | tf_op jit(solution)/shard_map/layer/pallas_call | solution.py:890
  166.0 3.6 %write.1 = (bf16[7,72,768]{2,1,0:T(8,128)(2,1)}, bf16[7,72,768]{2,1,0:T(8,128)(2,1)}, f32[24,32,768]{2,1,0:T(8,128)}, f32[6,32,3072]{2,1,0:T(8,128)}, f32[6,32,7...) custom-call(bf16[7,72,768]{2,1,0:T(8,128)(2,1)S(1)} %get-tuple-eleme, ...), custom_call_target="tpu_custom_call" | custom-call | tf_op jit(solution)/shard_map/write/pallas_call | solution.py:910

commit v12 on v11

--- a/solution.py
+++ b/solution.py
@@ -11,7 +11,7 @@
 HEAD_DIM = 64
 EPSILON = 1e-06
 SUB = 8
-LAGS = ([1, 2, 2, 2, 2, 2, 3] + [2] * 8, [1] + [2] * 15)
+LAGS = ([1, 2, 2, 2, 2, 2, 4] + [2] * 8, [1, 2, 2, 2, 2, 2, 3] + [2] * 8)
 MOST = 32
 TILE = 256
 U1 = 7

time: 170 us -> 170 us (level)
  no operation moved by 1% of the time
where the time goes in v12:
time: 170 us
  Pallas kernels  169 us (99%)
    pallas_call x1, Pallas kernels, shards(): pl.pallas_call(functools.partial(layer_kernel, plan, (*inputs, *outputs,...  165 us
    pallas_call x1, Pallas kernels, shards(): pl.pallas_call(functools.partial(write_kernel, plan), out_shape=shapes, i...  3.56 us

profile of v12, /device:TPU:0, one launch (start us, length us, event | category | flops | bytes accessed | tf_op | source)
XLA Modules:
  0.0 169.8 jit_solution(16447239277121920809)
XLA Ops:
  0.7 165.4 %layer.1 = (bf16[7,72,768]{2,1,0:T(8,128)(2,1)S(1)}, bf16[7,72,768]{2,1,0:T(8,128)(2,1)S(1)}, f32[72,32,768]{2,1,0:T(8,128)S(1)}, f32[16,256]{1,0:T(8,128)S(1)}) custom-call(s32[7]{0:T(128)} %refs_0_.1, bf16[768]{0:T(1024)(128)(2,1)} %refs_1_.1, bf16[768]{0:T(1024)(128)(2,1)} %refs_2_.1, bf16[768]{0:T(1024)(128)(2,1)} %refs_3_.1, bf16[768]{0:T(1024)(128)(2,1)} %refs_4_.1, ...), custom_call_target="tpu_custom_call" | custom-call | tf_op jit(solution)/shard_map/layer/pallas_call | solution.py:890
  166.1 3.6 %write.1 = (bf16[7,72,768]{2,1,0:T(8,128)(2,1)}, bf16[7,72,768]{2,1,0:T(8,128)(2,1)}, f32[24,32,768]{2,1,0:T(8,128)}, f32[6,32,3072]{2,1,0:T(8,128)}, f32[6,32,7...) custom-call(bf16[7,72,768]{2,1,0:T(8,128)(2,1)S(1)} %get-tuple-eleme, ...), custom_call_target="tpu_custom_call" | custom-call | tf_op jit(solution)/shard_map/write/pallas_call | solution.py:910
